TPU v7x, 128 devices: a whole 4x4x4 slice. The times are simulated.
128 devices in a mesh: dp: 32 (over x, z, core), enc: 4 (over y).
Axes of the slice: x: 4, y: 4, z: 4, core: 2. Of those that a mesh axis runs over, the one named last changes fastest.
Arguments:
- hidden: bfloat16 [16384, 4096], P('dp', 'enc'), may hold values from -6 to 6
- norm_gain: float32 [4096], replicated, may hold values from 0.25 to 1.75
- w_query: bfloat16 [4096, 2048], P('dp', 'enc'), may hold values from -0.09375 to 0.09375
- w_key: bfloat16 [896, 2048], P('dp', 'enc'), may hold values from -0.1875 to 0.1875
- w_value: bfloat16 [896, 2048], P('dp', 'enc'), may hold values from -0.1875 to 0.1875
- w_out: bfloat16 [2048, 4096], P('enc', 'dp'), may hold values from -0.125 to 0.125
- w_cond: bfloat16 [4096, 896], P('dp', 'enc'), may hold values from -0.75 to 0.75
- enc_gain: float32 [896], replicated, may hold values from 0.25 to 1.75
- store: bfloat16 [1024, 128, 896], P(('dp', 'enc')), may hold values from -6 to 6
- neighbour_ids: int32 [512], P(('dp', 'enc')), may hold values from 0 to 1023, as said below
- out_grad: bfloat16 [16384, 4096], P('dp', 'enc'), may hold values from -6 to 6
Outputs:
- layer_out: bfloat16 [16384, 4096], P('dp', 'enc')
- hidden_grad: float32 [16384, 4096], P('dp', 'enc')
- query_grad: float32 [4096, 2048], P('dp', 'enc')
- key_grad: float32 [896, 2048], P('dp', 'enc')
- value_grad: float32 [896, 2048], P('dp', 'enc')
- out_weight_grad: float32 [2048, 4096], P('enc', 'dp')
- cond_grad: float32 [4096, 896], P('dp', 'enc')
Inputs may be any that keep to these rules, and one draw needn't show every extreme that they name: `neighbour_ids`: slot n names a neighbour stored on a device of the same data index as the device holding slot n (device k holds rows k * 8 to (k + 1) * 8 - 1). Among the 4 slots of one device at most 2 name rows of one device, and for every data index one device is named by exactly 2 slots of each of the 4 devices.
All inputs are finite; a program needn't handle non-finite values.
Results may differ from a plain program's by a relative error of at most 0.019.
Values may be sent and summed in bfloat16 or wider, within the bound.
A program may use at most 192 MiB of HBM per device.

v0:
```python
import jax
import jax.numpy as jnp
from jax import lax
from jax.sharding import PartitionSpec as P

HSZ = 128
SPAN = 64
NBR = 2
NL = 128


epsilon = 1e-05


def side_by_side(arrays, axis, dim, along):
    ends, at = ([], 0)
    for a in arrays[:-1]:
        at += a.shape[along]
        ends.append(at)
    both = jnp.concatenate(arrays, axis=along)
    return tuple(jnp.split(lax.all_gather(both, axis, axis=dim, tiled=True), ends, axis=along))


def joined_along(tiles, dim):
    tiles = jnp.moveaxis(tiles, 0, dim)
    dims = tiles.shape
    return tiles.reshape(*dims[:dim], dims[dim] * dims[dim + 1], *dims[dim + 2 :])


def copy_for_each(shard, axis):
    copies = jnp.broadcast_to(shard, (lax.axis_size(axis), *shard.shape))
    return lax.all_to_all(copies, axis, split_axis=0, concat_axis=0, tiled=True)


def collect(shard, axis, dim):
    return joined_along(copy_for_each(shard, axis), dim)


def in_blocks(shard, dim, peers):
    dims = shard.shape
    tiles = shard.reshape(*dims[:dim], peers, dims[dim] // peers, *dims[dim + 1 :])
    return jnp.moveaxis(tiles, dim, 0)


def summed_on_arrival(shard, axis, dim):
    peers = lax.axis_size(axis)
    tiles = lax.all_to_all(in_blocks(shard, dim, peers), axis, 0, 0, tiled=True)
    return jnp.sum(tiles.astype(jnp.float32), axis=0)


def one_scatter(arrays, axis, dims):
    peers = lax.axis_size(axis)
    tiles = [in_blocks(a, dim, peers) for a, dim in zip(arrays, dims)]
    lines = jnp.concatenate([b.reshape(peers, -1) for b in tiles], axis=1)
    extent = max(16, -(-lines.shape[1] // 1024) * 8)
    lines = jnp.pad(lines, ((0, 0), (0, extent * 128 - lines.shape[1]))).reshape(-1, 128)
    flat, at, done = (lax.psum_scatter(lines, axis, tiled=True).reshape(-1), 0, [])
    for b in tiles:
        part = b[0]
        done.append(flat[at : at + part.size].reshape(part.shape))
        at += part.size
    return tuple(done)


def rms_scale(values):
    return lax.rsqrt(jnp.mean(values * values, axis=-1, keepdims=True) + epsilon)


def encoder_input(raw_rows, cond_rows):
    enc_in = raw_rows.astype(jnp.float32) + cond_rows.astype(jnp.float32)[..., None, :]
    return (enc_in, rms_scale(enc_in))


def encode_rows(raw_rows, cond_rows, enc_gain):
    enc_in, enc_rstd = encoder_input(raw_rows, cond_rows)
    return (enc_in * enc_rstd * enc_gain).astype(jnp.bfloat16)


def cond_gradient(raw_rows, cond_rows, enc_gain, grad_rows):
    enc_in, enc_rstd = encoder_input(raw_rows, cond_rows)
    scaled_enc = enc_gain * grad_rows.astype(jnp.float32)
    enc_mean = jnp.mean(enc_in * scaled_enc, axis=-1, keepdims=True)
    return jnp.sum(enc_rstd * scaled_enc - enc_in * enc_rstd**3 * enc_mean, axis=-2)


def contract_first(left, right):
    return lax.dot_general(
        left, right, (((0,), (0,)), ((), ())), preferred_element_type=jnp.float32
    )


def contract_last(left, right):
    return lax.dot_general(
        left, right, (((1,), (1,)), ((), ())), preferred_element_type=jnp.float32
    )


def shards(
    hidden,
    norm_gain,
    w_query,
    w_key,
    w_value,
    w_out,
    w_cond,
    enc_gain,
    store,
    neighbour_ids,
    out_grad,
):
    groups = lax.axis_size("enc")
    member = lax.axis_index("enc")
    tok_rows = hidden.shape[0]
    feature_cols = hidden.shape[1]
    model_width = feature_cols * groups
    head_cols = w_query.shape[1]
    enc_width = w_key.shape[0] * lax.axis_size("dp")
    enc_cols = w_cond.shape[1]
    span_count = tok_rows // SPAN
    requests = neighbour_ids.shape[0]
    capacity = max(2, (requests + 1) // 2)
    store_rows = store.shape[0]
    heads_here = head_cols // HSZ
    keys_len = NBR * NL
    score_scale = HSZ ** (-0.5)
    full_rows = lax.all_gather(hidden, "enc", axis=1, tiled=True)
    inputs = full_rows.astype(jnp.float32)
    row_rstd = rms_scale(inputs)
    normed = (inputs * row_rstd * norm_gain).astype(jnp.bfloat16)
    w_query_all, w_key_all, w_value_all, w_cond_all = (
        lax.all_gather(w_query, "dp", axis=0, tiled=True),
        *side_by_side((w_key, w_value), "dp", 0, 1),
        lax.all_gather(w_cond, "dp", axis=0, tiled=True),
    )
    queries = jnp.dot(normed, w_query_all, preferred_element_type=jnp.float32).astype(jnp.bfloat16)
    w_out_all = lax.all_gather(w_out, "dp", axis=1, tiled=True)
    summary = jnp.mean(inputs.reshape(span_count, SPAN, model_width), axis=1).astype(jnp.bfloat16)
    cond_part = jnp.dot(summary, w_cond_all, preferred_element_type=jnp.float32).astype(
        jnp.bfloat16
    )
    condition = collect(cond_part, "enc", 1)
    request_order = jnp.arange(requests)
    my_spans = (member * requests + request_order) // NBR
    cond_req = jnp.take(condition, my_spans, axis=0)
    owner_of = neighbour_ids // store_rows % groups
    store_row = neighbour_ids % store_rows
    earlier = (owner_of[:, None] == owner_of[None, :]) & (
        request_order[None, :] < request_order[:, None]
    )
    slot_rank = jnp.sum(earlier.astype(jnp.int32), axis=1)
    slot_index = owner_of * capacity + slot_rank
    selection = slot_index[None, :] == jnp.arange(groups * capacity)[:, None]
    row_buffer = jnp.sum(jnp.where(selection, store_row[None, :], 0), axis=1).reshape(
        groups, capacity
    )
    raw_buffer = lax.all_to_all(
        jnp.take(
            store,
            lax.all_to_all(row_buffer, "enc", split_axis=0, concat_axis=0, tiled=True),
            axis=0,
        ),
        "enc",
        split_axis=0,
        concat_axis=0,
        tiled=True,
    )
    raw_mine = jnp.take(raw_buffer.reshape(groups * capacity, NL, enc_width), slot_index, axis=0)
    encoded_mine = encode_rows(raw_mine, cond_req, enc_gain)
    encoded = lax.all_gather(encoded_mine, "enc", axis=0, tiled=True)
    flat_enc = encoded.reshape(-1, enc_width)
    keys_proj = jnp.dot(flat_enc, w_key_all, preferred_element_type=jnp.float32).astype(
        jnp.bfloat16
    )
    values_proj = jnp.dot(flat_enc, w_value_all, preferred_element_type=jnp.float32).astype(
        jnp.bfloat16
    )
    query_heads = queries.reshape(span_count, SPAN, heads_here, HSZ)
    key_heads = keys_proj.reshape(span_count, keys_len, heads_here, HSZ)
    value_heads = values_proj.reshape(span_count, keys_len, heads_here, HSZ)
    scores = (
        jnp.einsum("cqhd,ckhd->chqk", query_heads, key_heads, preferred_element_type=jnp.float32)
        * score_scale
    )
    attn_full = jax.nn.softmax(scores, axis=-1)
    attn_weights = attn_full.astype(jnp.bfloat16)
    attended = (
        jnp.einsum("chqk,ckhd->cqhd", attn_weights, value_heads, preferred_element_type=jnp.float32)
        .astype(jnp.bfloat16)
        .reshape(tok_rows, head_cols)
    )
    out_term = jnp.dot(attended, w_out_all, preferred_element_type=jnp.float32)
    projected = summed_on_arrival(out_term.astype(jnp.bfloat16), "enc", 1)
    layer_out = (hidden.astype(jnp.float32) + projected).astype(jnp.bfloat16)
    grad_rows = lax.all_gather(out_grad, "enc", axis=1, tiled=True)
    attended_grad = contract_last(grad_rows, w_out_all).astype(jnp.bfloat16)
    out_weight_grad = lax.psum_scatter(
        contract_first(attended, grad_rows).astype(jnp.bfloat16),
        "dp",
        scatter_dimension=1,
        tiled=True,
    ).astype(jnp.float32)
    grad_heads = attended_grad.reshape(span_count, SPAN, heads_here, HSZ)
    prob_grad = jnp.einsum(
        "cqhd,ckhd->chqk", grad_heads, value_heads, preferred_element_type=jnp.float32
    )
    score_grad = (
        attn_full
        * (prob_grad - jnp.sum(attn_full * prob_grad, axis=-1, keepdims=True))
        * score_scale
    ).astype(jnp.bfloat16)
    query_act_grad = (
        jnp.einsum("chqk,ckhd->cqhd", score_grad, key_heads, preferred_element_type=jnp.float32)
        .astype(jnp.bfloat16)
        .reshape(tok_rows, head_cols)
    )
    key_act_grad = (
        jnp.einsum("chqk,cqhd->ckhd", score_grad, query_heads, preferred_element_type=jnp.float32)
        .astype(jnp.bfloat16)
        .reshape(-1, head_cols)
    )
    value_act_grad = (
        jnp.einsum("chqk,cqhd->ckhd", attn_weights, grad_heads, preferred_element_type=jnp.float32)
        .astype(jnp.bfloat16)
        .reshape(-1, head_cols)
    )
    query_grad = lax.psum_scatter(
        contract_first(normed, query_act_grad).astype(jnp.bfloat16),
        "dp",
        scatter_dimension=0,
        tiled=True,
    ).astype(jnp.float32)
    enc_term = contract_last(key_act_grad, w_key_all) + contract_last(value_act_grad, w_value_all)
    encoded_grad = (
        summed_on_arrival(enc_term.astype(jnp.bfloat16), "enc", 0)
        .astype(jnp.bfloat16)
        .reshape(requests, NL, enc_width)
    )
    cond_mine = cond_gradient(raw_mine, cond_req, enc_gain, encoded_grad)
    slot_grads = collect(cond_mine, "enc", 0)
    cond_delta = jnp.sum(slot_grads.reshape(span_count, NBR, enc_width), axis=1).astype(
        jnp.bfloat16
    )
    delta_cols = lax.dynamic_slice_in_dim(cond_delta, member * enc_cols, enc_cols, 1)
    key_term = contract_first(flat_enc, key_act_grad)
    value_term = contract_first(flat_enc, value_act_grad)
    cond_term = contract_first(summary, delta_cols)
    key_grad, value_grad, cond_grad = tuple(
        (
            part.astype(jnp.float32)
            for part in one_scatter(
                (
                    key_term.astype(jnp.bfloat16),
                    value_term.astype(jnp.bfloat16),
                    cond_term.astype(jnp.bfloat16),
                ),
                "dp",
                (0, 0, 0),
            )
        )
    )
    summary_term = contract_last(delta_cols, w_cond_all)
    normed_term = contract_last(query_act_grad, w_query_all)
    normed_grad, summary_grad = (
        lax.psum(normed_term.astype(jnp.bfloat16), "enc").astype(jnp.float32),
        lax.psum(summary_term.astype(jnp.bfloat16), "enc").astype(jnp.float32),
    )
    scaled = normed_grad * norm_gain
    row_mean = jnp.mean(inputs * scaled, axis=-1, keepdims=True)
    full_grad = (
        grad_rows.astype(jnp.float32)
        + (row_rstd * scaled - inputs * row_rstd**3 * row_mean)
        + jnp.repeat(summary_grad / SPAN, SPAN, axis=0)
    )
    hidden_grad = lax.dynamic_slice_in_dim(full_grad, member * feature_cols, feature_cols, 1)
    return (layer_out, hidden_grad, query_grad, key_grad, value_grad, out_weight_grad, cond_grad)


def solution(mesh):
    placed = (
        P("dp", "enc"),
        P(),
        P("dp", "enc"),
        P("dp", "enc"),
        P("dp", "enc"),
        P("enc", "dp"),
        P("dp", "enc"),
        P(),
        P(("dp", "enc"), None, None),
        P(("dp", "enc")),
        P("dp", "enc"),
    )
    return jax.shard_map(
        shards,
        mesh=mesh,
        in_specs=placed,
        out_specs=(
            P("dp", "enc"),
            P("dp", "enc"),
            P("dp", "enc"),
            P("dp", "enc"),
            P("dp", "enc"),
            P("enc", "dp"),
            P("dp", "enc"),
        ),
        check_vma=False,
    )
```

profile of v0, /device:TPU:7, one launch (start us, length us, event | category | flops | bytes accessed | tf_op | source)
XLA Modules:
  0.0 739.2 jit_solution(10964547584921568469)
XLA Ops:
  11.8 8.1 %all_to_all.40 = s32[4,1,2]{2,1,0:T(1,128)S(1)} all-to-all(s32[4,1,2]{2,1,0:T(1,128)S(1)} %bitcast.99), channel_id=1, replica_groups=mesh['dp'=32,'enc'=4] {'enc'}, dimensions={0} | all-to-all | bytes 64 | tf_op jit(solution)/shard_map/all_to_all | solution.py:159
  20.3 2.0 gather_fusion
  22.3 3.1 broadcast_select_fusion
  25.4 3.6 all-to-all-start.1
  29.1 50.9 %all-gather.9.cloned.1.call-done = bf16[512,4096]{1,0:T(8,128)(2,1)} async-done(((bf16[512,1024]{1,0:T(8,128)(2,1)}), bf16[512,4096]{1,0:T(8,128)(2,1)}) %all-gather.9.cloned.1.call-update) | async-done | bytes 4194320 | tf_op jit(solution)/shard_map/all_gather | solution.py:126
  79.9 3.0 bitcast_reduce_fusion
  83.0 44.0 %all-gather.11.cloned.1.call-done = bf16[4096,224]{0,1:T(8,128)(2,1)} async-done(((bf16[128,224]{0,1:T(8,128)(2,1)}), bf16[4096,224]{0,1:T(8,128)(2,1)}) %all-gather.11.cloned.1.call-update) | async-done | bytes 1835024 | tf_op jit(solution)/shard_map/all_gather | solution.py:133
  127.0 2.1 convolution_convert_fusion.12
  129.7 4.0 all-to-all-start.2
  133.7 2.2 gather_fusion.1
  135.9 2.0 all-to-all-done.2
  142.4 30.7 %all-gather.21.cloned.1.call-done = bf16[32,28,1024]{2,1,0:T(8,128)(2,1)} async-done(((bf16[1,28,1024]{2,1,0:T(8,128)(2,1)}), bf16[32,28,1024]{2,1,0:T(8,128)(2,1)}) %all-gather.21.cloned.1.call-update) | async-done | bytes 1835024 | tf_op jit(solution)/shard_map/all_gather | solution.py:21
  173.2 3.7 reshape.330
  176.9 3.1 multiply_reduce_fusion.1
  180.6 40.2 %all-gather.15.cloned.1.call-done = bf16[4096,512]{1,0:T(8,128)(2,1)} async-done(((bf16[128,512]{1,0:T(8,128)(2,1)}), bf16[4096,512]{1,0:T(8,128)(2,1)}) %all-gather.15.cloned.1.call-update) | async-done | bytes 4194320 | tf_op jit(solution)/shard_map/all_gather | solution.py:131
  220.8 5.8 convolution_convert_fusion.11
  226.7 39.5 %all-gather.13.cloned.1.call-done = bf16[16,128,896]{2,1,0:T(8,128)(2,1)} async-done(((bf16[4,128,896]{2,1,0:T(8,128)(2,1)}), bf16[16,128,896]{2,1,0:T(8,128)(2,1)}) %all-gather.13.cloned.1.call-update) | async-done | bytes 3670032 | tf_op jit(solution)/shard_map/all_gather | solution.py:169
  266.2 5.9 convolution_convert_fusion.6
  272.2 4.0 reshape.289
  276.1 6.4 convolution_convert_fusion.7
  282.5 4.2 reshape.287
  286.7 2.4 fusion.15
  289.2 2.0 fusion.84
  291.2 6.0 fusion.34
  297.5 18.7 %all-gather.19.cloned.1.call-done = bf16[512,4096]{1,0:T(8,128)(2,1)} async-done(((bf16[512,1024]{1,0:T(8,128)(2,1)}), bf16[512,4096]{1,0:T(8,128)(2,1)}) %all-gather.19.cloned.1.call-update) | async-done | bytes 4194320 | tf_op jit(solution)/shard_map/all_gather | solution.py:194
  316.3 6.5 convolution_convert_fusion
  322.8 6.5 copy.112
  329.8 38.4 %all-gather.17.cloned.1.call-done = bf16[512,4096]{1,0:T(8,128)(2,1)} async-done(((bf16[512,128]{1,0:T(8,128)(2,1)}), bf16[512,4096]{1,0:T(8,128)(2,1)}) %all-gather.17.cloned.1.call-update) | async-done | bytes 4194320 | tf_op jit(solution)/shard_map/all_gather | solution.py:136
  368.2 5.8 convolution_convert_fusion.10
  374.1 3.8 fusion.9
  377.9 16.2 %fusion.37 = bf16[8,64,4,128]{3,1,2,0:T(8,128)(2,1)} fusion(bf16[8,256,4,128]{3,2,1,0:T(4,128)(2,1)} %reshape.289, f32[8,4,64,256]{3,2,1,0:T(8,128)} %fusion.9, f32[8,4,64,256]{3,2,1,0:T(8,128)} %get-tuple-element.50, f32[8,4,64]{2,1,0:T(4,128)S(1)} %get-tuple-element.49), kind=kOutput, calls=%fused_computation.62 | convolution fusion | flops 138152192 | bytes 6823936 | tf_op jit(solution)/shard_map/chqk,ckhd->cqhd/dot_general | solution.py:212
  394.1 1.5 copy.104
  395.6 6.8 convolution_convert_fusion.1
  402.5 16.7 %convert_bitcast_fusion.1 = bf16[8,256,4,128]{1,3,2,0:T(8,128)(2,1)} fusion(f32[8,4,64,256]{3,2,1,0:T(8,128)} %fusion.9, bf16[8,64,4,128]{3,2,1,0:T(4,128)(2,1)S(1)} %reshape.288, f32[8,4,64,256]{3,2,1,0:T(8,128)} %get-tuple-element.50, f32[8,4,64]{2,1,0:T(4,128)S(1)} %get-tuple-element.49), kind=kOutput, calls=%fused_computation.29 | convolution fusion | flops 138938624 | bytes 6823936 | tf_op jit(solution)/shard_map/chqk,cqhd->ckhd/dot_general | solution.py:217
  419.2 2.9 copy.106
  422.1 2.0 copy.118
  424.1 7.0 convert_bitcast_fusion
  431.1 2.8 copy.108
  436.8 2.4 fusion.47
  439.3 4.4 add_convert_fusion
  443.7 5.0 all-to-all-start.4
  448.7 6.7 convolution_convert_fusion.2
  455.4 3.0 convolution_convert_fusion.8
  458.5 3.0 convolution_convert_fusion.9
  461.5 30.3 %all-to-all-done.4 = bf16[4,512,896]{2,1,0:T(8,128)(2,1)} async-done(((bf16[4,512,896]{2,1,0:T(8,128)(2,1)}), bf16[4,512,896]{2,1,0:T(8,128)(2,1)}, u32[]{:S(2)}, u32[]{:S(2)}) %all-to-all-start.4) | async-done | bytes 3670048 | tf_op jit(solution)/shard_map/all_to_all | solution.py:47
  491.8 3.1 reduce_sum.133
  496.9 3.5 all-to-all-start.5
  500.4 4.5 convolution_convert_fusion.3
  505.0 2.4 copy.161
  508.6 2.0 reshape_reshape.14
  510.6 4.9 all-to-all-start.3
  516.4 2.5 copy.110
  518.9 5.0 reshape_reshape.15
  523.9 2.5 convolution_convert_fusion.5
  526.8 2.9 pad_maximum_fusion
  529.7 5.2 reshape.298
  535.0 6.5 convert_element_type.163
  541.5 31.9 %all-to-all-done.3 = bf16[4,512,1024]{2,1,0:T(8,128)(2,1)} async-done(((bf16[4,512,1024]{2,1,0:T(8,128)(2,1)}), bf16[4,512,1024]{2,1,0:T(8,128)(2,1)}, u32[]{:S(2)}, u32[]{:S(2)}) %all-to-all-start.3) | async-done | bytes 4194336 | tf_op jit(solution)/shard_map/all_to_all | solution.py:47
  573.4 3.4 convert_reduce_fusion
  579.9 1.6 convert_element_type.196
  581.6 64.2 %all-reduce.3.cloned.1.call-done = (bf16[8,4096]{1,0:T(8,128)(2,1)}, bf16[512,4096]{1,0:T(8,128)(2,1)}) async-done(((bf16[8,4096]{1,0:T(8,128)(2,1)}, bf16[512,4096]{1,0:T(8,128)(2,1)}), (bf16[8,4096]{1,0:T(8,128)(2,1)}, bf16[512,4096]{1,0:T(8,128)(2,1)})) %all-reduce.3.cloned.1.call-update) | async-done | bytes 4259856 | tf_op jit(solution)/shard_map/psum | solution.py:265
  645.8 4.9 multiply_reduce_fusion
  651.8 4.0 dynamic-slice_add_fusion
  655.8 72.6 %reduce-scatter.8.cloned.1.call-done = bf16[448,128]{1,0:T(8,128)(2,1)} async-done(((bf16[14336,128]{1,0:T(8,128)(2,1)}), bf16[448,128]{1,0:T(8,128)(2,1)}) %reduce-scatter.8.cloned.1.call-update) | async-done | bytes 114704 | tf_op jit(solution)/shard_map/reduce_scatter | solution.py:57
  (129 shorter events, 27.0 us)
Async XLA Ops:
  7.2 13.1 %copy-start = (bf16[8,128,896]{2,1,0:T(8,128)(2,1)S(1)}, bf16[8,128,896]{2,1,0:T(8,128)(2,1)}, u32[]{:S(2)}) copy-start(bf16[8,128,896]{2,1,0:T(8,128)(2,1)} %param.19) | copy-start | bytes 5505028
  7.2 72.8 %all-gather.9.cloned.1.call-start = ((), (), s32[]{:S(2)}) async-start(), calls=%async_computation.9 | async-start | bytes 5242880 | tf_op jit(solution)/shard_map/all_gather | solution.py:126
  7.9 119.1 %all-gather.11.cloned.1.call-start = ((), (), s32[]{:S(2)}) async-start(), calls=%async_computation.10 | async-start | bytes 1892352 | tf_op jit(solution)/shard_map/all_gather | solution.py:133
  8.7 164.5 %all-gather.21.cloned.1.call-start = ((), (), s32[]{:S(2)}) async-start(), calls=%async_computation.17 | async-start | bytes 2162688 | tf_op jit(solution)/shard_map/all_gather | solution.py:21
  10.2 210.6 %all-gather.15.cloned.1.call-start = ((), (), s32[]{:S(2)}) async-start(), calls=%async_computation.12 | async-start | bytes 4325376 | tf_op jit(solution)/shard_map/all_gather | solution.py:131
  11.6 128.1 %copy-start.19 = (pred[4]{0:T(512)(128)(4,1)}, pred[4]{0:T(512)(128)(4,1)S(1)}, u32[]{:S(2)}) copy-start(pred[4]{0:T(512)(128)(4,1)S(1)} %get-tuple-element.37) | copy-start | bytes 16
  25.4 103.7 %all-to-all-start.1 = ((bf16[4,2,128,896]{3,2,1,0:T(8,128)(2,1)}), bf16[4,2,128,896]{3,2,1,0:T(8,128)(2,1)S(1)}, u32[]{:S(2)}, u32[]{:S(2)}) async-start(bf16[4,2,128,896]{3,2,1,0:T(8,128)(2,1)} %broadcast_select_fusion), calls=%async_computation.1 | async-start | bytes 3670016 | tf_op jit(solution)/shard_map/all_to_all | solution.py:156
  83.0 56.7 %copy-start.13 = (f32[896]{0:T(1024)S(1)}, f32[896]{0:T(1024)}, u32[]{:S(2)}) copy-start(f32[896]{0:T(1024)} %param.18) | copy-start | bytes 10756
  129.1 4.7 copy-start.4
  129.7 8.2 %all-to-all-start.2 = ((bf16[4,8,224]{2,1,0:T(8,128)(2,1)}), bf16[4,8,224]{2,1,0:T(8,128)(2,1)S(1)}, u32[]{:S(2)}, u32[]{:S(2)}) async-start(bf16[4,8,224]{2,1,0:T(8,128)(2,1)} %broadcast_in_dim.82), calls=%async_computation.2 | async-start | bytes 32768 | tf_op jit(solution)/shard_map/all_to_all | solution.py:32
  133.7 132.5 %all-gather.13.cloned.1.call-start = ((), (), s32[]{:S(2)}) async-start(), calls=%async_computation.11 | async-start | bytes 4587520 | tf_op jit(solution)/shard_map/all_gather | solution.py:169
  139.7 37.2 %copy-start.15 = (f32[4,128]{1,0:T(4,128)}, f32[4,128]{1,0:T(4,128)S(1)}, u32[]{:S(2)}) copy-start(f32[4,128]{1,0:T(4,128)S(1)} %get-tuple-element.46) | copy-start | bytes 6148
  141.1 175.2 %all-gather.19.cloned.1.call-start = ((), (), s32[]{:S(2)}) async-start(), calls=%async_computation.14 | async-start | bytes 5242880 | tf_op jit(solution)/shard_map/all_gather | solution.py:194
  141.7 226.5 %all-gather.17.cloned.1.call-start = ((), (), s32[]{:S(2)}) async-start(), calls=%async_computation.13 | async-start | bytes 4325376 | tf_op jit(solution)/shard_map/all_gather | solution.py:136
  142.4 435.8 %reduce-scatter.10.cloned.1.call-start = ((), (), s32[]{:S(2)}) async-start(), calls=%async_computation.18 | async-start | bytes 4325376
  176.9 43.9 %copy-start.17 = (f32[4096]{0:T(1024)S(1)}, f32[4096]{0:T(1024)}, u32[]{:S(2)}) copy-start(f32[4096]{0:T(1024)} %param.12) | copy-start | bytes 49156
  180.6 215.0 %copy-start.22 = (f32[512]{0:T(512)}, f32[512]{0:T(512)S(1)}, u32[]{:S(2)}) copy-start(f32[512]{0:T(512)S(1)} %get-tuple-element.44) | copy-start | bytes 6148
  289.2 2.0 copy-start.2
  329.3 250.6 %reduce-scatter.6.cloned.1.call-start = ((), (), s32[]{:S(2)}) async-start(), calls=%async_computation.15 | async-start | bytes 4325376 | tf_op jit(solution)/shard_map/reduce_scatter | solution.py:226
  434.0 1.6 copy-start.5
  434.0 2.9 copy-start.9
  434.7 4.6 copy-start.7
  443.7 48.1 %all-to-all-start.4 = ((bf16[4,512,896]{2,1,0:T(8,128)(2,1)}), bf16[4,512,896]{2,1,0:T(8,128)(2,1)}, u32[]{:S(2)}, u32[]{:S(2)}) async-start(bf16[4,512,896]{2,1,0:T(8,128)(2,1)} %bitcast.88), calls=%async_computation.4 | async-start | bytes 7340032 | tf_op jit(solution)/shard_map/all_to_all | solution.py:47
  448.7 6.7 copy-start.8
  448.7 6.7 copy-start.25
  455.4 3.0 copy-start.6
  461.5 33.4 %copy-start.14 = (f32[896]{0:T(1024)S(1)}, f32[896]{0:T(1024)}, u32[]{:S(2)}) copy-start(f32[896]{0:T(1024)} %param.18) | copy-start | bytes 10756
  461.5 33.4 %copy-start.20 = (pred[4]{0:T(512)(128)(4,1)S(1)}, pred[4]{0:T(512)(128)(4,1)}, u32[]{:S(2)}) copy-start(pred[4]{0:T(512)(128)(4,1)} %copy-done.19) | copy-start | bytes 16
  461.5 34.0 %copy-start.16 = (f32[4,128]{1,0:T(4,128)S(1)}, f32[4,128]{1,0:T(4,128)}, u32[]{:S(2)}) copy-start(f32[4,128]{1,0:T(4,128)} %copy-done.15) | copy-start | bytes 6148
  461.5 34.0 %copy-start.24 = (f32[4,128]{1,0:T(4,128)S(1)}, f32[4,128]{1,0:T(4,128)}, u32[]{:S(2)}) copy-start(f32[4,128]{1,0:T(4,128)} %get-tuple-element.45) | copy-start | bytes 6148
  496.9 13.7 %all-to-all-start.5 = ((f32[4,4,896]{2,1,0:T(4,128)}), f32[4,4,896]{2,1,0:T(4,128)S(1)}, u32[]{:S(2)}, u32[]{:S(2)}) async-start(f32[4,4,896]{2,1,0:T(4,128)} %broadcast_in_dim.84), calls=%async_computation.5 | async-start | bytes 114688 | tf_op jit(solution)/shard_map/all_to_all | solution.py:32
  505.0 2.4 copy-start.11
  507.4 1.2 copy-start.10
  510.6 62.8 %all-to-all-start.3 = ((bf16[4,512,1024]{2,1,0:T(8,128)(2,1)}), bf16[4,512,1024]{2,1,0:T(8,128)(2,1)}, u32[]{:S(2)}, u32[]{:S(2)}) async-start(bf16[4,512,1024]{2,1,0:T(8,128)(2,1)} %bitcast.80), calls=%async_computation.3 | async-start | bytes 8388608 | tf_op jit(solution)/shard_map/all_to_all | solution.py:47
  515.4 130.3 %all-reduce.3.cloned.1.call-start = ((), (), s32[]{:S(2)}) async-start(), calls=%async_computation.19 | async-start | bytes 8519680 | tf_op jit(solution)/shard_map/psum | solution.py:265
  526.4 202.0 %reduce-scatter.8.cloned.1.call-start = ((), (), s32[]{:S(2)}) async-start(), calls=%async_computation.16 | async-start | bytes 3784704 | tf_op jit(solution)/shard_map/reduce_scatter | solution.py:57
  541.5 35.3 %copy-start.3 = (bf16[512,1024]{1,0:T(8,128)(2,1)S(1)}, bf16[512,1024]{1,0:T(8,128)(2,1)}, u32[]{:S(2)}) copy-start(bf16[512,1024]{1,0:T(8,128)(2,1)} %param.11) | copy-start | bytes 3145732
  576.8 69.0 %copy-start.18 = (f32[4096]{0:T(1024)S(1)}, f32[4096]{0:T(1024)}, u32[]{:S(2)}) copy-start(f32[4096]{0:T(1024)} %param.12) | copy-start | bytes 49156
  645.8 4.9 copy-start.12
  650.7 1.0 copy-start.21
  650.7 1.0 copy-start.23
  651.8 80.4 %copy-start.1 = (bf16[8,128,896]{2,1,0:T(8,128)(2,1)S(1)}, bf16[8,128,896]{2,1,0:T(8,128)(2,1)}, u32[]{:S(2)}) copy-start(bf16[8,128,896]{2,1,0:T(8,128)(2,1)} %param.19) | copy-start | bytes 5505028
Sparse Core Ops, SparseCore 0:
  9.7 70.2 all-gather.8
  82.1 44.8 all-gather.10
  129.8 43.3 all-gather.20
  175.3 45.4 all-gather.14
  222.8 43.3 all-gather.12
  267.8 48.4 all-gather.18
  318.4 49.6 all-gather.16
  371.8 78.9 reduce-scatter.9
  454.9 82.2 reduce-scatter.5
  540.1 105.6 all-reduce.2
  649.9 78.4 reduce-scatter.7
where the time goes:
time: 752 us; the launch traced here: 739 us
  waiting for transfers between devices  467 us (62%)
  matrix products  119 us (16%)
  local copies, waits for them, and re-layouts  60.3 us (8%)
  other arithmetic  48.4 us (6%)
  starting transfers between devices  22.1 us (3%)
  between operations  14.9 us (2%)
  blocking collectives  8.08 us (1%)
    reduce_scatter x1, waiting for transfers between devices, one_scatter(): lax.psum_scatter(lines, axis, tiled=True).reshape(-1)  72.6 us
    psum x1, waiting for transfers between devices, shards(): lax.psum(summary_term.astype(jnp.bfloat16), 'enc').astype(jnp.float32)  64.2 us
    all_to_all x2, waiting for transfers between devices, summed_on_arrival(): tiles = lax.all_to_all(in_blocks(shard, dim, peers), axis, 0, 0, tiled=True)  62.2 us
    all_gather x1, waiting for transfers between devices, shards(): full_rows = lax.all_gather(hidden, 'enc', axis=1, tiled=True)  50.9 us
    all_gather x1, waiting for transfers between devices, shards(): lax.all_gather(w_cond, 'dp', axis=0, tiled=True)  44 us
    all_gather x1, waiting for transfers between devices, shards(): lax.all_gather(w_query, 'dp', axis=0, tiled=True)  40.2 us
    all_gather x1, waiting for transfers between devices, shards(): encoded = lax.all_gather(encoded_mine, 'enc', axis=0, tiled=True)  39.5 us
    all_gather x1, waiting for transfers between devices, shards(): w_out_all = lax.all_gather(w_out, 'dp', axis=1, tiled=True)  38.4 us
  transfers between devices with their start and end apart: 16, of which 12 were waited for; matrix products, arithmetic and copies ran while one was open for 30% of the time, Pallas kernels for 0%

commit v1 on v0

v1 whole, which is shorter than its diff:
```python
import functools

import jax
import jax.numpy as jnp
from jax import lax
from jax.experimental import pallas as pl
from jax.experimental.pallas import tpu as pltpu
from jax.sharding import PartitionSpec as P

MESH = pl.DeviceIdType.MESH
F32 = jnp.float32
BF16 = jnp.bfloat16
HSZ = 128
SPAN = 64
NL = 128
DE = 896
PE = 1024
EPS = 1e-05
ANY = pl.BlockSpec(memory_space=pl.ANY)
VM = pl.BlockSpec(memory_space=pltpu.VMEM)
DMA = pltpu.SemaphoreType.DMA


def place():
    d = lax.axis_index("dp")
    return d // 8, (d // 2) % 4, d % 2, lax.axis_index("enc")


def at(x, z, c, y):
    return ((x * 4 + z) * 2 + c, y)


def around(v, k):
    return (v + k) % 4


def remote(src, dst, send, recv, device):
    copy = pltpu.make_async_remote_copy(
        src, dst, send, recv, device_id=device, device_id_type=MESH
    )
    copy.start()
    return copy


def meet(peers, partner=None, has_partner=None):
    barrier = pltpu.get_barrier_semaphore()
    for peer in peers:
        pl.semaphore_signal(barrier, inc=1, device_id=peer, device_id_type=MESH)
    if partner is not None:

        @pl.when(has_partner)
        def _():
            pl.semaphore_signal(barrier, inc=1, device_id=partner, device_id_type=MESH)

        pl.semaphore_wait(barrier, jnp.where(has_partner, len(peers) + 1, len(peers)))
    else:
        pl.semaphore_wait(barrier, len(peers))


def sum_rows(out, terms, step=16):
    rows = out.shape[0]

    def body(i, carry):
        at_row = pl.ds(pl.multiple_of(i * step, step), step)
        total = terms[0][at_row].astype(F32)
        for t in terms[1:]:
            total = total + t[at_row].astype(F32)
        out[at_row] = total.astype(out.dtype)
        return carry

    lax.fori_loop(0, rows // step, body, 0)


def cols(i, n):
    return pl.ds(pl.multiple_of(i * n, n), n)


def gather_kernel(
    ids, sq, store, wq, wo, wc,
    raw, sq_all, gq, go, gc,
    ids_all, ids_s, out_rows, in_rows, tq, to, tc,
    s_small, r_small, s_row, r_row, s_t, r_t, s_x, r_x, s_z, r_z, s_c, r_c, s_loc,
):
    x, z, c, y = place()
    yp = [at(x, z, c, around(y, k)) for k in (1, 2, 3)]
    xp = [at(around(x, k), z, c, y) for k in (1, 2, 3)]
    zp = [at(x, around(z, k), c, y) for k in (1, 2, 3)]
    sib = at(x, z, 1 - c, y)
    partner = at(y, z, c, x)
    meet(yp + xp + zp + [sib], partner, x != y)

    small = []
    for k in (1, 2, 3):
        small.append(remote(ids, ids_all.at[y], s_small.at[0, k], r_small.at[0, k], yp[k - 1]))
        small.append(remote(sq, sq_all.at[y], s_small.at[1, k], r_small.at[1, k], yp[k - 1]))
    keep_ids = pltpu.make_async_copy(ids, ids_all.at[y], s_loc.at[0])
    keep_sq = pltpu.make_async_copy(sq, sq_all.at[y], s_loc.at[1])
    keep_ids.start()
    keep_sq.start()

    @pl.when(x != y)
    def _():
        for n, (w, t) in enumerate(((wq, tq), (wo, to), (wc, tc))):
            remote(w, t, s_t.at[n], r_t.at[n], partner)

    @pl.when(x == y)
    def _():
        for n, (w, t) in enumerate(((wq, tq), (wo, to), (wc, tc))):
            pltpu.make_async_copy(w, t, r_t.at[n]).start()

    keep_ids.wait()
    keep_sq.wait()
    for copy in small:
        copy.wait_recv()
    to_s = pltpu.make_async_copy(ids_all, ids_s, s_loc.at[2])
    to_s.start()
    to_s.wait()

    def picks(r):
        every = [ids_s[r, 0, k] for k in range(4)]
        owner = [(v // 8) % 4 for v in every]
        row = [v % 8 for v in every]
        rank = []
        for k in range(4):
            n = jnp.int32(0)
            for j in range(k):
                n = n + jnp.where(owner[j] == owner[k], 1, 0)
            rank.append(n)
        return owner, row, rank

    row_copies = []
    for k in (2, 1, 3):
        r = around(y, k)
        owner, row, rank = picks(r)
        for q in range(2):
            pick = jnp.int32(0)
            for j in range(4):
                pick = pick + jnp.where((owner[j] == y) & (rank[j] == q), row[j], 0)
            out_rows[k, q] = store[pick]
        row_copies.append(
            remote(out_rows.at[k], in_rows.at[y], s_row.at[k], r_row.at[k], yp[k - 1])
        )
    owner, row, rank = picks(y)
    for q in range(2):
        pick = jnp.int32(0)
        for j in range(4):
            pick = pick + jnp.where((owner[j] == y) & (rank[j] == q), row[j], 0)
        in_rows[y, q] = store[pick]

    triples = ((tq, gq, 512), (to, go, 512), (tc, gc, 256))
    first, keep = [], []
    for n, (t, g, w) in enumerate(triples):
        pltpu.make_async_copy(t, t, r_t.at[n]).wait()
        mine = g.at[z, c, :, cols(x, w)]
        local = pltpu.make_async_copy(t, mine, s_loc.at[3 + n])
        local.start()
        keep.append(local)
        for k in (2, 1, 3):
            peer = zp[k - 1] if n == 1 else xp[k - 1]
            first.append(remote(t, mine, s_x.at[n, k], r_x.at[n, k], peer))
    second = []
    for n, (t, g, w) in enumerate(triples):
        keep[n].wait()
        for copy in first[3 * n : 3 * n + 3]:
            copy.wait_recv()
        block = g.at[:, c, :, cols(x, w)] if n == 1 else g.at[z, c]
        for k in (2, 1, 3):
            peer = xp[k - 1] if n == 1 else zp[k - 1]
            second.append(remote(block, block, s_z.at[n, k], r_z.at[n, k], peer))
    third = []
    for n, (t, g, w) in enumerate(triples):
        for copy in second[3 * n : 3 * n + 3]:
            copy.wait_recv()
        third.append(remote(g.at[:, c], g.at[:, c], s_c.at[n], r_c.at[n], sib))

    for copy in row_copies:
        copy.wait_recv()
    for k in range(4):
        raw[k] = in_rows[owner[k], jnp.minimum(rank[k], 1)]
    for copy in third:
        copy.wait_recv()
    for copy in small + row_copies + first + second + third:
        copy.wait_send()

    @pl.when(x != y)
    def _():
        for n, (t, _, _) in enumerate(triples):
            pltpu.make_async_copy(t, t, s_t.at[n]).wait()


def gather_weights(ids, sq, store, wq, wo, wc):
    return pl.pallas_call(
        gather_kernel,
        out_shape=(
            jax.ShapeDtypeStruct((4, NL, DE), BF16),
            jax.ShapeDtypeStruct((4, 8, 128), F32),
            jax.ShapeDtypeStruct((4, 2, 128, 2048), BF16),
            jax.ShapeDtypeStruct((4, 2, 128, 2048), BF16),
            jax.ShapeDtypeStruct((4, 2, 128, 1024), BF16),
        ),
        in_specs=[VM] * 6,
        out_specs=(VM, VM, ANY, ANY, ANY),
        scratch_shapes=[
            pltpu.VMEM((4, 8, 128), jnp.int32),
            pltpu.SMEM((4, 8, 128), jnp.int32),
            pltpu.VMEM((4, 2, NL, DE), BF16),
            pltpu.VMEM((4, 2, NL, DE), BF16),
            pltpu.VMEM((128, 512), BF16),
            pltpu.VMEM((128, 512), BF16),
            pltpu.VMEM((128, 256), BF16),
            DMA((2, 4)), DMA((2, 4)),
            DMA((4,)), DMA((4,)),
            DMA((3,)), DMA((3,)),
            DMA((3, 4)), DMA((3, 4)),
            DMA((3, 4)), DMA((3, 4)),
            DMA((3,)), DMA((3,)),
            DMA((6,)),
        ],
        compiler_params=pltpu.CompilerParams(
            collective_id=0, has_side_effects=True, vmem_limit_bytes=32 << 20
        ),
        name="gather_weights",
    )(ids, sq, store, wq, wo, wc)


def scatter_kernel(
    qp, ap, cp, wk, wv,
    q, a, cond, gk, gv,
    rq, ra, rc, yk, yv,
    s_y, r_y, s_w, r_w, s_x, r_x, s_z, r_z, s_c, r_c, s_loc,
):
    x, z, c, y = place()
    yp = [at(x, z, c, around(y, k)) for k in (1, 2, 3)]
    xp = [at(around(x, k), z, c, y) for k in (1, 2, 3)]
    zp = [at(x, around(z, k), c, y) for k in (1, 2, 3)]
    sib = at(x, z, 1 - c, y)
    meet(yp + xp + zp + [sib])
    across = []
    for n, (w, t) in enumerate(((wk, yk), (wv, yv))):
        local = pltpu.make_async_copy(w, t.at[:, cols(y, 512)], s_loc.at[n])
        local.start()
        for k in (2, 1, 3):
            across.append(
                remote(w, t.at[:, cols(y, 512)], s_w.at[n, k], r_w.at[n, k], yp[k - 1])
            )
        local.wait()
    parts = []
    for n, (p, r) in enumerate(((cp, rc), (qp, rq), (ap, ra))):
        for k in (2, 1, 3):
            parts.append(
                remote(p.at[around(y, k)], r.at[k], s_y.at[n, k], r_y.at[n, k], yp[k - 1])
            )
    pairs = ((yk, gk), (yv, gv))
    first, keep = [], []
    for n, (t, g) in enumerate(pairs):
        for copy in across[3 * n : 3 * n + 3]:
            copy.wait_recv()
        mine = g.at[x, z, c]
        local = pltpu.make_async_copy(t, mine, s_loc.at[2 + n])
        local.start()
        keep.append(local)
        for k in (2, 1, 3):
            peer = zp[k - 1] if n else xp[k - 1]
            first.append(remote(t, mine, s_x.at[n, k], r_x.at[n, k], peer))
    second = []
    for n, (t, g) in enumerate(pairs):
        keep[n].wait()
        for copy in first[3 * n : 3 * n + 3]:
            copy.wait_recv()
        block = g.at[x, :, c] if n else g.at[:, z, c]
        for k in (2, 1, 3):
            peer = xp[k - 1] if n else zp[k - 1]
            second.append(remote(block, block, s_z.at[n, k], r_z.at[n, k], peer))
    for copy in parts[:6]:
        copy.wait_recv()
    cond[...] = cp[y] + rc[1] + rc[2] + rc[3]
    sum_rows(q, [qp.at[y], rq.at[1], rq.at[2], rq.at[3]])
    third = []
    for n, (t, g) in enumerate(pairs):
        for copy in second[3 * n : 3 * n + 3]:
            copy.wait_recv()
        third.append(remote(g.at[:, :, c], g.at[:, :, c], s_c.at[n], r_c.at[n], sib))
    for copy in parts[6:]:
        copy.wait_recv()
    sum_rows(a, [ap.at[y], ra.at[1], ra.at[2], ra.at[3]])
    for copy in third:
        copy.wait_recv()
    for copy in across + parts + first + second + third:
        copy.wait_send()


def scatter_partials(qp, ap, cp, wk, wv):
    return pl.pallas_call(
        scatter_kernel,
        out_shape=(
            jax.ShapeDtypeStruct((128, 2048), BF16),
            jax.ShapeDtypeStruct((128, 2048), BF16),
            jax.ShapeDtypeStruct((2, 1024), F32),
            jax.ShapeDtypeStruct((4, 4, 2, 32, 2048), BF16),
            jax.ShapeDtypeStruct((4, 4, 2, 32, 2048), BF16),
        ),
        in_specs=[VM] * 5,
        out_specs=(VM, VM, VM, ANY, ANY),
        scratch_shapes=[
            pltpu.VMEM((4, 128, 2048), BF16),
            pltpu.VMEM((4, 128, 2048), BF16),
            pltpu.VMEM((4, 2, 1024), F32),
            pltpu.VMEM((32, 2048), BF16),
            pltpu.VMEM((32, 2048), BF16),
            DMA((3, 4)), DMA((3, 4)),
            DMA((2, 4)), DMA((2, 4)),
            DMA((2, 4)), DMA((2, 4)),
            DMA((2, 4)), DMA((2, 4)),
            DMA((2,)), DMA((2,)),
            DMA((4,)),
        ],
        compiler_params=pltpu.CompilerParams(
            collective_id=1, has_side_effects=True, vmem_limit_bytes=32 << 20
        ),
        name="scatter_partials",
    )(qp, ap, cp, wk, wv)


def ring_kernel(
    att, qag, cd, kp, vp,
    att_all, qag_all, cd_all, ko, vo,
    b_k, b_v, t_k, t_v, u_k, u_v, w_k, w_v, x_k, x_v, p_k, p_v,
    s_y, r_y, s_d, r_d, s_c, r_c, s_1, r_1, s_2, r_2, s_3, r_3, s_loc,
):
    x, z, c, y = place()
    yp = [at(x, z, c, around(y, k)) for k in (1, 2, 3)]
    xp = [at(around(x, k), z, c, y) for k in (1, 2, 3)]
    zp = [at(x, around(z, k), c, y) for k in (1, 2, 3)]
    sib = at(x, z, 1 - c, y)
    meet(yp + xp + zp + [sib])
    swaps = [
        remote(p.at[:, :, 1 - c], b, s_c.at[n], r_c.at[n], sib)
        for n, (p, b) in enumerate(((kp, b_k), (vp, b_v)))
    ]
    keep = []
    small, ring = [], []
    for k in (1, 2, 3):
        small.append(remote(cd, cd_all.at[y], s_d.at[k], r_d.at[k], yp[k - 1]))
    for n, (src, dst) in enumerate(((att, att_all), (qag, qag_all))):
        local = pltpu.make_async_copy(src, dst.at[y], s_loc.at[n])
        local.start()
        keep.append(local)
        ring.append(remote(src, dst.at[y], s_y.at[n, 0], r_y.at[n, 0], yp[0]))
        ring.append(remote(src, dst.at[y], s_y.at[n, 1], r_y.at[n, 1], yp[2]))
    cd_all[y] = cd[...]

    sent = []
    halves = ((kp, b_k, t_k, u_k), (vp, b_v, t_v, u_v))
    for n, (p, b, t, u) in enumerate(halves):
        swaps[n].wait_recv()

        def fold(i, carry, p=p, b=b, t=t):
            t[i // 4, i % 4] = (
                p[i // 4, i % 4, c].astype(F32) + b[i // 4, i % 4].astype(F32)
            ).astype(BF16)
            return carry

        lax.fori_loop(0, 16, fold, 0)
        for k in (2, 1, 3):
            if n:
                src, peer = t.at[around(x, k)], xp[k - 1]
            else:
                src, peer = t.at[:, around(z, k)], zp[k - 1]
            sent.append(remote(src, u.at[k], s_1.at[n, k], r_1.at[n, k], peer))

    passed = []
    for n, dst in enumerate((att_all, qag_all)):
        left, right = around(y, 3), around(y, 1)
        ring[2 * n].wait_recv()
        block = dst.at[left, pl.ds(0, 64)]
        passed.append(remote(block, block, s_y.at[n, 2], r_y.at[n, 2], yp[0]))
        ring[2 * n + 1].wait_recv()
        block = dst.at[right, pl.ds(64, 64)]
        passed.append(remote(block, block, s_y.at[n, 3], r_y.at[n, 3], yp[2]))

    sent2 = []
    for n, (t, u, w, v) in enumerate(((t_k, u_k, w_k, x_k), (t_v, u_v, w_v, x_v))):
        for copy in sent[3 * n : 3 * n + 3]:
            copy.wait_recv()

        def fold(i, carry, t=t, u=u, w=w, n=n):
            own = t[x, i] if n else t[i, z]
            w[i] = (
                own.astype(F32) + u[1, i].astype(F32) + u[2, i].astype(F32) + u[3, i].astype(F32)
            ).astype(BF16)
            return carry

        lax.fori_loop(0, 4, fold, 0)
        for k in (2, 1, 3):
            if n:
                src, peer = w.at[around(z, k)], zp[k - 1]
            else:
                src, peer = w.at[around(x, k)], xp[k - 1]
            sent2.append(remote(src, v.at[k], s_2.at[n, k], r_2.at[n, k], peer))
    sent3 = []
    ends = ((w_k, x_k, p_k), (w_v, x_v, p_v))
    for n, (w, v, p) in enumerate(ends):
        for copy in sent2[3 * n : 3 * n + 3]:
            copy.wait_recv()
        own = w[z] if n else w[x]
        p[0] = (
            own.astype(F32) + v[1].astype(F32) + v[2].astype(F32) + v[3].astype(F32)
        ).astype(BF16)
        for k in (2, 1, 3):
            sent3.append(
                remote(
                    p.at[0, :, cols(around(y, k), 512)],
                    p.at[k, :, pl.ds(0, 512)],
                    s_3.at[n, k],
                    r_3.at[n, k],
                    yp[k - 1],
                )
            )
    for n, (out, p) in enumerate(((ko, p_k), (vo, p_v))):
        for copy in sent3[3 * n : 3 * n + 3]:
            copy.wait_recv()
        out[...] = (
            p[0, :, cols(y, 512)].astype(F32)
            + p[1, :, pl.ds(0, 512)].astype(F32)
            + p[2, :, pl.ds(0, 512)].astype(F32)
            + p[3, :, pl.ds(0, 512)].astype(F32)
        )
    for copy in keep:
        copy.wait()
    for copy in small + passed:
        copy.wait_recv()
    for copy in swaps + small + ring + sent + passed + sent2 + sent3:
        copy.wait_send()


def ring_gather(att, qag, cd, kp, vp):
    return pl.pallas_call(
        ring_kernel,
        out_shape=(
            jax.ShapeDtypeStruct((4, 128, 2048), BF16),
            jax.ShapeDtypeStruct((4, 128, 2048), BF16),
            jax.ShapeDtypeStruct((4, 2, 1024), F32),
            jax.ShapeDtypeStruct((32, 512), F32),
            jax.ShapeDtypeStruct((32, 512), F32),
        ),
        in_specs=[VM] * 5,
        out_specs=(VM,) * 5,
        scratch_shapes=[pltpu.VMEM((4, 4, 32, 2048), BF16)] * 4
        + [pltpu.VMEM((4, 4, 32, 2048), BF16)] * 2
        + [pltpu.VMEM((4, 32, 2048), BF16)] * 6
        + [
            DMA((2, 4)), DMA((2, 4)),
            DMA((4,)), DMA((4,)),
            DMA((2,)), DMA((2,)),
            DMA((2, 4)), DMA((2, 4)),
            DMA((2, 4)), DMA((2, 4)),
            DMA((2, 4)), DMA((2, 4)),
            DMA((2,)),
        ],
        compiler_params=pltpu.CompilerParams(
            collective_id=2, has_side_effects=True, vmem_limit_bytes=56 << 20
        ),
        name="ring_gather",
    )(att, qag, cd, kp, vp)


def reduce_kernel(
    qp, op, cp, rs,
    qo, oo, co, rs_all,
    b_q, b_o, b_c, u_q, u_o, u_c, w_q, w_o, w_c, v_q, v_o, v_c, f_q, f_o, f_c,
    s_d, r_d, s_c, r_c, s_1, r_1, s_2, r_2, s_t, r_t,
):
    x, z, c, y = place()
    yp = [at(x, z, c, around(y, k)) for k in (1, 2, 3)]
    xp = [at(around(x, k), z, c, y) for k in (1, 2, 3)]
    zp = [at(x, around(z, k), c, y) for k in (1, 2, 3)]
    sib = at(x, z, 1 - c, y)
    partner = at(y, z, c, x)
    meet(yp + xp + zp + [sib], partner, x != y)
    parts = (qp, op, cp)
    swaps = [
        remote(p.at[:, 1 - c], b, s_c.at[n], r_c.at[n], sib)
        for n, (p, b) in enumerate(zip(parts, (b_q, b_o, b_c)))
    ]
    small = [
        remote(rs, rs_all.at[y], s_d.at[k], r_d.at[k], yp[k - 1]) for k in (1, 2, 3)
    ]
    rs_all[y] = rs[...]
    widths = (512, 512, 256)
    sent = []
    for n, (p, b, u, wd) in enumerate(zip(parts, (b_q, b_o, b_c), (u_q, u_o, u_c), widths)):
        swaps[n].wait_recv()

        def fold(i, carry, p=p, b=b):
            r = pl.ds(pl.multiple_of((i % 8) * 16, 16), 16)
            b[i // 8, r] = (p[i // 8, c, r].astype(F32) + b[i // 8, r].astype(F32)).astype(BF16)
            return carry

        lax.fori_loop(0, 32, fold, 0)
        for k in (2, 1, 3):
            if n == 1:
                src, peer = b.at[:, :, cols(around(x, k), wd)], xp[k - 1]
            else:
                src, peer = b.at[around(z, k)], zp[k - 1]
            sent.append(remote(src, u.at[k], s_1.at[n, k], r_1.at[n, k], peer))
    sent2 = []
    for n, (b, u, w, v, wd) in enumerate(
        zip((b_q, b_o, b_c), (u_q, u_o, u_c), (w_q, w_o, w_c), (v_q, v_o, v_c), widths)
    ):
        for copy in sent[3 * n : 3 * n + 3]:
            copy.wait_recv()

        if n == 1:

            def fold(i, carry, b=b, u=u, w=w, wd=wd):
                r = pl.ds(pl.multiple_of((i % 8) * 16, 16), 16)
                w[i // 8, r] = (
                    b[i // 8, r, cols(x, wd)].astype(F32)
                    + u[1, i // 8, r].astype(F32)
                    + u[2, i // 8, r].astype(F32)
                    + u[3, i // 8, r].astype(F32)
                ).astype(BF16)
                return carry

            lax.fori_loop(0, 32, fold, 0)
        else:
            sum_rows(w, [b.at[z], u.at[1], u.at[2], u.at[3]])
        for k in (2, 1, 3):
            if n == 1:
                src, peer = w.at[around(z, k)], zp[k - 1]
            else:
                src, peer = w.at[:, cols(around(x, k), wd)], xp[k - 1]
            sent2.append(remote(src, v.at[k], s_2.at[n, k], r_2.at[n, k], peer))
    lasts = tuple(zip((w_q, w_o, w_c), (v_q, v_o, v_c), (f_q, f_o, f_c), (qo, oo, co), widths))
    for n, (w, v, f, out, wd) in enumerate(lasts):
        for copy in sent2[3 * n : 3 * n + 3]:
            copy.wait_recv()
        own = w.at[z] if n == 1 else w.at[:, cols(x, wd)]
        sum_rows(f, [own, v.at[1], v.at[2], v.at[3]])

        @pl.when(x != y)
        def _(f=f, out=out, n=n):
            remote(f, out, s_t.at[n], r_t.at[n], partner)

        @pl.when(x == y)
        def _(f=f, out=out, n=n):
            pltpu.make_async_copy(f, out, r_t.at[n]).start()

    for n, (w, v, f, out, wd) in enumerate(lasts):
        pltpu.make_async_copy(f, out, r_t.at[n]).wait()
    for copy in small:
        copy.wait_recv()
    for copy in swaps + small + sent + sent2:
        copy.wait_send()

    @pl.when(x != y)
    def _():
        for n, (w, v, f, out, wd) in enumerate(lasts):
            pltpu.make_async_copy(f, out, s_t.at[n]).wait()


def reduce_weights(qp, op, cp, rs):
    wide, slim = (4, 128, 2048), (4, 128, 1024)
    return pl.pallas_call(
        reduce_kernel,
        out_shape=(
            jax.ShapeDtypeStruct((128, 512), BF16),
            jax.ShapeDtypeStruct((128, 512), BF16),
            jax.ShapeDtypeStruct((128, 256), BF16),
            jax.ShapeDtypeStruct((4, 8, 128), F32),
        ),
        in_specs=[VM] * 4,
        out_specs=(VM,) * 4,
        scratch_shapes=[
            pltpu.VMEM(wide, BF16), pltpu.VMEM(wide, BF16), pltpu.VMEM(slim, BF16),
            pltpu.VMEM(wide, BF16), pltpu.VMEM((4, 4, 128, 512), BF16), pltpu.VMEM(slim, BF16),
            pltpu.VMEM((128, 2048), BF16), pltpu.VMEM((4, 128, 512), BF16),
            pltpu.VMEM((128, 1024), BF16),
            pltpu.VMEM((4, 128, 512), BF16), pltpu.VMEM((4, 128, 512), BF16),
            pltpu.VMEM((4, 128, 256), BF16),
            pltpu.VMEM((128, 512), BF16), pltpu.VMEM((128, 512), BF16),
            pltpu.VMEM((128, 256), BF16),
            DMA((4,)), DMA((4,)),
            DMA((3,)), DMA((3,)),
            DMA((3, 4)), DMA((3, 4)),
            DMA((3, 4)), DMA((3, 4)),
            DMA((3,)), DMA((3,)),
        ],
        compiler_params=pltpu.CompilerParams(
            collective_id=3, has_side_effects=True, vmem_limit_bytes=56 << 20
        ),
        name="reduce_weights",
    )(qp, op, cp, rs)


def dot_nn(a, b):
    return jnp.dot(a, b, preferred_element_type=F32)


def dot_nt(a, b):
    return lax.dot_general(a, b, (((1,), (1,)), ((), ())), preferred_element_type=F32)


def dot_tn(a, b):
    return lax.dot_general(a, b, (((0,), (0,)), ((), ())), preferred_element_type=F32)


def attention_kernel(q_ref, g_ref, k_ref, v_ref, att_ref, qag_ref, kag_ref, vag_ref):
    scale = HSZ ** (-0.5)
    for h in range(q_ref.shape[1] // HSZ):
        lanes = slice(h * HSZ, (h + 1) * HSZ)
        for s in range(2):
            rows, keys = slice(s * SPAN, (s + 1) * SPAN), slice(s * 2 * NL, (s + 1) * 2 * NL)
            q, g = q_ref[rows, lanes], g_ref[rows, lanes]
            k, v = k_ref[keys, lanes], v_ref[keys, lanes]
            score = dot_nt(q, k) * scale
            e = jnp.exp(score - jnp.max(score, axis=-1, keepdims=True))
            full = e / jnp.sum(e, axis=-1, keepdims=True)
            weights = full.astype(BF16)
            att_ref[rows, lanes] = dot_nn(weights, v).astype(BF16)
            pg = dot_nt(g, v)
            sg = (full * (pg - jnp.sum(full * pg, axis=-1, keepdims=True)) * scale).astype(BF16)
            qag_ref[rows, lanes] = dot_nn(sg, k).astype(BF16)
            kag_ref[keys, lanes] = dot_tn(sg, q).astype(BF16)
            vag_ref[keys, lanes] = dot_tn(weights, g).astype(BF16)


def attention(q, g, k, v):
    few = pl.BlockSpec((128, 256), lambda h: (0, h))
    many = pl.BlockSpec((512, 256), lambda h: (0, h))
    return pl.pallas_call(
        attention_kernel,
        grid=(8,),
        out_shape=(
            jax.ShapeDtypeStruct((128, 2048), BF16),
            jax.ShapeDtypeStruct((128, 2048), BF16),
            jax.ShapeDtypeStruct((512, 2048), BF16),
            jax.ShapeDtypeStruct((512, 2048), BF16),
        ),
        in_specs=[few, few, many, many],
        out_specs=(few, few, many, many),
        name="attention",
    )(q, g, k, v)


def wide_columns(n):
    r = lax.broadcasted_iota(jnp.int32, (28 * n, 32 * n), 0)
    s = lax.broadcasted_iota(jnp.int32, (28 * n, 32 * n), 1)
    return ((r // 28 == s // 32) & (r % 28 == s % 32)).astype(BF16)


def lines(v):
    return jnp.pad(v.reshape(4, 128), ((0, 4), (0, 0)))


def shards(
    hidden, norm_gain, w_query, w_key, w_value, w_out, w_cond, enc_gain, store, neighbour_ids,
    out_grad,
):
    y = lax.axis_index("enc")
    xf = hidden.astype(F32)
    gain = lax.dynamic_slice_in_dim(norm_gain, y * 1024, 1024)
    sq = lines(jnp.sum(xf * xf, axis=-1))
    summary = jnp.mean(xf.reshape(8, SPAN, 1024), axis=1).astype(BF16)
    ids = jnp.pad(neighbour_ids.reshape(1, 4), ((0, 7), (0, 124)))
    wc = dot_nn(w_cond, wide_columns(8)).astype(BF16)
    raw, sq_all, gq, go, gc = gather_weights(ids, sq, store, w_query, w_out.T, wc)
    gq, go, gc = gq.reshape(1024, 2048), go.reshape(1024, 2048), gc.reshape(1024, 1024)

    rstd = lax.rsqrt(jnp.sum(sq_all, axis=0)[:4].reshape(512, 1) / 4096 + EPS)
    normed = (xf * rstd * gain).astype(BF16)
    qp = dot_nn(normed, gq).astype(BF16).reshape(4, 128, 2048)
    ap = dot_nn(out_grad, go).astype(BF16).reshape(4, 128, 2048)
    cp = dot_nn(summary, gc).reshape(4, 2, 1024)
    wk = jnp.pad(w_key, ((0, 4), (0, 0)))
    wv = jnp.pad(w_value, ((0, 4), (0, 0)))
    q, ag, cond, gk, gv = scatter_partials(qp, ap, cp, wk, wv)
    gk, gv = gk.reshape(PE, 2048), gv.reshape(PE, 2048)

    egain = jnp.pad(enc_gain.reshape(32, 28), ((0, 0), (0, 4))).reshape(PE)
    rawp = dot_nn(raw.reshape(512, DE), wide_columns(32))
    cond_rows = cond.astype(BF16).astype(F32)
    enc_in = (rawp.reshape(2, 256, PE) + cond_rows[:, None, :]).reshape(512, PE)
    enc_rstd = lax.rsqrt(jnp.sum(enc_in * enc_in, axis=-1, keepdims=True) / DE + EPS)
    encoded = (enc_in * enc_rstd * egain).astype(BF16)
    keys = dot_nn(encoded, gk).astype(BF16)
    values = dot_nn(encoded, gv).astype(BF16)
    att, qag, kag, vag = attention(q, ag, keys, values)
    kp = dot_tn(encoded, kag).astype(BF16).reshape(4, 4, 2, 32, 2048)
    vp = dot_tn(encoded, vag).astype(BF16).reshape(4, 4, 2, 32, 2048)
    eg = (dot_nt(kag, gk) + dot_nt(vag, gv)).astype(BF16).astype(F32)
    ey = egain * eg
    emean = jnp.sum(enc_in * ey, axis=-1, keepdims=True) / DE
    slot = jnp.sum(
        (enc_rstd * ey - enc_in * enc_rstd**3 * emean).reshape(2, 256, PE), axis=1
    )
    cd = slot.astype(BF16).astype(F32)
    att_all, qag_all, cd_all, kg, vg = ring_gather(att, qag, cd, kp, vp)
    att_all, qag_all = att_all.reshape(512, 2048), qag_all.reshape(512, 2048)
    cd_all = cd_all.reshape(8, PE).astype(BF16)

    layer_out = (xf + dot_nt(att_all, go)).astype(BF16)
    op = dot_tn(out_grad, att_all).astype(BF16).reshape(4, 2, 128, 2048)
    gp = dot_tn(normed, qag_all).astype(BF16).reshape(4, 2, 128, 2048)
    hp = dot_tn(summary, cd_all).astype(BF16).reshape(4, 2, 128, 1024)
    scaled = dot_nt(qag_all, gq) * gain
    rs = lines(jnp.sum(xf * scaled, axis=-1))
    summary_grad = dot_nt(cd_all, gc)
    qo, oo, co, rs_all = reduce_weights(gp, op, hp, rs)

    row_mean = jnp.sum(rs_all, axis=0)[:4].reshape(512, 1) / 4096
    hidden_grad = (
        out_grad.astype(F32)
        + (rstd * scaled - xf * rstd**3 * row_mean)
        + jnp.repeat(summary_grad / SPAN, SPAN, axis=0)
    )
    cond_grad = co.astype(F32).reshape(128, 8, 32)[:, :, :28].reshape(128, 224)
    return (
        layer_out,
        hidden_grad,
        qo.astype(F32),
        kg[:28],
        vg[:28],
        oo.T.astype(F32),
        cond_grad,
    )


def solution(mesh):
    placed = (
        P("dp", "enc"), P(), P("dp", "enc"), P("dp", "enc"), P("dp", "enc"), P("enc", "dp"),
        P("dp", "enc"), P(), P(("dp", "enc"), None, None), P(("dp", "enc")), P("dp", "enc"),
    )
    return jax.shard_map(
        shards,
        mesh=mesh,
        in_specs=placed,
        out_specs=(
            P("dp", "enc"), P("dp", "enc"), P("dp", "enc"), P("dp", "enc"), P("dp", "enc"),
            P("enc", "dp"), P("dp", "enc"),
        ),
        check_vma=False,
    )
```

time: 752 us -> 354 us (0.47); the launches traced: 739 us -> 353 us
  waiting for transfers between devices: 467 us -> 0 us
  Pallas kernels: 0 us -> 272 us
  matrix products: 119 us -> 54.5 us
  local copies, waits for them, and re-layouts: 60.3 us -> 16.4 us
  other arithmetic: 48.4 us -> 9.31 us
  starting transfers between devices: 22.1 us -> 0 us
  between operations: 14.9 us -> 1.19 us
  blocking collectives: 8.08 us -> 0 us
    pallas_call x0 -> x5, Pallas kernels: none -> 272 us  [the longest x1 71.5 us: reduce_weights(): pl.pallas_call(reduce_kernel, out_shape=(jax.ShapeDtypeStruct((128, 512),...]
    all_gather x7 -> x0, waiting for transfers between devices: 262 us -> none  [the longest x1 50.9 us: shards(): full_rows = lax.all_gather(hidden, 'enc', axis=1, tiled=True)]
    reduce_scatter x2 -> x0, waiting for transfers between devices: 72.6 us -> none  [the longest x1 72.6 us: one_scatter(): lax.psum_scatter(lines, axis, tiled=True).reshape(-1)]
    dot_general x21 -> x17, matrix products: 119 us -> 54.5 us  [the longest x5 19.8 us: dot_tn(): lax.dot_general(a, b, (((0,), (0,)), ((), ())), preferred_element_type=F32)]
    psum x1 -> x0, waiting for transfers between devices: 64.2 us -> none  [shards(): lax.psum(summary_term.astype(jnp.bfloat16), 'enc').astype(jnp.float32)]
    all_to_all x5 -> x0, waiting for transfers between devices: 64.1 us -> none  [the longest x2 62.2 us: summed_on_arrival(): tiles = lax.all_to_all(in_blocks(shard, dim, peers), axis, 0, 0, tiled=True)]
    all_to_all x5 -> x0, starting transfers between devices: 21 us -> none  [the longest x2 9.85 us: summed_on_arrival(): tiles = lax.all_to_all(in_blocks(shard, dim, peers), axis, 0, 0, tiled=True)]
    reduce_sum x11 -> x5, other arithmetic: 19.7 us -> 3.09 us  [the longest x1 1.6 us: shards(): sq = lines(jnp.sum(xf * xf, axis=-1))]
  transfers between devices with their start and end apart: 16 -> 0, of which waited for: 12 -> 0; matrix products, arithmetic and copies ran while one was open for 30% -> 0% of each run, Pallas kernels for 0% -> 0%
where the time goes in v1:
time: 354 us; the launch traced here: 353 us
  Pallas kernels  272 us (77%)
  matrix products  54.5 us (15%)
  local copies, waits for them, and re-layouts  16.4 us (5%)
  other arithmetic  9.31 us (3%)
    pallas_call x1, Pallas kernels, reduce_weights(): pl.pallas_call(reduce_kernel, out_shape=(jax.ShapeDtypeStruct((128, 512),...  71.5 us
    pallas_call x1, Pallas kernels, gather_weights(): pl.pallas_call(gather_kernel, out_shape=(jax.ShapeDtypeStruct((4, NL, DE)...  69.3 us
    pallas_call x1, Pallas kernels, scatter_partials(): pl.pallas_call(scatter_kernel, out_shape=(jax.ShapeDtypeStruct((128, 2048...  56.9 us
    pallas_call x1, Pallas kernels, ring_gather(): pl.pallas_call(ring_kernel, out_shape=(jax.ShapeDtypeStruct((4, 128, 2048...  54.5 us
    dot_general x5, matrix products, dot_tn(): lax.dot_general(a, b, (((0,), (0,)), ((), ())), preferred_element_type=F32)  19.8 us
    pallas_call x1, Pallas kernels, attention(): pl.pallas_call(attention_kernel, grid=(8,), out_shape=(jax.ShapeDtypeStru...  19.5 us
    dot_general x5, matrix products, dot_nt(): lax.dot_general(a, b, (((1,), (1,)), ((), ())), preferred_element_type=F32)  17.5 us
    dot_general x7, matrix products, dot_nn(): return jnp.dot(a, b, preferred_element_type=F32)  17.2 us

profile of v1, /device:TPU:7, one launch (start us, length us, event | category | flops | bytes accessed | tf_op | source)
XLA Modules:
  0.0 353.1 jit_solution(4498433740632115516)
XLA Ops:
  0.6 0.0 copy-start
  0.6 0.0 copy-start.14
  0.7 1.6 fusion.4
  2.4 0.6 fusion.58
  3.0 0.6 fusion.56
  3.5 0.7 dynamic_slice.3
  4.2 0.7 pad.22.ids
  4.9 0.8 reshape.203
  5.7 0.1 mul.127
  5.8 0.8 pad.24.wk
  6.5 0.8 pad.25.wv
  7.3 0.2 bitcast_reduce_fusion.1
  7.6 0.0 copy-done
  7.6 0.4 fusion.33.wc
  8.0 0.1 copy.24
  8.1 0.0 copy-start.2
  8.2 1.5 copy-done.2
  9.6 69.3 %gather_weights.1 = (bf16[4,128,896]{2,1,0:T(8,128)(2,1)S(1)}, f32[4,8,128]{2,1,0:T(8,128)S(1)}, bf16[4,2,128,2048]{3,2,1,0:T(8,128)(2,1)S(1)}, bf16[4,2,128,204...) custom-call(s32[8,128]{1,0:T(8,128)S(1)} %pad.22.ids, f32[8,128]{1,0:T(8,128)S(1)} %pad.23.sq, ...), custom_call_target="tpu_custom_call" | custom-call | tf_op jit(solution)/shard_map/gather_weights/pallas_call | solution.py:192
  79.0 2.0 copy-done.6
  80.9 2.0 copy-done.8
  83.0 0.4 fusion.67.cp
  83.4 0.8 copy-done.15
  84.2 4.8 %convolution_convert_fusion.7 = bf16[512,2048]{1,0:T(8,128)(2,1)S(1)} fusion(bf16[1024,2048]{1,0:T(8,128)(2,1)} %bitcast.108, bf16[512,1024]{1,0:T(8,128)(2,1)S(1)} %copy-done.15, f32[1024]{0:T(1024)S(1)} %dynamic_slice.3, f32[512]{0:T(512)S(1)} %rsqrt_bitcast_fusion), kind=kOutput, calls=%fused_computation.12 | convolution fusion | flops 2150629376 | bytes 7346176 | tf_op jit(solution)/shard_map/dot_general | solution.py:597
  88.9 0.0 copy-done.9
  89.0 0.0 copy-done.20
  89.0 2.4 convolution_convert_fusion.4
  91.3 0.0 copy-start.26
  91.3 0.0 copy-start.27
  91.4 0.0 copy-start.28
  91.4 0.0 copy-start.29
  91.4 56.9 %scatter_partials.1 = (bf16[128,2048]{1,0:T(8,128)(2,1)S(1)}, bf16[128,2048]{1,0:T(8,128)(2,1)S(1)}, f32[2,1024]{1,0:T(2,128)S(1)}, bf16[4,4,2,32,2048]{4,3,2,1,...) custom-call(bf16[4,128,2048]{2,1,0:T(8,128)(2,1)S(1)} %bitcast.105, bf16[4,128,2048]{2,1,0:T(8,128)(2,1)S(1)} %bitcast.106, ...), custom_call_target="tpu_custom_call" | custom-call | tf_op jit(solution)/shard_map/scatter_partials/pallas_call | solution.py:293
  148.2 0.0 copy-start.3
  148.3 0.0 copy-done.26
  148.3 0.0 copy-done.27
  148.3 1.8 multiply_reduce_fusion
  150.2 0.2 multiply_convert_fusion
  150.5 0.1 copy-done.11
  150.6 3.8 %convolution_convert_fusion.5.v_ref = bf16[512,2048]{1,0:T(8,128)(2,1)} fusion(bf16[512,1024]{1,0:T(8,128)(2,1)S(1)} %bitcast.122, bf16[1024,2048]{1,0:T(8,128)(2,1)S(1)} %bitcast.112), kind=kOutput, calls=%fused_computation.10 | convolution fusion | flops 2148532224 | bytes 7340032 | tf_op jit(solution)/shard_map/dot_general | solution.py:597
  154.4 3.7 %convolution_convert_fusion.6.k_ref = bf16[512,2048]{1,0:T(8,128)(2,1)} fusion(bf16[512,1024]{1,0:T(8,128)(2,1)S(1)} %bitcast.123, bf16[1024,2048]{1,0:T(8,128)(2,1)S(1)} %bitcast.114), kind=kOutput, calls=%fused_computation.11 | convolution fusion | flops 2148532224 | bytes 7340032 | tf_op jit(solution)/shard_map/dot_general | solution.py:597
  158.1 19.5 %attention.1 = (bf16[128,2048]{1,0:T(8,128)(2,1)}, bf16[128,2048]{1,0:T(8,128)(2,1)}, bf16[512,2048]{1,0:T(8,128)(2,1)}, bf16[512,2048]{1,0:T(8,128)(2,1)}) custom-call(bf16[128,2048]{1,0:T(8,128)(2,1)} %copy-done.3, bf16[128,2048]{1,0:T(8,128)(2,1)} %copy-done.4, bf16[512,2048]{1,0:T(8,128)(2,1)} %convolution_convert_fusion.6.k_ref, ...), custom_call_target="tpu_custom_call" | custom-call | tf_op jit(solution)/shard_map/attention/pallas_call | solution.py:631
  177.6 5.3 %fusion.68 = f32[512,1024]{1,0:T(8,128)S(1)} fusion(bf16[512,2048]{1,0:T(8,128)(2,1)} %get-tuple-element.42, bf16[1024,2048]{1,0:T(8,128)(2,1)} %bitcast.115), kind=kOutput, calls=%fused_computation.122 | convolution fusion | flops 2147483648 | bytes 8388608 | tf_op jit(solution)/shard_map/dot_general | solution.py:601
  182.9 2.7 fusion.17
  185.6 0.5 bitcast_reduce_fusion
  186.1 0.6 convert_element_type.208.cd
  186.7 4.4 %convolution_convert_fusion.2 = bf16[1024,2048]{1,0:T(8,128)(2,1)} fusion(bf16[512,1024]{1,0:T(8,128)(2,1)S(1)} %get-tuple-element.67, bf16[512,2048]{1,0:T(8,128)(2,1)S(1)} %copy-done.31), kind=kOutput, calls=%fused_computation.2 | convolution fusion | flops 2149580800 | bytes 7340032 | tf_op jit(solution)/shard_map/dot_general | solution.py:605
  191.2 4.4 %convolution_convert_fusion.3 = bf16[1024,2048]{1,0:T(8,128)(2,1)} fusion(bf16[512,1024]{1,0:T(8,128)(2,1)S(1)} %get-tuple-element.67, bf16[512,2048]{1,0:T(8,128)(2,1)S(1)} %copy-done.30), kind=kOutput, calls=%fused_computation.3 | convolution fusion | flops 2149580800 | bytes 7340032 | tf_op jit(solution)/shard_map/dot_general | solution.py:605
  195.5 54.5 %ring_gather.1 = (bf16[4,128,2048]{2,1,0:T(8,128)(2,1)}, bf16[4,128,2048]{2,1,0:T(8,128)(2,1)}, f32[4,2,1024]{2,1,0:T(2,128)}, f32[32,512]{1,0:T(8,128)}, f32[32,512]{1,0:T(8,128)}) custom-call(bf16[128,2048]{1,0:T(8,128)(2,1)} %get-tuple-element.40.att, bf16[128,2048]{1,0:T(8,128)(2,1)} %get-tuple-element.41.qag, f32[2,1024]{1,0:T(2,128)} %convert_element_type.208.cd, ...), custom_call_target="tpu_custom_call" | custom-call | tf_op jit(solution)/shard_map/ring_gather/pallas_call | solution.py:437
  250.1 5.1 %fusion.7 = bf16[512,1024]{1,0:T(8,128)(2,1)} fusion(bf16[512,1024]{1,0:T(8,128)(2,1)S(1)} %copy-done.16, bf16[512,2048]{1,0:T(8,128)(2,1)} %bitcast.133, bf16[1024,2048]{1,0:T(8,128)(2,1)S(1)} %bitcast.111), kind=kOutput, calls=%fused_computation.21 | convolution fusion | flops 2149056512 | bytes 8388608 | tf_op jit(solution)/shard_map/dot_general | solution.py:601
  255.2 3.7 %fusion.12 = (f32[512]{0:T(512)S(1)}, f32[512,1024]{1,0:T(8,128)}) fusion(bf16[512,1024]{1,0:T(8,128)(2,1)S(1)} %copy-done.16, f32[1024]{0:T(1024)S(1)} %dynamic_slice.3, bf16[512,2048]{1,0:T(8,128)(2,1)S(1)} %bitcast.135, bf16[1024,2048]{1,0:T(8,128)(2,1)S(1)} %bitcast.109), kind=kOutput, calls=%fused_computation.26 | convolution fusion | flops 2149580288 | bytes 9443328 | tf_op jit(solution)/shard_map/dot_general | solution.py:601
  259.0 0.6 pad.27.rs
  259.6 0.6 convolution_multiply_fusion
  260.2 2.1 convolution_convert_fusion.8
  262.4 4.5 %convolution_convert_fusion.1 = bf16[1024,2048]{1,0:T(8,128)(2,1)} fusion(bf16[512,2048]{1,0:T(8,128)(2,1)S(1)} %bitcast.136, bf16[512,1024]{1,0:T(8,128)(2,1)S(1)} %copy-done.16, f32[1024]{0:T(1024)S(1)} %dynamic_slice.3, f32[512]{0:T(512)S(1)} %rsqrt_bitcast_fusion), kind=kOutput, calls=%fused_computation.1 | convolution fusion | flops 2151677952 | bytes 7346176 | tf_op jit(solution)/shard_map/dot_general | solution.py:605
  266.9 4.4 %convolution_convert_fusion = bf16[2048,1024]{0,1:T(8,128)(2,1)} fusion(bf16[512,2048]{1,0:T(8,128)(2,1)S(1)} %bitcast.134, bf16[512,1024]{1,0:T(8,128)(2,1)S(1)} %copy-done.21), kind=kOutput, calls=%fused_computation | convolution fusion | flops 2149580800 | bytes 7340032 | tf_op jit(solution)/shard_map/dot_general | solution.py:605
  271.3 71.5 %reduce_weights.1 = (bf16[128,512]{1,0:T(8,128)(2,1)}, bf16[128,512]{1,0:T(8,128)(2,1)}, bf16[128,256]{1,0:T(8,128)(2,1)}, f32[4,8,128]{2,1,0:T(8,128)}) custom-call(bf16[4,2,128,2048]{3,2,1,0:T(8,128)(2,1)} %bitcast.118, bf16[4,2,128,2048]{3,2,1,0:T(8,128)(2,1)} %bitcast.119, bf16[4,2,128,1024]{3,2,1,0:T(8,128)(2,1)} %bitcast.117, f32[8,128]{1,0:T(8,128)} %pad.27.rs), custom_call_target="tpu_custom_call" | custom-call | tf_op jit(solution)/shard_map/reduce_weights/pallas_call | solution.py:564
  342.8 0.7 reduce_sum.79
  343.6 0.0 copy-start.1
  343.6 3.3 fusion.11
  346.9 0.9 copy.28
  347.9 0.7 reshape.221
  348.6 0.7 convert_element_type.147
  349.3 0.8 copy.29
  350.2 1.5 copy.36
  351.6 1.5 copy.37
  (78 shorter events, 0.3 us)
Async XLA Ops:
  0.6 6.9 %copy-start = (bf16[128,224]{0,1:T(8,128)(2,1)S(1)}, bf16[128,224]{0,1:T(8,128)(2,1)}, u32[]{:S(2)}) copy-start(bf16[128,224]{0,1:T(8,128)(2,1)} %param.17) | copy-start | bytes 172036
  0.6 6.7 %copy-start.14 = (bf16[512,1024]{1,0:T(8,128)(2,1)S(1)}, bf16[512,1024]{1,0:T(8,128)(2,1)}, u32[]{:S(2)}) copy-start(bf16[512,1024]{1,0:T(8,128)(2,1)} %param.11) | copy-start | bytes 3145732
  0.7 7.3 %copy-start.24 = (bf16[512,128]{1,0:T(8,128)(2,1)S(1)}, bf16[512,128]{1,0:T(8,128)(2,1)}, u32[]{:S(2)}) copy-start(bf16[512,128]{1,0:T(8,128)(2,1)} %param.16) | copy-start | bytes 393220
  0.7 7.5 %copy-start.5 = (bf16[128,512]{1,0:T(8,128)(2,1)S(1)}, bf16[128,512]{1,0:T(8,128)(2,1)}, u32[]{:S(2)}) copy-start(bf16[128,512]{1,0:T(8,128)(2,1)} %wq.1) | copy-start | bytes 393220
  8.1 1.5 copy-start.2
  79.0 2.0 copy-start.6
  80.9 2.0 copy-start.8
  83.0 1.2 copy-start.15
  84.2 4.8 %copy-start.9 = (bf16[4,2,128,2048]{3,2,1,0:T(8,128)(2,1)S(1)}, bf16[4,2,128,2048]{3,2,1,0:T(8,128)(2,1)}, u32[]{:S(2)}) copy-start(bf16[4,2,128,2048]{3,2,1,0:T(8,128)(2,1)} %copy-done.8) | copy-start | bytes 12582916
  84.2 4.8 %copy-start.20 = (bf16[512,1024]{1,0:T(8,128)(2,1)S(1)}, bf16[512,1024]{1,0:T(8,128)(2,1)}, u32[]{:S(2)}) copy-start(bf16[512,1024]{1,0:T(8,128)(2,1)} %param.21) | copy-start | bytes 3145732
  91.3 57.0 %copy-start.26 = (pred[896]{0:T(1024)(128)(4,1)S(1)}, pred[896]{0:T(1024)(128)(4,1)}, u32[]{:S(2)}) copy-start(pred[896]{0:T(1024)(128)(4,1)} %get-tuple-element.98) | copy-start | bytes 2692
  91.3 57.0 %copy-start.27 = (pred[896]{0:T(1024)(128)(4,1)S(1)}, pred[896]{0:T(1024)(128)(4,1)}, u32[]{:S(2)}) copy-start(pred[896]{0:T(1024)(128)(4,1)} %get-tuple-element.99) | copy-start | bytes 2692
  91.4 57.0 %copy-start.28 = (pred[1024]{0:T(1024)(128)(4,1)S(1)}, pred[1024]{0:T(1024)(128)(4,1)}, u32[]{:S(2)}) copy-start(pred[1024]{0:T(1024)(128)(4,1)} %get-tuple-element.96) | copy-start | bytes 3076
  91.4 57.0 %copy-start.29 = (pred[1024]{0:T(1024)(128)(4,1)S(1)}, pred[1024]{0:T(1024)(128)(4,1)}, u32[]{:S(2)}) copy-start(pred[1024]{0:T(1024)(128)(4,1)} %get-tuple-element.97) | copy-start | bytes 3076
  148.2 1.9 copy-start.3
  148.3 1.9 copy-start.4
  148.3 2.3 copy-start.11
  148.3 6.1 %copy-start.13 = (bf16[4,4,2,32,2048]{4,3,2,1,0:T(8,128)(2,1)}, bf16[4,4,2,32,2048]{4,3,2,1,0:T(8,128)(2,1)S(1)}, u32[]{:S(2)}) copy-start(bf16[4,4,2,32,2048]{4,3,2,1,0:T(8,128)(2,1)S(1)} %get-tuple-element.38) | copy-start | bytes 12582916
  150.2 4.2 %copy-start.17 = (f32[2,256,1024]{2,1,0:T(8,128)}, f32[2,256,1024]{2,1,0:T(8,128)S(1)}, u32[]{:S(2)}) copy-start(f32[2,256,1024]{2,1,0:T(8,128)S(1)} %get-tuple-element.72) | copy-start | bytes 6291460
  177.5 5.4 %copy-start.12 = (bf16[4,4,2,32,2048]{4,3,2,1,0:T(8,128)(2,1)S(1)}, bf16[4,4,2,32,2048]{4,3,2,1,0:T(8,128)(2,1)}, u32[]{:S(2)}) copy-start(bf16[4,4,2,32,2048]{4,3,2,1,0:T(8,128)(2,1)} %copy-done.11) | copy-start | bytes 12582916
  177.5 5.4 %copy-start.18 = (f32[2,256,1024]{2,1,0:T(8,128)S(1)}, f32[2,256,1024]{2,1,0:T(8,128)}, u32[]{:S(2)}) copy-start(f32[2,256,1024]{2,1,0:T(8,128)} %copy-done.17) | copy-start | bytes 6291460
  177.5 5.4 %copy-start.31 = (bf16[512,2048]{1,0:T(8,128)(2,1)S(1)}, bf16[512,2048]{1,0:T(8,128)(2,1)}, u32[]{:S(2)}) copy-start(bf16[512,2048]{1,0:T(8,128)(2,1)} %get-tuple-element.43) | copy-start | bytes 6291460
  186.7 4.4 %copy-start.30 = (bf16[512,2048]{1,0:T(8,128)(2,1)S(1)}, bf16[512,2048]{1,0:T(8,128)(2,1)}, u32[]{:S(2)}) copy-start(bf16[512,2048]{1,0:T(8,128)(2,1)} %get-tuple-element.42) | copy-start | bytes 6291460
  195.5 54.6 %copy-start.10 = (bf16[4,2,128,2048]{3,2,1,0:T(8,128)(2,1)S(1)}, bf16[4,2,128,2048]{3,2,1,0:T(8,128)(2,1)}, u32[]{:S(2)}) copy-start(bf16[4,2,128,2048]{3,2,1,0:T(8,128)(2,1)} %copy-done.8) | copy-start | bytes 12582916
  195.5 54.6 %copy-start.16 = (bf16[512,1024]{1,0:T(8,128)(2,1)S(1)}, bf16[512,1024]{1,0:T(8,128)(2,1)}, u32[]{:S(2)}) copy-start(bf16[512,1024]{1,0:T(8,128)(2,1)} %param.11) | copy-start | bytes 3145732
  250.1 5.1 %copy-start.7 = (bf16[4,2,128,2048]{3,2,1,0:T(8,128)(2,1)S(1)}, bf16[4,2,128,2048]{3,2,1,0:T(8,128)(2,1)}, u32[]{:S(2)}) copy-start(bf16[4,2,128,2048]{3,2,1,0:T(8,128)(2,1)} %copy-done.6) | copy-start | bytes 12582916
  250.1 5.1 %copy-start.33 = (bf16[4,128,2048]{2,1,0:T(8,128)(2,1)S(1)}, bf16[4,128,2048]{2,1,0:T(8,128)(2,1)}, u32[]{:S(2)}) copy-start(bf16[4,128,2048]{2,1,0:T(8,128)(2,1)} %get-tuple-element.45) | copy-start | bytes 6291460
  255.2 4.3 %copy-start.25 = (f32[4,2,1024]{2,1,0:T(2,128)S(1)}, f32[4,2,1024]{2,1,0:T(2,128)}, u32[]{:S(2)}) copy-start(f32[4,2,1024]{2,1,0:T(2,128)} %get-tuple-element.46) | copy-start | bytes 98308
  259.6 2.8 copy-start.34
  262.4 4.5 %copy-start.21 = (bf16[512,1024]{1,0:T(8,128)(2,1)S(1)}, bf16[512,1024]{1,0:T(8,128)(2,1)}, u32[]{:S(2)}) copy-start(bf16[512,1024]{1,0:T(8,128)(2,1)} %param.21) | copy-start | bytes 3145732
  262.4 4.5 %copy-start.32 = (bf16[4,128,2048]{2,1,0:T(8,128)(2,1)S(1)}, bf16[4,128,2048]{2,1,0:T(8,128)(2,1)}, u32[]{:S(2)}) copy-start(bf16[4,128,2048]{2,1,0:T(8,128)(2,1)} %get-tuple-element.44) | copy-start | bytes 6291460
  271.3 72.3 %copy-start.19 = (f32[512,1024]{1,0:T(8,128)S(1)}, f32[512,1024]{1,0:T(8,128)}, u32[]{:S(2)}) copy-start(f32[512,1024]{1,0:T(8,128)} %get-tuple-element.75) | copy-start | bytes 6291460
  343.6 5.0 %copy-start.23 = (bf16[128,512]{1,0:T(8,128)(2,1)S(1)}, bf16[128,512]{1,0:T(8,128)(2,1)}, u32[]{:S(2)}) copy-start(bf16[128,512]{1,0:T(8,128)(2,1)} %get-tuple-element.48) | copy-start | bytes 393220
  343.6 5.7 %copy-start.22 = (bf16[128,512]{1,0:T(8,128)(2,1)S(1)}, bf16[128,512]{1,0:T(8,128)(2,1)}, u32[]{:S(2)}) copy-start(bf16[128,512]{1,0:T(8,128)(2,1)} %get-tuple-element.51) | copy-start | bytes 393220
  343.6 9.5 %copy-start.1 = (bf16[128,224]{0,1:T(8,128)(2,1)S(1)}, bf16[128,224]{0,1:T(8,128)(2,1)}, u32[]{:S(2)}) copy-start(bf16[128,224]{0,1:T(8,128)(2,1)} %param.17) | copy-start | bytes 172036

commit v2 on v1

--- a/solution.py
+++ b/solution.py
@@ -75,11 +75,76 @@
     return pl.ds(pl.multiple_of(i * n, n), n)
 
 
-def gather_kernel(
-    ids, sq, store, wq, wo, wc,
-    raw, sq_all, gq, go, gc,
-    ids_all, ids_s, out_rows, in_rows, tq, to, tc,
-    s_small, r_small, s_row, r_row, s_t, r_t, s_x, r_x, s_z, r_z, s_c, r_c, s_loc,
+def pick_rows(ids_s, r):
+    every = [ids_s[r, 0, k] for k in range(4)]
+    owner = [(v // 8) % 4 for v in every]
+    row = [v % 8 for v in every]
+    rank = []
+    for k in range(4):
+        n = jnp.int32(0)
+        for j in range(k):
+            n = n + jnp.where(owner[j] == owner[k], 1, 0)
+        rank.append(n)
+    return owner, row, rank
+
+
+class Plane:
+    def __init__(self, put, line, cut, whole, axes, sems):
+        self.put, self.line, self.cut, self.whole = put, line, cut, whole
+        self.x, self.z, self.xp, self.zp, self.sib = axes
+        self.s, self.r = sems
+        self.one, self.two, self.on, self.last = [[], []], [[], []], [[], []], None
+
+    def first(self):
+        for h in range(2):
+            src, dst, keep = self.put(h)
+            for k in (2, 1, 3):
+                peer = (self.zp if h else self.xp)[k - 1]
+                self.one[h].append(remote(src, dst, self.s.at[h, k], self.r.at[h, k], peer))
+            if keep is not None:
+                copy = pltpu.make_async_copy(src, dst, self.s.at[h, 0])
+                copy.start()
+                copy.wait()
+
+    def second(self):
+        for h in range(2):
+            for copy in self.one[h]:
+                copy.wait_recv()
+            block = self.line(h, self.x if h else self.z)
+            for k in (1, 3):
+                peer = (self.xp if h else self.zp)[k - 1]
+                self.two[h].append(
+                    remote(block, block, self.s.at[h, 3 + k], self.r.at[h, 3 + k], peer)
+                )
+
+    def relay(self):
+        for h in range(2):
+            place = self.x if h else self.z
+            for j, k in ((0, 1), (1, 3)):
+                self.two[h][j].wait_recv()
+                block = self.cut(h, around(place, 4 - k), j)
+                peer = (self.xp if h else self.zp)[k - 1]
+                self.on[h].append(
+                    remote(block, block, self.s.at[h, 7 + k], self.r.at[h, 7 + k], peer)
+                )
+
+    def swap(self):
+        for copy in self.on[0] + self.on[1]:
+            copy.wait_recv()
+        self.last = remote(self.whole, self.whole, self.s.at[0, 5], self.r.at[0, 5], self.sib)
+
+    def sent(self):
+        every = self.one[0] + self.one[1] + self.two[0] + self.two[1]
+        for copy in every + self.on[0] + self.on[1] + [self.last]:
+            copy.wait_send()
+
+
+def forward_kernel(
+    ids, sq, gain, xs, og, sm, store, wq, wo, wc, wk, wv,
+    raw, sq_all, q, a, cond, nt, ogt, hq, ho, hc, gk, gv,
+    ids_all, ids_s, out_rows, in_rows, tq, to, tc, yk, yv, gq, go, gc,
+    normed, qp, ap, cp, rq, ra, rc,
+    s_small, r_small, s_row, r_row, s_t, r_t, s_p, r_p, s_w, r_w, s_y, r_y, s_loc, s_out,
 ):
     x, z, c, y = place()
     yp = [at(x, z, c, around(y, k)) for k in (1, 2, 3)]
@@ -87,119 +152,223 @@
     zp = [at(x, around(z, k), c, y) for k in (1, 2, 3)]
     sib = at(x, z, 1 - c, y)
     partner = at(y, z, c, x)
+    axes = (x, z, xp, zp, sib)
     meet(yp + xp + zp + [sib], partner, x != y)
+
+    moves = ((wq, tq), (wo, to), (wc, tc))
+
+    @pl.when(x != y)
+    def _():
+        for n, (w, t) in enumerate(moves):
+            remote(w, t, s_t.at[n], r_t.at[n], partner)
+
+    @pl.when(x == y)
+    def _():
+        for n, (w, t) in enumerate(moves):
+            pltpu.make_async_copy(w, t, r_t.at[n]).start()
 
     small = []
     for k in (1, 2, 3):
         small.append(remote(ids, ids_all.at[y], s_small.at[0, k], r_small.at[0, k], yp[k - 1]))
+    for k in (1, 2, 3):
         small.append(remote(sq, sq_all.at[y], s_small.at[1, k], r_small.at[1, k], yp[k - 1]))
-    keep_ids = pltpu.make_async_copy(ids, ids_all.at[y], s_loc.at[0])
-    keep_sq = pltpu.make_async_copy(sq, sq_all.at[y], s_loc.at[1])
-    keep_ids.start()
-    keep_sq.start()
+    across = []
+    for n, (w, t) in enumerate(((wk, yk), (wv, yv))):
+        for k in (2, 1, 3):
+            across.append(
+                remote(w, t.at[:, cols(y, 512)], s_w.at[n, k], r_w.at[n, k], yp[k - 1])
+            )
+        t[:, cols(y, 512)] = w[...]
+    ids_all[y] = ids[...]
+    sq_all[y] = sq[...]
+    for copy in small[:3]:
+        copy.wait_recv()
+    to_s = pltpu.make_async_copy(ids_all, ids_s, s_loc.at[0])
+    to_s.start()
+    to_s.wait()
+
+    row_copies = []
+    for k in (2, 1, 3, 0):
+        owner, row, rank = pick_rows(ids_s, around(y, k))
+        for n in range(2):
+            pick = jnp.int32(0)
+            for j in range(4):
+                pick = pick + jnp.where((owner[j] == y) & (rank[j] == n), row[j], 0)
+            if k:
+                out_rows[k, n] = store[pick]
+            else:
+                in_rows[y, n] = store[pick]
+        if k:
+            row_copies.append(
+                remote(out_rows.at[k], in_rows.at[y], s_row.at[k], r_row.at[k], yp[k - 1])
+            )
+
+    def weight(n, t, g, w):
+        def put(h):
+            rows = pl.ds(64 * h, 64)
+            return t.at[rows], g.at[z, c, rows, cols(x, w)], True
+
+        def line(h, i):
+            if h:
+                return g.at[:, c, pl.ds(64, 64), cols(i, w)]
+            return g.at[i, c, pl.ds(0, 64)]
+
+        def cut(h, i, j):
+            if h:
+                return g.at[:, c, pl.ds(64 + 32 * j, 32), cols(i, w)]
+            return g.at[i, c, pl.ds(32 * j, 32)]
+
+        return Plane(put, line, cut, g.at[:, c], axes, (s_p.at[n], r_p.at[n]))
+
+    pq, po, pc = weight(0, tq, gq, 512), weight(1, to, go, 512), weight(2, tc, gc, 256)
+
+    def kv_put(h):
+        return (yv, gv.at[x, z, c], True) if h else (yk, gk.at[x, z, c], True)
+
+    def kv_line(h, i):
+        return gv.at[i, :, c] if h else gk.at[:, i, c]
+
+    def kv_cut(h, i, j):
+        if h:
+            return gv.at[i, pl.ds(2 * j, 2), c]
+        return gk.at[pl.ds(2 * j, 2), i, c]
+
+    def arrived(n, w, t):
+        pltpu.make_async_copy(w, t, r_t.at[n]).wait()
+
+    arrived(0, wq, tq)
+    pq.first()
+    arrived(1, wo, to)
+    po.first()
+    pq.second()
+    arrived(2, wc, tc)
+    pc.first()
+    for copy in small[3:]:
+        copy.wait_recv()
+    total = sq_all[0] + sq_all[1] + sq_all[2] + sq_all[3]
+    rstd = lax.rsqrt(total / 4096 + EPS).T
+    for j in range(4):
+        rows = slice(128 * j, 128 * (j + 1))
+        normed[rows] = (xs[rows].astype(F32) * rstd[:, j : j + 1] * gain[...]).astype(BF16)
+    po.second()
+    pq.relay()
+    for copy in across:
+        copy.wait_recv()
+    pk = KeyPlane(kv_put, kv_line, kv_cut, (gk.at[:, :, c], gv.at[:, :, c]), axes, (s_p.at[3], r_p.at[3]))
+    pk.first()
+    pc.second()
+    pq.swap()
+    po.relay()
+
+    parts, outs = [], []
+
+    def partial(n, act, g, h, p, r, plane):
+        plane.last.wait_recv()
+        keep = pltpu.make_async_copy(g, h, s_out.at[n])
+        keep.start()
+        outs.append(keep)
+
+        def tile(i, carry):
+            lanes = cols(i, 256)
+            w = g[:, :, :, lanes].reshape(1024, 256)
+            p[:, :, lanes] = dot_nn(act[...], w).astype(BF16).reshape(4, 128, 256)
+            return carry
+
+        lax.fori_loop(0, 8, tile, 0)
+        for k in (2, 1, 3):
+            parts.append(
+                remote(p.at[around(y, k)], r.at[k], s_y.at[n, k], r_y.at[n, k], yp[k - 1])
+            )
+
+    partial(0, normed, gq, hq, qp, rq, pq)
+    pk.second()
+    po.swap()
+    pc.relay()
+    partial(1, og, go, ho, ap, ra, po)
+    pk.relay()
+    pc.swap()
+    for j in range(4):
+        rows = slice(128 * j, 128 * (j + 1))
+        nt[:, rows] = normed[rows].T
+        ogt[:, rows] = og[rows].T
+    pc.last.wait_recv()
+    keep = pltpu.make_async_copy(gc, hc, s_out.at[2])
+    keep.start()
+    outs.append(keep)
+    for i in range(4):
+        lanes = slice(256 * i, 256 * (i + 1))
+        w = gc[:, :, :, lanes].reshape(1024, 256)
+        cp[:, lanes] = dot_nn(sm[...], w)
+    for j in range(4):
+        rc[j + 4] = cp[2 * j : 2 * j + 2]
+    for k in (2, 1, 3):
+        parts.append(
+            remote(rc.at[4 + around(y, k)], rc.at[k], s_y.at[2, k], r_y.at[2, k], yp[k - 1])
+        )
+    for copy in row_copies:
+        copy.wait_recv()
+    owner, row, rank = pick_rows(ids_s, y)
+    for k in range(4):
+        raw[k] = in_rows[owner[k], jnp.minimum(rank[k], 1)]
+    pk.swap()
+    for copy in parts[:3]:
+        copy.wait_recv()
+    sum_rows(q, [qp.at[y], rq.at[1], rq.at[2], rq.at[3]])
+    for copy in parts[3:]:
+        copy.wait_recv()
+    sum_rows(a, [ap.at[y], ra.at[1], ra.at[2], ra.at[3]])
+    cond[...] = rc[4 + y] + rc[1] + rc[2] + rc[3]
+    for copy in pk.last:
+        copy.wait_recv()
+    for copy in outs:
+        copy.wait()
+    for copy in small + across + row_copies + parts:
+        copy.wait_send()
+    for plane in (pq, po, pc, pk):
+        plane.sent()
 
     @pl.when(x != y)
     def _():
-        for n, (w, t) in enumerate(((wq, tq), (wo, to), (wc, tc))):
-            remote(w, t, s_t.at[n], r_t.at[n], partner)
-
-    @pl.when(x == y)
-    def _():
-        for n, (w, t) in enumerate(((wq, tq), (wo, to), (wc, tc))):
-            pltpu.make_async_copy(w, t, r_t.at[n]).start()
-
-    keep_ids.wait()
-    keep_sq.wait()
-    for copy in small:
-        copy.wait_recv()
-    to_s = pltpu.make_async_copy(ids_all, ids_s, s_loc.at[2])
-    to_s.start()
-    to_s.wait()
-
-    def picks(r):
-        every = [ids_s[r, 0, k] for k in range(4)]
-        owner = [(v // 8) % 4 for v in every]
-        row = [v % 8 for v in every]
-        rank = []
-        for k in range(4):
-            n = jnp.int32(0)
-            for j in range(k):
-                n = n + jnp.where(owner[j] == owner[k], 1, 0)
-            rank.append(n)
-        return owner, row, rank
-
-    row_copies = []
-    for k in (2, 1, 3):
-        r = around(y, k)
-        owner, row, rank = picks(r)
-        for q in range(2):
-            pick = jnp.int32(0)
-            for j in range(4):
-                pick = pick + jnp.where((owner[j] == y) & (rank[j] == q), row[j], 0)
-            out_rows[k, q] = store[pick]
-        row_copies.append(
-            remote(out_rows.at[k], in_rows.at[y], s_row.at[k], r_row.at[k], yp[k - 1])
-        )
-    owner, row, rank = picks(y)
-    for q in range(2):
-        pick = jnp.int32(0)
-        for j in range(4):
-            pick = pick + jnp.where((owner[j] == y) & (rank[j] == q), row[j], 0)
-        in_rows[y, q] = store[pick]
-
-    triples = ((tq, gq, 512), (to, go, 512), (tc, gc, 256))
-    first, keep = [], []
-    for n, (t, g, w) in enumerate(triples):
-        pltpu.make_async_copy(t, t, r_t.at[n]).wait()
-        mine = g.at[z, c, :, cols(x, w)]
-        local = pltpu.make_async_copy(t, mine, s_loc.at[3 + n])
-        local.start()
-        keep.append(local)
-        for k in (2, 1, 3):
-            peer = zp[k - 1] if n == 1 else xp[k - 1]
-            first.append(remote(t, mine, s_x.at[n, k], r_x.at[n, k], peer))
-    second = []
-    for n, (t, g, w) in enumerate(triples):
-        keep[n].wait()
-        for copy in first[3 * n : 3 * n + 3]:
+        for n, (w, t) in enumerate(moves):
+            pltpu.make_async_copy(w, t, s_t.at[n]).wait()
+
+
+class KeyPlane(Plane):
+    def swap(self):
+        for copy in self.on[0] + self.on[1]:
             copy.wait_recv()
-        block = g.at[:, c, :, cols(x, w)] if n == 1 else g.at[z, c]
-        for k in (2, 1, 3):
-            peer = xp[k - 1] if n == 1 else zp[k - 1]
-            second.append(remote(block, block, s_z.at[n, k], r_z.at[n, k], peer))
-    third = []
-    for n, (t, g, w) in enumerate(triples):
-        for copy in second[3 * n : 3 * n + 3]:
-            copy.wait_recv()
-        third.append(remote(g.at[:, c], g.at[:, c], s_c.at[n], r_c.at[n], sib))
-
-    for copy in row_copies:
-        copy.wait_recv()
-    for k in range(4):
-        raw[k] = in_rows[owner[k], jnp.minimum(rank[k], 1)]
-    for copy in third:
-        copy.wait_recv()
-    for copy in small + row_copies + first + second + third:
-        copy.wait_send()
-
-    @pl.when(x != y)
-    def _():
-        for n, (t, _, _) in enumerate(triples):
-            pltpu.make_async_copy(t, t, s_t.at[n]).wait()
-
-
-def gather_weights(ids, sq, store, wq, wo, wc):
+        self.last = [
+            remote(ref, ref, self.s.at[n, 5], self.r.at[n, 5], self.sib)
+            for n, ref in enumerate(self.whole)
+        ]
+
+    def sent(self):
+        every = self.one[0] + self.one[1] + self.two[0] + self.two[1]
+        for copy in every + self.on[0] + self.on[1] + self.last:
+            copy.wait_send()
+
+
+def forward(ids, sq, gain, xs, og, sm, store, wq, wo, wc, wk, wv):
+    wide, slim, keys = (4, 2, 128, 2048), (4, 2, 128, 1024), (4, 4, 2, 32, 2048)
+    shape = jax.ShapeDtypeStruct
     return pl.pallas_call(
-        gather_kernel,
+        forward_kernel,
         out_shape=(
-            jax.ShapeDtypeStruct((4, NL, DE), BF16),
-            jax.ShapeDtypeStruct((4, 8, 128), F32),
-            jax.ShapeDtypeStruct((4, 2, 128, 2048), BF16),
-            jax.ShapeDtypeStruct((4, 2, 128, 2048), BF16),
-            jax.ShapeDtypeStruct((4, 2, 128, 1024), BF16),
+            shape((4, NL, DE), BF16),
+            shape((4, 8, 128), F32),
+            shape((128, 2048), BF16),
+            shape((128, 2048), BF16),
+            shape((2, 1024), F32),
+            shape((1024, 512), BF16),
+            shape((1024, 512), BF16),
+            shape(wide, BF16),
+            shape(wide, BF16),
+            shape(slim, BF16),
+            shape(keys, BF16),
+            shape(keys, BF16),
         ),
-        in_specs=[VM] * 6,
-        out_specs=(VM, VM, ANY, ANY, ANY),
+        in_specs=[VM] * 12,
+        out_specs=(VM,) * 7 + (ANY,) * 5,
         scratch_shapes=[
             pltpu.VMEM((4, 8, 128), jnp.int32),
             pltpu.SMEM((4, 8, 128), jnp.int32),
@@ -208,117 +377,32 @@
             pltpu.VMEM((128, 512), BF16),
             pltpu.VMEM((128, 512), BF16),
             pltpu.VMEM((128, 256), BF16),
+            pltpu.VMEM((32, 2048), BF16),
+            pltpu.VMEM((32, 2048), BF16),
+            pltpu.VMEM(wide, BF16),
+            pltpu.VMEM(wide, BF16),
+            pltpu.VMEM(slim, BF16),
+            pltpu.VMEM((512, 1024), BF16),
+            pltpu.VMEM((4, 128, 2048), BF16),
+            pltpu.VMEM((4, 128, 2048), BF16),
+            pltpu.VMEM((8, 1024), F32),
+            pltpu.VMEM((4, 128, 2048), BF16),
+            pltpu.VMEM((4, 128, 2048), BF16),
+            pltpu.VMEM((8, 2, 1024), F32),
             DMA((2, 4)), DMA((2, 4)),
             DMA((4,)), DMA((4,)),
             DMA((3,)), DMA((3,)),
+            DMA((4, 2, 11)), DMA((4, 2, 11)),
+            DMA((2, 4)), DMA((2, 4)),
             DMA((3, 4)), DMA((3, 4)),
-            DMA((3, 4)), DMA((3, 4)),
-            DMA((3,)), DMA((3,)),
-            DMA((6,)),
+            DMA((1,)),
+            DMA((3,)),
         ],
         compiler_params=pltpu.CompilerParams(
-            collective_id=0, has_side_effects=True, vmem_limit_bytes=32 << 20
+            collective_id=0, has_side_effects=True, vmem_limit_bytes=52 << 20
         ),
-        name="gather_weights",
-    )(ids, sq, store, wq, wo, wc)
-
-
-def scatter_kernel(
-    qp, ap, cp, wk, wv,
-    q, a, cond, gk, gv,
-    rq, ra, rc, yk, yv,
-    s_y, r_y, s_w, r_w, s_x, r_x, s_z, r_z, s_c, r_c, s_loc,
-):
-    x, z, c, y = place()
-    yp = [at(x, z, c, around(y, k)) for k in (1, 2, 3)]
-    xp = [at(around(x, k), z, c, y) for k in (1, 2, 3)]
-    zp = [at(x, around(z, k), c, y) for k in (1, 2, 3)]
-    sib = at(x, z, 1 - c, y)
-    meet(yp + xp + zp + [sib])
-    across = []
-    for n, (w, t) in enumerate(((wk, yk), (wv, yv))):
-        local = pltpu.make_async_copy(w, t.at[:, cols(y, 512)], s_loc.at[n])
-        local.start()
-        for k in (2, 1, 3):
-            across.append(
-                remote(w, t.at[:, cols(y, 512)], s_w.at[n, k], r_w.at[n, k], yp[k - 1])
-            )
-        local.wait()
-    parts = []
-    for n, (p, r) in enumerate(((cp, rc), (qp, rq), (ap, ra))):
-        for k in (2, 1, 3):
-            parts.append(
-                remote(p.at[around(y, k)], r.at[k], s_y.at[n, k], r_y.at[n, k], yp[k - 1])
-            )
-    pairs = ((yk, gk), (yv, gv))
-    first, keep = [], []
-    for n, (t, g) in enumerate(pairs):
-        for copy in across[3 * n : 3 * n + 3]:
-            copy.wait_recv()
-        mine = g.at[x, z, c]
-        local = pltpu.make_async_copy(t, mine, s_loc.at[2 + n])
-        local.start()
-        keep.append(local)
-        for k in (2, 1, 3):
-            peer = zp[k - 1] if n else xp[k - 1]
-            first.append(remote(t, mine, s_x.at[n, k], r_x.at[n, k], peer))
-    second = []
-    for n, (t, g) in enumerate(pairs):
-        keep[n].wait()
-        for copy in first[3 * n : 3 * n + 3]:
-            copy.wait_recv()
-        block = g.at[x, :, c] if n else g.at[:, z, c]
-        for k in (2, 1, 3):
-            peer = xp[k - 1] if n else zp[k - 1]
-            second.append(remote(block, block, s_z.at[n, k], r_z.at[n, k], peer))
-    for copy in parts[:6]:
-        copy.wait_recv()
-    cond[...] = cp[y] + rc[1] + rc[2] + rc[3]
-    sum_rows(q, [qp.at[y], rq.at[1], rq.at[2], rq.at[3]])
-    third = []
-    for n, (t, g) in enumerate(pairs):
-        for copy in second[3 * n : 3 * n + 3]:
-            copy.wait_recv()
-        third.append(remote(g.at[:, :, c], g.at[:, :, c], s_c.at[n], r_c.at[n], sib))
-    for copy in parts[6:]:
-        copy.wait_recv()
-    sum_rows(a, [ap.at[y], ra.at[1], ra.at[2], ra.at[3]])
-    for copy in third:
-        copy.wait_recv()
-    for copy in across + parts + first + second + third:
-        copy.wait_send()
-
-
-def scatter_partials(qp, ap, cp, wk, wv):
-    return pl.pallas_call(
-        scatter_kernel,
-        out_shape=(
-            jax.ShapeDtypeStruct((128, 2048), BF16),
-            jax.ShapeDtypeStruct((128, 2048), BF16),
-            jax.ShapeDtypeStruct((2, 1024), F32),
-            jax.ShapeDtypeStruct((4, 4, 2, 32, 2048), BF16),
-            jax.ShapeDtypeStruct((4, 4, 2, 32, 2048), BF16),
-        ),
-        in_specs=[VM] * 5,
-        out_specs=(VM, VM, VM, ANY, ANY),
-        scratch_shapes=[
-            pltpu.VMEM((4, 128, 2048), BF16),
-            pltpu.VMEM((4, 128, 2048), BF16),
-            pltpu.VMEM((4, 2, 1024), F32),
-            pltpu.VMEM((32, 2048), BF16),
-            pltpu.VMEM((32, 2048), BF16),
-            DMA((3, 4)), DMA((3, 4)),
-            DMA((2, 4)), DMA((2, 4)),
-            DMA((2, 4)), DMA((2, 4)),
-            DMA((2, 4)), DMA((2, 4)),
-            DMA((2,)), DMA((2,)),
-            DMA((4,)),
-        ],
-        compiler_params=pltpu.CompilerParams(
-            collective_id=1, has_side_effects=True, vmem_limit_bytes=32 << 20
-        ),
-        name="scatter_partials",
-    )(qp, ap, cp, wk, wv)
+        name="forward",
+    )(ids, sq, gain, xs, og, sm, store, wq, wo, wc, wk, wv)
 
 
 def ring_kernel(
@@ -664,18 +748,15 @@
     summary = jnp.mean(xf.reshape(8, SPAN, 1024), axis=1).astype(BF16)
     ids = jnp.pad(neighbour_ids.reshape(1, 4), ((0, 7), (0, 124)))
     wc = dot_nn(w_cond, wide_columns(8)).astype(BF16)
-    raw, sq_all, gq, go, gc = gather_weights(ids, sq, store, w_query, w_out.T, wc)
-    gq, go, gc = gq.reshape(1024, 2048), go.reshape(1024, 2048), gc.reshape(1024, 1024)
-
-    rstd = lax.rsqrt(jnp.sum(sq_all, axis=0)[:4].reshape(512, 1) / 4096 + EPS)
-    normed = (xf * rstd * gain).astype(BF16)
-    qp = dot_nn(normed, gq).astype(BF16).reshape(4, 128, 2048)
-    ap = dot_nn(out_grad, go).astype(BF16).reshape(4, 128, 2048)
-    cp = dot_nn(summary, gc).reshape(4, 2, 1024)
     wk = jnp.pad(w_key, ((0, 4), (0, 0)))
     wv = jnp.pad(w_value, ((0, 4), (0, 0)))
-    q, ag, cond, gk, gv = scatter_partials(qp, ap, cp, wk, wv)
+    raw, sq_all, q, ag, cond, normed_t, out_grad_t, gq, go, gc, gk, gv = forward(
+        ids, sq, gain.reshape(1, 1024), hidden, out_grad, summary, store,
+        w_query, w_out.T, wc, wk, wv,
+    )
+    gq, go, gc = gq.reshape(1024, 2048), go.reshape(1024, 2048), gc.reshape(1024, 1024)
     gk, gv = gk.reshape(PE, 2048), gv.reshape(PE, 2048)
+    rstd = lax.rsqrt(jnp.sum(sq_all, axis=0)[:4].reshape(512, 1) / 4096 + EPS)
 
     egain = jnp.pad(enc_gain.reshape(32, 28), ((0, 0), (0, 4))).reshape(PE)
     rawp = dot_nn(raw.reshape(512, DE), wide_columns(32))
@@ -700,8 +781,8 @@
     cd_all = cd_all.reshape(8, PE).astype(BF16)
 
     layer_out = (xf + dot_nt(att_all, go)).astype(BF16)
-    op = dot_tn(out_grad, att_all).astype(BF16).reshape(4, 2, 128, 2048)
-    gp = dot_tn(normed, qag_all).astype(BF16).reshape(4, 2, 128, 2048)
+    op = dot_nn(out_grad_t, att_all).astype(BF16).reshape(4, 2, 128, 2048)
+    gp = dot_nn(normed_t, qag_all).astype(BF16).reshape(4, 2, 128, 2048)
     hp = dot_tn(summary, cd_all).astype(BF16).reshape(4, 2, 128, 1024)
     scaled = dot_nt(qag_all, gq) * gain
     rs = lines(jnp.sum(xf * scaled, axis=-1))

time: 354 us -> 318 us (0.90)
  Pallas kernels: 272 us -> 248 us
  local copies, waits for them, and re-layouts: 16.4 us -> 9.96 us
  matrix products: 54.5 us -> 49.4 us
    pallas_call x2 -> x1, Pallas kernels: 126 us -> 105 us  [forward(): pl.pallas_call(forward_kernel, out_shape=(shape((4, NL, DE), BF16), shape...]
    dot_general x5 -> x3, matrix products: 19.8 us -> 10.9 us  [dot_tn(): lax.dot_general(a, b, (((0,), (0,)), ((), ())), preferred_element_type=F32)]
    unnamed x75 -> x59, local copies, waits for them, and re-layouts: 10.4 us -> 4.83 us
    dot_general x7 -> x6, matrix products: 17.2 us -> 21 us  [dot_nn(): return jnp.dot(a, b, preferred_element_type=F32)]
where the time goes in v2:
time: 318 us; the launch traced here: 317 us
  Pallas kernels  248 us (78%)
  matrix products  49.4 us (16%)
  local copies, waits for them, and re-layouts  9.96 us (3%)
  other arithmetic  8.6 us (3%)
    pallas_call x1, Pallas kernels, forward(): pl.pallas_call(forward_kernel, out_shape=(shape((4, NL, DE), BF16), shape...  105 us
    pallas_call x1, Pallas kernels, reduce_weights(): pl.pallas_call(reduce_kernel, out_shape=(jax.ShapeDtypeStruct((128, 512),...  71.6 us
    pallas_call x1, Pallas kernels, ring_gather(): pl.pallas_call(ring_kernel, out_shape=(jax.ShapeDtypeStruct((4, 128, 2048...  51.9 us
    dot_general x6, matrix products, dot_nn(): return jnp.dot(a, b, preferred_element_type=F32)  21 us
    pallas_call x1, Pallas kernels, attention(): pl.pallas_call(attention_kernel, grid=(8,), out_shape=(jax.ShapeDtypeStru...  19.5 us
    dot_general x5, matrix products, dot_nt(): lax.dot_general(a, b, (((1,), (1,)), ((), ())), preferred_element_type=F32)  17.5 us
    dot_general x3, matrix products, dot_tn(): lax.dot_general(a, b, (((0,), (0,)), ((), ())), preferred_element_type=F32)  10.9 us

profile of v2, /device:TPU:7, one launch (start us, length us, event | category | flops | bytes accessed | tf_op | source)
XLA Modules:
  0.0 317.0 jit_solution(17017933991347366593)
XLA Ops:
  0.6 0.0 copy-start
  0.6 0.0 copy-start.5
  0.7 0.0 copy-start.11
  0.7 0.0 copy-start.4
  0.7 1.6 multiply_reduce_fusion.2
  2.4 0.7 dynamic_slice.3
  3.1 0.7 pad.22.ids
  3.8 0.8 reshape.186
  4.6 0.1 mul.111
  4.7 0.8 pad.24.wk
  5.4 0.8 pad.25.wv
  6.2 0.0 copy-done.5
  6.2 0.2 bitcast_reduce_fusion.1
  6.4 0.0 copy-done
  6.5 0.4 fusion.24.wc
  6.9 0.0 copy-done.11
  6.9 0.1 copy.22
  7.0 0.0 copy-done.4
  7.0 105.0 %forward.1 = (bf16[4,128,896]{2,1,0:T(8,128)(2,1)}, f32[4,8,128]{2,1,0:T(8,128)S(1)}, bf16[128,2048]{1,0:T(8,128)(2,1)S(1)}, bf16[128,2048]{1,0:T(8,128)(2,1)S(1...) custom-call(s32[8,128]{1,0:T(8,128)S(1)} %pad.22.ids, ...), custom_call_target="tpu_custom_call" | custom-call | tf_op jit(solution)/shard_map/forward/pallas_call | solution.py:354
  112.0 0.0 copy-start.2
  112.0 0.8 copy-done.2
  112.8 0.8 copy-done.3
  113.6 0.0 copy-start.18
  113.7 3.1 multiply_reduce_fusion.1
  116.8 0.2 multiply_convert_fusion
  117.0 0.0 copy-done.18
  117.1 3.7 %convolution_convert_fusion.4.v_ref = bf16[512,2048]{1,0:T(8,128)(2,1)} fusion(bf16[512,1024]{1,0:T(8,128)(2,1)S(1)} %bitcast.100, bf16[1024,2048]{1,0:T(8,128)(2,1)S(1)} %bitcast.113), kind=kOutput, calls=%fused_computation.9 | convolution fusion | flops 2148532224 | bytes 7340032 | tf_op jit(solution)/shard_map/dot_general | solution.py:681
  120.8 3.7 %convolution_convert_fusion.5.k_ref = bf16[512,2048]{1,0:T(8,128)(2,1)} fusion(bf16[512,1024]{1,0:T(8,128)(2,1)S(1)} %bitcast.101, bf16[1024,2048]{1,0:T(8,128)(2,1)S(1)} %bitcast.116), kind=kOutput, calls=%fused_computation.10 | convolution fusion | flops 2148532224 | bytes 7340032 | tf_op jit(solution)/shard_map/dot_general | solution.py:681
  124.5 19.5 %attention.1 = (bf16[128,2048]{1,0:T(8,128)(2,1)}, bf16[128,2048]{1,0:T(8,128)(2,1)}, bf16[512,2048]{1,0:T(8,128)(2,1)}, bf16[512,2048]{1,0:T(8,128)(2,1)}) custom-call(bf16[128,2048]{1,0:T(8,128)(2,1)} %copy-done.2, bf16[128,2048]{1,0:T(8,128)(2,1)} %copy-done.3, bf16[512,2048]{1,0:T(8,128)(2,1)} %convolution_convert_fusion.5.k_ref, ...), custom_call_target="tpu_custom_call" | custom-call | tf_op jit(solution)/shard_map/attention/pallas_call | solution.py:715
  144.0 0.0 copy-start.22
  144.0 5.3 %fusion.56 = f32[512,1024]{1,0:T(8,128)S(1)} fusion(bf16[512,2048]{1,0:T(8,128)(2,1)} %get-tuple-element.40, bf16[1024,2048]{1,0:T(8,128)(2,1)} %bitcast.115), kind=kOutput, calls=%fused_computation.109 | convolution fusion | flops 2147483648 | bytes 8388608 | tf_op jit(solution)/shard_map/dot_general | solution.py:685
  149.3 2.8 fusion.8
  152.1 0.6 bitcast_reduce_fusion
  152.7 0.6 convert_element_type.151.cd
  153.3 4.4 %convolution_convert_fusion.2 = bf16[1024,2048]{1,0:T(8,128)(2,1)} fusion(bf16[512,1024]{1,0:T(8,128)(2,1)S(1)} %get-tuple-element.71, bf16[512,2048]{1,0:T(8,128)(2,1)S(1)} %copy-done.22), kind=kOutput, calls=%fused_computation.2 | convolution fusion | flops 2149580800 | bytes 7340032 | tf_op jit(solution)/shard_map/dot_general | solution.py:689
  157.6 4.4 %convolution_convert_fusion.3 = bf16[1024,2048]{1,0:T(8,128)(2,1)} fusion(bf16[512,1024]{1,0:T(8,128)(2,1)S(1)} %get-tuple-element.71, bf16[512,2048]{1,0:T(8,128)(2,1)S(1)} %copy-done.21), kind=kOutput, calls=%fused_computation.3 | convolution fusion | flops 2149580800 | bytes 7340032 | tf_op jit(solution)/shard_map/dot_general | solution.py:689
  162.0 51.9 %ring_gather.1 = (bf16[4,128,2048]{2,1,0:T(8,128)(2,1)}, bf16[4,128,2048]{2,1,0:T(8,128)(2,1)}, f32[4,2,1024]{2,1,0:T(2,128)}, f32[32,512]{1,0:T(8,128)}, f32[32,512]{1,0:T(8,128)}) custom-call(bf16[128,2048]{1,0:T(8,128)(2,1)} %get-tuple-element.38.att, bf16[128,2048]{1,0:T(8,128)(2,1)} %get-tuple-element.39.qag, f32[2,1024]{1,0:T(2,128)} %convert_element_type.151.cd, ...), custom_call_target="tpu_custom_call" | custom-call | tf_op jit(solution)/shard_map/ring_gather/pallas_call | solution.py:521
  213.9 5.1 %add_convert_fusion = bf16[512,1024]{1,0:T(8,128)(2,1)} fusion(bf16[512,1024]{1,0:T(8,128)(2,1)S(1)} %copy-done.6, bf16[512,2048]{1,0:T(8,128)(2,1)} %bitcast.117, bf16[1024,2048]{1,0:T(8,128)(2,1)S(1)} %bitcast.112), kind=kOutput, calls=%fused_computation.23 | convolution fusion | flops 2149056512 | bytes 8388608 | tf_op jit(solution)/shard_map/dot_general | solution.py:685
  219.1 0.0 copy-done.16
  219.1 3.7 %multiply_reduce_fusion = (f32[512]{0:T(512)S(1)}, f32[512,1024]{1,0:T(8,128)}) fusion(bf16[512,1024]{1,0:T(8,128)(2,1)S(1)} %copy-done.6, f32[1024]{0:T(1024)S(1)} %dynamic_slice.3, bf16[512,2048]{1,0:T(8,128)(2,1)S(1)} %bitcast.119, bf16[1024,2048]{1,0:T(8,128)(2,1)S(1)} %bitcast.111), kind=kOutput, calls=%fused_computation.22 | convolution fusion | flops 2149580288 | bytes 9443328 | tf_op jit(solution)/shard_map/dot_general | solution.py:685
  222.8 0.6 pad.27.rs
  223.4 0.0 copy-done.8
  223.4 0.0 copy-start.25
  223.4 0.6 convolution_multiply_fusion
  224.1 0.9 copy-done.25
  225.0 5.7 %convolution_convert_fusion.1 = bf16[1024,2048]{1,0:T(8,128)(2,1)} fusion(bf16[1024,512]{1,0:T(8,128)(2,1)} %get-tuple-element.47, bf16[512,2048]{1,0:T(8,128)(2,1)S(1)} %bitcast.120), kind=kOutput, calls=%fused_computation.1 | convolution fusion | flops 2149580800 | bytes 7340032 | tf_op jit(solution)/shard_map/dot_general | solution.py:681
  230.7 4.3 %convolution_convert_fusion = bf16[1024,2048]{1,0:T(8,128)(2,1)} fusion(bf16[1024,512]{1,0:T(8,128)(2,1)S(1)} %copy-done.26, bf16[512,2048]{1,0:T(8,128)(2,1)S(1)} %bitcast.118), kind=kOutput, calls=%fused_computation | convolution fusion | flops 2149580800 | bytes 7340032 | tf_op jit(solution)/shard_map/dot_general | solution.py:681
  235.0 2.1 convolution_convert_fusion.6
  237.2 71.6 %reduce_weights.1 = (bf16[128,512]{1,0:T(8,128)(2,1)}, bf16[128,512]{1,0:T(8,128)(2,1)}, bf16[128,256]{1,0:T(8,128)(2,1)}, f32[4,8,128]{2,1,0:T(8,128)}) custom-call(bf16[4,2,128,2048]{3,2,1,0:T(8,128)(2,1)} %bitcast.95, bf16[4,2,128,2048]{3,2,1,0:T(8,128)(2,1)} %bitcast.96, bf16[4,2,128,1024]{3,2,1,0:T(8,128)(2,1)} %bitcast.94, f32[8,128]{1,0:T(8,128)} %pad.27.rs), custom_call_target="tpu_custom_call" | custom-call | tf_op jit(solution)/shard_map/reduce_weights/pallas_call | solution.py:648
  308.8 0.7 reduce_sum.79
  309.6 0.0 copy-done.7
  309.6 0.0 copy-start.10
  309.6 0.0 copy-start.9
  309.6 0.0 copy-start.13
  309.6 0.0 copy-start.12
  309.6 0.0 copy-start.1
  309.6 3.7 %bitcast_add_fusion = f32[512,1024]{1,0:T(8,128)} fusion(bf16[512,1024]{1,0:T(8,128)(2,1)S(1)} %copy-done.7, bf16[512,1024]{1,0:T(8,128)(2,1)S(1)} %copy-done.6, f32[512,1024]{1,0:T(8,128)} %get-tuple-element.79, f32[8,1024]{1,0:T(8,128)S(1)} %convolution_multiply_fusion, f32[512]{0:T(512)S(1)} %multiply_bitcast_fusion, f32[512]{0:T(512)S(1)} %multiply_multiply_fusion, ...), kind=kLoop, calls=%fused_computation.11 | loop fusion | flops 4718592 | bytes 6334464 | tf_op jit(solution)/shard_map/add | solution.py:794
  313.4 0.1 copy.24
  313.5 0.7 reshape.207
  314.2 0.0 copy-done.10
  314.2 0.7 convert_element_type.116
  314.9 0.8 copy.25
  315.8 0.6 copy.30
  316.4 0.6 copy.31
  (57 shorter events, 0.3 us)
Async XLA Ops:
  0.6 5.8 %copy-start = (bf16[128,224]{0,1:T(8,128)(2,1)S(1)}, bf16[128,224]{0,1:T(8,128)(2,1)}, u32[]{:S(2)}) copy-start(bf16[128,224]{0,1:T(8,128)(2,1)} %param.17) | copy-start | bytes 172036
  0.6 5.6 %copy-start.5 = (bf16[512,1024]{1,0:T(8,128)(2,1)S(1)}, bf16[512,1024]{1,0:T(8,128)(2,1)}, u32[]{:S(2)}) copy-start(bf16[512,1024]{1,0:T(8,128)(2,1)} %xs.1) | copy-start | bytes 3145732
  0.7 6.2 %copy-start.11 = (bf16[512,128]{1,0:T(8,128)(2,1)S(1)}, bf16[512,128]{1,0:T(8,128)(2,1)}, u32[]{:S(2)}) copy-start(bf16[512,128]{1,0:T(8,128)(2,1)} %param.16) | copy-start | bytes 393220
  0.7 6.3 %copy-start.4 = (bf16[128,512]{1,0:T(8,128)(2,1)S(1)}, bf16[128,512]{1,0:T(8,128)(2,1)}, u32[]{:S(2)}) copy-start(bf16[128,512]{1,0:T(8,128)(2,1)} %wq.1) | copy-start | bytes 393220
  112.0 0.8 copy-start.2
  112.8 0.8 copy-start.3
  113.6 3.4 %copy-start.18 = (bf16[4,4,2,32,2048]{4,3,2,1,0:T(8,128)(2,1)S(1)}, bf16[4,4,2,32,2048]{4,3,2,1,0:T(8,128)(2,1)}, u32[]{:S(2)}) copy-start(bf16[4,4,2,32,2048]{4,3,2,1,0:T(8,128)(2,1)} %get-tuple-element.37) | copy-start | bytes 12582916
  117.1 3.8 %copy-start.20 = (bf16[4,4,2,32,2048]{4,3,2,1,0:T(8,128)(2,1)S(1)}, bf16[4,4,2,32,2048]{4,3,2,1,0:T(8,128)(2,1)}, u32[]{:S(2)}) copy-start(bf16[4,4,2,32,2048]{4,3,2,1,0:T(8,128)(2,1)} %get-tuple-element.36) | copy-start | bytes 12582916
  144.0 5.4 %copy-start.19 = (bf16[4,4,2,32,2048]{4,3,2,1,0:T(8,128)(2,1)S(1)}, bf16[4,4,2,32,2048]{4,3,2,1,0:T(8,128)(2,1)}, u32[]{:S(2)}) copy-start(bf16[4,4,2,32,2048]{4,3,2,1,0:T(8,128)(2,1)} %get-tuple-element.37) | copy-start | bytes 12582916
  144.0 5.4 %copy-start.22 = (bf16[512,2048]{1,0:T(8,128)(2,1)S(1)}, bf16[512,2048]{1,0:T(8,128)(2,1)}, u32[]{:S(2)}) copy-start(bf16[512,2048]{1,0:T(8,128)(2,1)} %get-tuple-element.41) | copy-start | bytes 6291460
  153.3 4.4 %copy-start.21 = (bf16[512,2048]{1,0:T(8,128)(2,1)S(1)}, bf16[512,2048]{1,0:T(8,128)(2,1)}, u32[]{:S(2)}) copy-start(bf16[512,2048]{1,0:T(8,128)(2,1)} %get-tuple-element.40) | copy-start | bytes 6291460
  162.0 51.9 %copy-start.6 = (bf16[512,1024]{1,0:T(8,128)(2,1)S(1)}, bf16[512,1024]{1,0:T(8,128)(2,1)}, u32[]{:S(2)}) copy-start(bf16[512,1024]{1,0:T(8,128)(2,1)} %xs.1) | copy-start | bytes 3145732
  162.0 51.9 %copy-start.17 = (bf16[4,2,128,2048]{3,2,1,0:T(8,128)(2,1)S(1)}, bf16[4,2,128,2048]{3,2,1,0:T(8,128)(2,1)}, u32[]{:S(2)}) copy-start(bf16[4,2,128,2048]{3,2,1,0:T(8,128)(2,1)} %get-tuple-element.43) | copy-start | bytes 12582916
  213.9 5.1 %copy-start.16 = (bf16[4,2,128,2048]{3,2,1,0:T(8,128)(2,1)S(1)}, bf16[4,2,128,2048]{3,2,1,0:T(8,128)(2,1)}, u32[]{:S(2)}) copy-start(bf16[4,2,128,2048]{3,2,1,0:T(8,128)(2,1)} %get-tuple-element.46) | copy-start | bytes 12582916
  213.9 5.1 %copy-start.24 = (bf16[4,128,2048]{2,1,0:T(8,128)(2,1)S(1)}, bf16[4,128,2048]{2,1,0:T(8,128)(2,1)}, u32[]{:S(2)}) copy-start(bf16[4,128,2048]{2,1,0:T(8,128)(2,1)} %get-tuple-element.45) | copy-start | bytes 6291460
  219.1 4.3 %copy-start.15 = (f32[4,2,1024]{2,1,0:T(2,128)S(1)}, f32[4,2,1024]{2,1,0:T(2,128)}, u32[]{:S(2)}) copy-start(f32[4,2,1024]{2,1,0:T(2,128)} %get-tuple-element.49) | copy-start | bytes 98308
  219.1 4.4 %copy-start.8 = (bf16[4,2,128,1024]{3,2,1,0:T(8,128)(2,1)S(1)}, bf16[4,2,128,1024]{3,2,1,0:T(8,128)(2,1)}, u32[]{:S(2)}) copy-start(bf16[4,2,128,1024]{3,2,1,0:T(8,128)(2,1)} %get-tuple-element.51) | copy-start | bytes 6291460
  223.4 1.6 copy-start.25
  225.0 5.7 %copy-start.23 = (bf16[4,128,2048]{2,1,0:T(8,128)(2,1)S(1)}, bf16[4,128,2048]{2,1,0:T(8,128)(2,1)}, u32[]{:S(2)}) copy-start(bf16[4,128,2048]{2,1,0:T(8,128)(2,1)} %get-tuple-element.42) | copy-start | bytes 6291460
  225.0 5.7 %copy-start.26 = (bf16[1024,512]{1,0:T(8,128)(2,1)S(1)}, bf16[1024,512]{1,0:T(8,128)(2,1)}, u32[]{:S(2)}) copy-start(bf16[1024,512]{1,0:T(8,128)(2,1)} %get-tuple-element.48) | copy-start | bytes 3145732
  237.2 72.4 %copy-start.7 = (bf16[512,1024]{1,0:T(8,128)(2,1)S(1)}, bf16[512,1024]{1,0:T(8,128)(2,1)}, u32[]{:S(2)}) copy-start(bf16[512,1024]{1,0:T(8,128)(2,1)} %og.1) | copy-start | bytes 3145732
  309.6 3.8 %copy-start.14 = (bf16[128,256]{1,0:T(8,128)(2,1)S(1)}, bf16[128,256]{1,0:T(8,128)(2,1)}, u32[]{:S(2)}) copy-start(bf16[128,256]{1,0:T(8,128)(2,1)} %get-tuple-element.56) | copy-start | bytes 196612
  309.6 4.6 %copy-start.10 = (bf16[128,512]{1,0:T(8,128)(2,1)S(1)}, bf16[128,512]{1,0:T(8,128)(2,1)}, u32[]{:S(2)}) copy-start(bf16[128,512]{1,0:T(8,128)(2,1)} %get-tuple-element.52) | copy-start | bytes 393220
  309.6 5.3 %copy-start.9 = (bf16[128,512]{1,0:T(8,128)(2,1)S(1)}, bf16[128,512]{1,0:T(8,128)(2,1)}, u32[]{:S(2)}) copy-start(bf16[128,512]{1,0:T(8,128)(2,1)} %get-tuple-element.55) | copy-start | bytes 393220
  309.6 6.2 %copy-start.13 = (f32[32,512]{1,0:T(8,128)S(1)}, f32[32,512]{1,0:T(8,128)}, u32[]{:S(2)}) copy-start(f32[32,512]{1,0:T(8,128)} %get-tuple-element.53) | copy-start | bytes 196612
  309.6 6.8 %copy-start.12 = (f32[32,512]{1,0:T(8,128)S(1)}, f32[32,512]{1,0:T(8,128)}, u32[]{:S(2)}) copy-start(f32[32,512]{1,0:T(8,128)} %get-tuple-element.54) | copy-start | bytes 196612
  309.6 7.4 %copy-start.1 = (bf16[128,224]{0,1:T(8,128)(2,1)S(1)}, bf16[128,224]{0,1:T(8,128)(2,1)}, u32[]{:S(2)}) copy-start(bf16[128,224]{0,1:T(8,128)(2,1)} %param.17) | copy-start | bytes 172036

commit v3 on v2

--- a/solution.py
+++ b/solution.py
@@ -405,41 +405,169 @@
     )(ids, sq, gain, xs, og, sm, store, wq, wo, wc, wk, wv)
 
 
-def ring_kernel(
-    att, qag, cd, kp, vp,
-    att_all, qag_all, cd_all, ko, vo,
-    b_k, b_v, t_k, t_v, u_k, u_v, w_k, w_v, x_k, x_v, p_k, p_v,
-    s_y, r_y, s_d, r_d, s_c, r_c, s_1, r_1, s_2, r_2, s_3, r_3, s_loc,
+def dot_nn(a, b):
+    return jnp.dot(a, b, preferred_element_type=F32)
+
+
+def dot_nt(a, b):
+    return lax.dot_general(a, b, (((1,), (1,)), ((), ())), preferred_element_type=F32)
+
+
+def dot_tn(a, b):
+    return lax.dot_general(a, b, (((0,), (0,)), ((), ())), preferred_element_type=F32)
+
+
+class Halves:
+    def __init__(self, p, bufs, out, w, spots, sems):
+        self.p, self.out, self.w = p, out, w
+        self.b, self.ua, self.ub, self.wa, self.wb, self.va, self.vb, self.f = bufs
+        self.x, self.z, self.c, self.y, self.xp, self.zp, self.sib = spots
+        self.s, self.r = sems
+        self.one, self.two, self.swapped = [[], []], [[], []], None
+
+    def swap(self):
+        src = self.p.at[:, pl.ds(2 * (1 - self.c), 2)]
+        self.swapped = remote(src, self.b, self.s.at[0], self.r.at[0], self.sib)
+
+    def first(self):
+        self.swapped.wait_recv()
+        p, b, c = self.p, self.b, self.c
+
+        def fold(i, carry):
+            j, h, k = i // 4, (i // 2) % 2, i % 2
+            b[j, h, k] = (p[j, 2 * c + h, k].astype(F32) + b[j, h, k].astype(F32)).astype(BF16)
+            return carry
+
+        lax.fori_loop(0, 16, fold, 0)
+        for k in (2, 1, 3):
+            self.one[0].append(
+                remote(b.at[around(self.z, k), 0], self.ua.at[k - 1], self.s.at[k], self.r.at[k], self.zp[k - 1])
+            )
+            lanes = cols(around(self.x, k), self.w)
+            self.one[1].append(
+                remote(b.at[:, 1, :, :, lanes], self.ub.at[k - 1], self.s.at[3 + k], self.r.at[3 + k], self.xp[k - 1])
+            )
+
+    def second(self):
+        b, ua, ub, wa, wb = self.b, self.ua, self.ub, self.wa, self.wb
+        for copy in self.one[0]:
+            copy.wait_recv()
+        for i in range(2):
+            wa[i] = (
+                b[self.z, 0, i].astype(F32) + ua[0, i].astype(F32)
+                + ua[1, i].astype(F32) + ua[2, i].astype(F32)
+            ).astype(BF16)
+        for k in (2, 1, 3):
+            lanes = cols(around(self.x, k), self.w)
+            self.two[0].append(
+                remote(wa.at[:, :, lanes], self.va.at[k - 1], self.s.at[6 + k], self.r.at[6 + k], self.xp[k - 1])
+            )
+        for copy in self.one[1]:
+            copy.wait_recv()
+
+        def fold(i, carry):
+            j, k = i // 2, i % 2
+            wb[j, k] = (
+                b[j, 1, k, :, cols(self.x, self.w)].astype(F32) + ub[0, j, k].astype(F32)
+                + ub[1, j, k].astype(F32) + ub[2, j, k].astype(F32)
+            ).astype(BF16)
+            return carry
+
+        lax.fori_loop(0, 8, fold, 0)
+        for k in (2, 1, 3):
+            self.two[1].append(
+                remote(wb.at[around(self.z, k)], self.vb.at[k - 1], self.s.at[9 + k], self.r.at[9 + k], self.zp[k - 1])
+            )
+
+    def third(self):
+        x, y, z, f, va, vb = self.x, self.y, self.z, self.f, self.va, self.vb
+        for copy in self.two[0] + self.two[1]:
+            copy.wait_recv()
+        for i in range(2):
+            f[0, i] = (
+                self.wa[i, :, cols(x, self.w)].astype(F32) + va[0, i].astype(F32)
+                + va[1, i].astype(F32) + va[2, i].astype(F32)
+            ).astype(BF16)
+            f[1, i] = (
+                self.wb[z, i].astype(F32) + vb[0, i].astype(F32)
+                + vb[1, i].astype(F32) + vb[2, i].astype(F32)
+            ).astype(BF16)
+
+        @pl.when(x != y)
+        def _():
+            remote(f, self.out, self.s.at[13], self.r.at[13], at(y, z, self.c, x))
+
+        @pl.when(x == y)
+        def _():
+            pltpu.make_async_copy(f, self.out, self.r.at[13]).start()
+
+    def end(self):
+        pltpu.make_async_copy(self.f, self.out, self.r.at[13]).wait()
+        for copy in self.one[0] + self.one[1] + self.two[0] + self.two[1]:
+            copy.wait_send()
+
+        @pl.when(self.x != self.y)
+        def _():
+            pltpu.make_async_copy(self.f, self.out, self.s.at[13]).wait()
+
+
+def backward_kernel(
+    att, qag, kag, vag, enc, ein, egain, xs, og, gain, nt, ogt, sm, sq, gc, gq, go, gk, gv,
+    layer, hidden, qo, oo, co, ko, vo,
+    tile, et, att_all, qag_all, cd_all, rs_all, p1, p2, p3, line_up, erstd, emean, rsum, sgrad, slot,
+    b_k, b_v, u_k, u_v, w_k, w_v, x_k, x_v, f_k, f_v,
+    bq0, bq1, bq2, bq3, bq4, bq5, bq6, bq7,
+    bo0, bo1, bo2, bo3, bo4, bo5, bo6, bo7,
+    bc0, bc1, bc2, bc3, bc4, bc5, bc6, bc7,
+    s_y, r_y, s_d, r_d, s_c, r_c, s_1, r_1, s_2, r_2, s_3, r_3, s_h, r_h, s_tile,
 ):
     x, z, c, y = place()
     yp = [at(x, z, c, around(y, k)) for k in (1, 2, 3)]
     xp = [at(around(x, k), z, c, y) for k in (1, 2, 3)]
     zp = [at(x, around(z, k), c, y) for k in (1, 2, 3)]
     sib = at(x, z, 1 - c, y)
-    meet(yp + xp + zp + [sib])
-    swaps = [
-        remote(p.at[:, :, 1 - c], b, s_c.at[n], r_c.at[n], sib)
-        for n, (p, b) in enumerate(((kp, b_k), (vp, b_v)))
-    ]
-    keep = []
-    small, ring = [], []
-    for k in (1, 2, 3):
-        small.append(remote(cd, cd_all.at[y], s_d.at[k], r_d.at[k], yp[k - 1]))
+    meet(yp + xp + zp + [sib], at(y, z, c, x), x != y)
+    spots = (x, z, c, y, xp, zp, sib)
+    rq = Halves(p1, (bq0, bq1, bq2, bq3, bq4, bq5, bq6, bq7), qo, 512, spots, (s_h.at[0], r_h.at[0]))
+    ro = Halves(p2, (bo0, bo1, bo2, bo3, bo4, bo5, bo6, bo7), oo, 512, spots, (s_h.at[1], r_h.at[1]))
+    rc = Halves(p3, (bc0, bc1, bc2, bc3, bc4, bc5, bc6, bc7), co, 256, spots, (s_h.at[2], r_h.at[2]))
+
+    ring = []
     for n, (src, dst) in enumerate(((att, att_all), (qag, qag_all))):
-        local = pltpu.make_async_copy(src, dst.at[y], s_loc.at[n])
-        local.start()
-        keep.append(local)
-        ring.append(remote(src, dst.at[y], s_y.at[n, 0], r_y.at[n, 0], yp[0]))
-        ring.append(remote(src, dst.at[y], s_y.at[n, 1], r_y.at[n, 1], yp[2]))
-    cd_all[y] = cd[...]
+        for j, k in ((0, 1), (1, 3)):
+            ring.append(remote(src, dst.at[y], s_y.at[n, j], r_y.at[n, j], yp[k - 1]))
+    et[...] = enc[...].T
+
+    def product(left, right, p, width=256):
+        def step(i, carry):
+            lanes = cols(i, width)
+            r = right[..., lanes].reshape(left.shape[1], width)
+            p[..., lanes] = dot_nn(left[...], r).astype(BF16).reshape(4, 4, 2, 32, width)
+            return carry
+
+        lax.fori_loop(0, p.shape[-1] // width, step, 0)
+
+    swaps = []
+    for n, (act, p, b) in enumerate(((kag, p1, b_k), (vag, p2, b_v))):
+        product(et, act, p)
+        swaps.append(remote(p.at[:, :, 1 - c], b, s_c.at[n], r_c.at[n], sib))
+    att_all[y] = att[...]
+    qag_all[y] = qag[...]
+
+    passed = []
+
+    def relay(n, dst):
+        for j, k in ((0, 1), (1, 3)):
+            ring[2 * n + j].wait_recv()
+            block = dst.at[around(y, 4 - k), pl.ds(64 * j, 64)]
+            passed.append(remote(block, block, s_y.at[n, 2 + j], r_y.at[n, 2 + j], yp[k - 1]))
 
     sent = []
-    halves = ((kp, b_k, t_k, u_k), (vp, b_v, t_v, u_v))
-    for n, (p, b, t, u) in enumerate(halves):
+    for n, (p, b, u) in enumerate(((p1, b_k, u_k), (p2, b_v, u_v))):
         swaps[n].wait_recv()
 
-        def fold(i, carry, p=p, b=b, t=t):
-            t[i // 4, i % 4] = (
+        def fold(i, carry, p=p, b=b):
+            b[i // 4, i % 4] = (
                 p[i // 4, i % 4, c].astype(F32) + b[i // 4, i % 4].astype(F32)
             ).astype(BF16)
             return carry
@@ -447,30 +575,85 @@
         lax.fori_loop(0, 16, fold, 0)
         for k in (2, 1, 3):
             if n:
-                src, peer = t.at[around(x, k)], xp[k - 1]
+                src, peer = b.at[around(x, k)], xp[k - 1]
             else:
-                src, peer = t.at[:, around(z, k)], zp[k - 1]
-            sent.append(remote(src, u.at[k], s_1.at[n, k], r_1.at[n, k], peer))
-
-    passed = []
-    for n, dst in enumerate((att_all, qag_all)):
-        left, right = around(y, 3), around(y, 1)
-        ring[2 * n].wait_recv()
-        block = dst.at[left, pl.ds(0, 64)]
-        passed.append(remote(block, block, s_y.at[n, 2], r_y.at[n, 2], yp[0]))
-        ring[2 * n + 1].wait_recv()
-        block = dst.at[right, pl.ds(64, 64)]
-        passed.append(remote(block, block, s_y.at[n, 3], r_y.at[n, 3], yp[2]))
+                src, peer = b.at[:, around(z, k)], zp[k - 1]
+            sent.append(remote(src, u.at[k - 1], s_1.at[n, k], r_1.at[n, k], peer))
+    for copy in swaps:
+        copy.wait_send()
+    relay(0, att_all)
+
+    def fetch(h, i, j):
+        return pltpu.make_async_copy(h.at[i], tile.at[j], s_tile.at[j])
+
+    ee = ein[...]
+    erstd[...] = lax.rsqrt(jnp.sum(ee * ee, axis=-1, keepdims=True) / DE + EPS)
+    emean[...] = jnp.zeros_like(emean)
+    fetch(gk, 0, 0).start()
+    fetch(gv, 0, 1).start()
+
+    def encoder(i, carry):
+        lanes = cols(i, 256)
+        fetch(gk, i, 0).wait()
+        part = dot_nt(kag[...], tile[0])
+
+        @pl.when(i < 3)
+        def _():
+            fetch(gk, i + 1, 0).start()
+
+        fetch(gv, i, 1).wait()
+        part = part + dot_nt(vag[...], tile[1])
+
+        @pl.when(i < 3)
+        def _():
+            fetch(gv, i + 1, 1).start()
+
+        ey = part.astype(BF16).astype(F32) * egain[:, lanes]
+        emean[...] += jnp.sum(ein[:, lanes] * ey, axis=-1, keepdims=True)
+        ry = ey * erstd[...]
+        for s in range(2):
+            slot[s : s + 1, lanes] = jnp.sum(ry[256 * s : 256 * s + 256], axis=0, keepdims=True)
+        return carry
+
+    lax.fori_loop(0, 4, encoder, 0)
+    relay(1, qag_all)
+    for s in range(2):
+        rows = slice(256 * s, 256 * s + 256)
+        weight = erstd[rows] ** 3 * (emean[rows] / DE)
+        row = slot[s : s + 1] - jnp.sum(ein[rows] * weight, axis=0, keepdims=True)
+        slot[s : s + 1] = row.astype(BF16).astype(F32)
+    cd_all[y] = slot[...]
+    small = [remote(slot, cd_all.at[y], s_d.at[0, k], r_d.at[0, k], yp[k - 1]) for k in (1, 2, 3)]
+
+    for copy in passed[:2]:
+        copy.wait_recv()
+    product(ogt, att_all, p2)
+    ro.swap()
+
+    def streamed(h, act, use):
+        fetch(h, 0, 0).start()
+
+        def step(i, carry):
+            fetch(h, i, i % 2).wait()
+
+            @pl.when(i < 3)
+            def _():
+                fetch(h, i + 1, (i + 1) % 2).start()
+
+            use(cols(i, 256), dot_nt(act[...].reshape(512, 2048), tile[i % 2]))
+            return carry
+
+        lax.fori_loop(0, 4, step, 0)
 
     sent2 = []
-    for n, (t, u, w, v) in enumerate(((t_k, u_k, w_k, x_k), (t_v, u_v, w_v, x_v))):
+    for n, (b, u, w, v) in enumerate(((b_k, u_k, w_k, x_k), (b_v, u_v, w_v, x_v))):
         for copy in sent[3 * n : 3 * n + 3]:
             copy.wait_recv()
 
-        def fold(i, carry, t=t, u=u, w=w, n=n):
-            own = t[x, i] if n else t[i, z]
+        def fold(i, carry, b=b, u=u, w=w, n=n):
+            own = b[x, i] if n else b[i, z]
             w[i] = (
-                own.astype(F32) + u[1, i].astype(F32) + u[2, i].astype(F32) + u[3, i].astype(F32)
+                own.astype(F32) + u[0, i].astype(F32) + u[1, i].astype(F32) + u[2, i].astype(F32)
             ).astype(BF16)
             return carry
 
@@ -480,213 +663,165 @@
                 src, peer = w.at[around(z, k)], zp[k - 1]
             else:
                 src, peer = w.at[around(x, k)], xp[k - 1]
-            sent2.append(remote(src, v.at[k], s_2.at[n, k], r_2.at[n, k], peer))
+            sent2.append(remote(src, v.at[k - 1], s_2.at[n, k], r_2.at[n, k], peer))
+    ro.first()
+    for copy in passed[2:]:
+        copy.wait_recv()
+    product(nt, qag_all, p1)
+    rq.swap()
+
+    def add_out(lanes, value):
+        layer[:, lanes] = (xs[:, lanes].astype(F32) + value).astype(BF16)
+
+    streamed(go, att_all, add_out)
+    rq.first()
     sent3 = []
-    ends = ((w_k, x_k, p_k), (w_v, x_v, p_v))
-    for n, (w, v, p) in enumerate(ends):
+    for n, (w, v, f) in enumerate(((w_k, x_k, f_k), (w_v, x_v, f_v))):
         for copy in sent2[3 * n : 3 * n + 3]:
             copy.wait_recv()
         own = w[z] if n else w[x]
-        p[0] = (
-            own.astype(F32) + v[1].astype(F32) + v[2].astype(F32) + v[3].astype(F32)
+        f[0] = (
+            own.astype(F32) + v[0].astype(F32) + v[1].astype(F32) + v[2].astype(F32)
         ).astype(BF16)
         for k in (2, 1, 3):
-            sent3.append(
-                remote(
-                    p.at[0, :, cols(around(y, k), 512)],
-                    p.at[k, :, pl.ds(0, 512)],
-                    s_3.at[n, k],
-                    r_3.at[n, k],
-                    yp[k - 1],
-                )
-            )
-    for n, (out, p) in enumerate(((ko, p_k), (vo, p_v))):
+            src, dst = f.at[0, :, cols(around(y, k), 512)], f.at[k, :, pl.ds(0, 512)]
+            sent3.append(remote(src, dst, s_3.at[n, k], r_3.at[n, k], yp[k - 1]))
+    for copy in small:
+        copy.wait_recv()
+    cd = cd_all[...].reshape(8, 1024).astype(BF16)
+    for i in range(4):
+        lanes = slice(256 * i, 256 * i + 256)
+        p3[..., lanes] = dot_tn(sm[...], cd[:, lanes]).astype(BF16).reshape(4, 4, 2, 32, 256)
+    rc.swap()
+    for i in range(4):
+        sgrad[:, 256 * i : 256 * i + 256] = dot_nt(cd, gc[i].reshape(256, 1024)) / SPAN
+    rsum[...] = jnp.zeros_like(rsum)
+
+    def add_scaled(lanes, value):
+        scaled = value * gain[:, lanes]
+        hidden[:, lanes] = scaled
+        rsum[...] += jnp.sum(xs[:, lanes].astype(F32) * scaled, axis=-1, keepdims=True)
+
+    streamed(gq, qag_all, add_scaled)
+    line_up[...] = jnp.zeros_like(line_up)
+    for j in range(4):
+        line_up[:, j : j + 1] = rsum[128 * j : 128 * j + 128]
+    rs_all[4] = line_up[...].T[:8]
+    for k in (1, 2, 3):
+        small.append(
+            remote(rs_all.at[4], rs_all.at[y], s_d.at[1, k], r_d.at[1, k], yp[k - 1])
+        )
+    rs_all[y] = rs_all[4]
+    rc.first()
+    ro.second()
+    for n, (out, f) in enumerate(((ko, f_k), (vo, f_v))):
         for copy in sent3[3 * n : 3 * n + 3]:
             copy.wait_recv()
         out[...] = (
-            p[0, :, cols(y, 512)].astype(F32)
-            + p[1, :, pl.ds(0, 512)].astype(F32)
-            + p[2, :, pl.ds(0, 512)].astype(F32)
-            + p[3, :, pl.ds(0, 512)].astype(F32)
+            f[0, :, cols(y, 512)].astype(F32)
+            + f[1, :, pl.ds(0, 512)].astype(F32)
+            + f[2, :, pl.ds(0, 512)].astype(F32)
+            + f[3, :, pl.ds(0, 512)].astype(F32)
         )
-    for copy in keep:
-        copy.wait()
-    for copy in small + passed:
-        copy.wait_recv()
-    for copy in swaps + small + ring + sent + passed + sent2 + sent3:
+    rq.second()
+    ro.third()
+    rc.second()
+    for copy in small[3:]:
+        copy.wait_recv()
+    total = rs_all[0] + rs_all[1] + rs_all[2] + rs_all[3]
+    mean = (total / 4096).T
+    rstd = lax.rsqrt((sq[0] + sq[1] + sq[2] + sq[3]) / 4096 + EPS).T
+    for s in range(8):
+        rows, half, j = slice(64 * s, 64 * s + 64), slice(64 * (s % 2), 64 * (s % 2) + 64), s // 2
+        r, m = rstd[half, j : j + 1], mean[half, j : j + 1]
+        hidden[rows] = (
+            og[rows].astype(F32)
+            + (r * hidden[rows] - xs[rows].astype(F32) * (r * r * r * m))
+            + sgrad[s : s + 1]
+        )
+    rq.third()
+    rc.third()
+    for r in (ro, rq, rc):
+        r.swapped.wait_send()
+        r.end()
+    for copy in small + ring + sent + passed + sent2 + sent3:
         copy.wait_send()
 
 
-def ring_gather(att, qag, cd, kp, vp):
+def halves_scratch(w):
+    return [
+        pltpu.VMEM((4, 2, 2, 32, 4 * w), BF16),
+        pltpu.VMEM((3, 2, 32, 4 * w), BF16),
+        pltpu.VMEM((3, 4, 2, 32, w), BF16),
+        pltpu.VMEM((2, 32, 4 * w), BF16),
+        pltpu.VMEM((4, 2, 32, w), BF16),
+        pltpu.VMEM((3, 2, 32, w), BF16),
+        pltpu.VMEM((3, 2, 32, w), BF16),
+        pltpu.VMEM((2, 2, 32, w), BF16),
+    ]
+
+
+def backward(*operands):
+    shape = jax.ShapeDtypeStruct
+    rows = (4, 4, 2, 32)
     return pl.pallas_call(
-        ring_kernel,
+        backward_kernel,
         out_shape=(
-            jax.ShapeDtypeStruct((4, 128, 2048), BF16),
-            jax.ShapeDtypeStruct((4, 128, 2048), BF16),
-            jax.ShapeDtypeStruct((4, 2, 1024), F32),
-            jax.ShapeDtypeStruct((32, 512), F32),
-            jax.ShapeDtypeStruct((32, 512), F32),
+            shape((512, 1024), BF16),
+            shape((512, 1024), F32),
+            shape((2, 2, 32, 512), BF16),
+            shape((2, 2, 32, 512), BF16),
+            shape((2, 2, 32, 256), BF16),
+            shape((32, 512), F32),
+            shape((32, 512), F32),
         ),
-        in_specs=[VM] * 5,
-        out_specs=(VM,) * 5,
-        scratch_shapes=[pltpu.VMEM((4, 4, 32, 2048), BF16)] * 4
-        + [pltpu.VMEM((4, 4, 32, 2048), BF16)] * 2
-        + [pltpu.VMEM((4, 32, 2048), BF16)] * 6
+        in_specs=[VM] * 15 + [ANY] * 4,
+        out_specs=(VM,) * 7,
+        scratch_shapes=[
+            pltpu.VMEM((2, 256, 2048), BF16),
+            pltpu.VMEM((1024, 512), BF16),
+            pltpu.VMEM((4, 128, 2048), BF16),
+            pltpu.VMEM((4, 128, 2048), BF16),
+            pltpu.VMEM((4, 2, 1024), F32),
+            pltpu.VMEM((5, 8, 128), F32),
+            pltpu.VMEM(rows + (2048,), BF16),
+            pltpu.VMEM(rows + (2048,), BF16),
+            pltpu.VMEM(rows + (1024,), BF16),
+            pltpu.VMEM((128, 128), F32),
+            pltpu.VMEM((512, 1), F32),
+            pltpu.VMEM((512, 1), F32),
+            pltpu.VMEM((512, 1), F32),
+            pltpu.VMEM((8, 1024), F32),
+            pltpu.VMEM((2, 1024), F32),
+            pltpu.VMEM((4, 4, 32, 2048), BF16),
+            pltpu.VMEM((4, 4, 32, 2048), BF16),
+            pltpu.VMEM((3, 4, 32, 2048), BF16),
+            pltpu.VMEM((3, 4, 32, 2048), BF16),
+            pltpu.VMEM((4, 32, 2048), BF16),
+            pltpu.VMEM((4, 32, 2048), BF16),
+            pltpu.VMEM((3, 32, 2048), BF16),
+            pltpu.VMEM((3, 32, 2048), BF16),
+            pltpu.VMEM((4, 32, 2048), BF16),
+            pltpu.VMEM((4, 32, 2048), BF16),
+        ]
+        + halves_scratch(512)
+        + halves_scratch(512)
+        + halves_scratch(256)
         + [
             DMA((2, 4)), DMA((2, 4)),
-            DMA((4,)), DMA((4,)),
+            DMA((2, 4)), DMA((2, 4)),
             DMA((2,)), DMA((2,)),
             DMA((2, 4)), DMA((2, 4)),
             DMA((2, 4)), DMA((2, 4)),
             DMA((2, 4)), DMA((2, 4)),
+            DMA((3, 14)), DMA((3, 14)),
             DMA((2,)),
         ],
         compiler_params=pltpu.CompilerParams(
-            collective_id=2, has_side_effects=True, vmem_limit_bytes=56 << 20
+            collective_id=1, has_side_effects=True, vmem_limit_bytes=60 << 20
         ),
-        name="ring_gather",
-    )(att, qag, cd, kp, vp)
-
-
-def reduce_kernel(
-    qp, op, cp, rs,
-    qo, oo, co, rs_all,
-    b_q, b_o, b_c, u_q, u_o, u_c, w_q, w_o, w_c, v_q, v_o, v_c, f_q, f_o, f_c,
-    s_d, r_d, s_c, r_c, s_1, r_1, s_2, r_2, s_t, r_t,
-):
-    x, z, c, y = place()
-    yp = [at(x, z, c, around(y, k)) for k in (1, 2, 3)]
-    xp = [at(around(x, k), z, c, y) for k in (1, 2, 3)]
-    zp = [at(x, around(z, k), c, y) for k in (1, 2, 3)]
-    sib = at(x, z, 1 - c, y)
-    partner = at(y, z, c, x)
-    meet(yp + xp + zp + [sib], partner, x != y)
-    parts = (qp, op, cp)
-    swaps = [
-        remote(p.at[:, 1 - c], b, s_c.at[n], r_c.at[n], sib)
-        for n, (p, b) in enumerate(zip(parts, (b_q, b_o, b_c)))
-    ]
-    small = [
-        remote(rs, rs_all.at[y], s_d.at[k], r_d.at[k], yp[k - 1]) for k in (1, 2, 3)
-    ]
-    rs_all[y] = rs[...]
-    widths = (512, 512, 256)
-    sent = []
-    for n, (p, b, u, wd) in enumerate(zip(parts, (b_q, b_o, b_c), (u_q, u_o, u_c), widths)):
-        swaps[n].wait_recv()
-
-        def fold(i, carry, p=p, b=b):
-            r = pl.ds(pl.multiple_of((i % 8) * 16, 16), 16)
-            b[i // 8, r] = (p[i // 8, c, r].astype(F32) + b[i // 8, r].astype(F32)).astype(BF16)
-            return carry
-
-        lax.fori_loop(0, 32, fold, 0)
-        for k in (2, 1, 3):
-            if n == 1:
-                src, peer = b.at[:, :, cols(around(x, k), wd)], xp[k - 1]
-            else:
-                src, peer = b.at[around(z, k)], zp[k - 1]
-            sent.append(remote(src, u.at[k], s_1.at[n, k], r_1.at[n, k], peer))
-    sent2 = []
-    for n, (b, u, w, v, wd) in enumerate(
-        zip((b_q, b_o, b_c), (u_q, u_o, u_c), (w_q, w_o, w_c), (v_q, v_o, v_c), widths)
-    ):
-        for copy in sent[3 * n : 3 * n + 3]:
-            copy.wait_recv()
-
-        if n == 1:
-
-            def fold(i, carry, b=b, u=u, w=w, wd=wd):
-                r = pl.ds(pl.multiple_of((i % 8) * 16, 16), 16)
-                w[i // 8, r] = (
-                    b[i // 8, r, cols(x, wd)].astype(F32)
-                    + u[1, i // 8, r].astype(F32)
-                    + u[2, i // 8, r].astype(F32)
-                    + u[3, i // 8, r].astype(F32)
-                ).astype(BF16)
-                return carry
-
-            lax.fori_loop(0, 32, fold, 0)
-        else:
-            sum_rows(w, [b.at[z], u.at[1], u.at[2], u.at[3]])
-        for k in (2, 1, 3):
-            if n == 1:
-                src, peer = w.at[around(z, k)], zp[k - 1]
-            else:
-                src, peer = w.at[:, cols(around(x, k), wd)], xp[k - 1]
-            sent2.append(remote(src, v.at[k], s_2.at[n, k], r_2.at[n, k], peer))
-    lasts = tuple(zip((w_q, w_o, w_c), (v_q, v_o, v_c), (f_q, f_o, f_c), (qo, oo, co), widths))
-    for n, (w, v, f, out, wd) in enumerate(lasts):
-        for copy in sent2[3 * n : 3 * n + 3]:
-            copy.wait_recv()
-        own = w.at[z] if n == 1 else w.at[:, cols(x, wd)]
-        sum_rows(f, [own, v.at[1], v.at[2], v.at[3]])
-
-        @pl.when(x != y)
-        def _(f=f, out=out, n=n):
-            remote(f, out, s_t.at[n], r_t.at[n], partner)
-
-        @pl.when(x == y)
-        def _(f=f, out=out, n=n):
-            pltpu.make_async_copy(f, out, r_t.at[n]).start()
-
-    for n, (w, v, f, out, wd) in enumerate(lasts):
-        pltpu.make_async_copy(f, out, r_t.at[n]).wait()
-    for copy in small:
-        copy.wait_recv()
-    for copy in swaps + small + sent + sent2:
-        copy.wait_send()
-
-    @pl.when(x != y)
-    def _():
-        for n, (w, v, f, out, wd) in enumerate(lasts):
-            pltpu.make_async_copy(f, out, s_t.at[n]).wait()
-
-
-def reduce_weights(qp, op, cp, rs):
-    wide, slim = (4, 128, 2048), (4, 128, 1024)
-    return pl.pallas_call(
-        reduce_kernel,
-        out_shape=(
-            jax.ShapeDtypeStruct((128, 512), BF16),
-            jax.ShapeDtypeStruct((128, 512), BF16),
-            jax.ShapeDtypeStruct((128, 256), BF16),
-            jax.ShapeDtypeStruct((4, 8, 128), F32),
-        ),
-        in_specs=[VM] * 4,
-        out_specs=(VM,) * 4,
-        scratch_shapes=[
-            pltpu.VMEM(wide, BF16), pltpu.VMEM(wide, BF16), pltpu.VMEM(slim, BF16),
-            pltpu.VMEM(wide, BF16), pltpu.VMEM((4, 4, 128, 512), BF16), pltpu.VMEM(slim, BF16),
-            pltpu.VMEM((128, 2048), BF16), pltpu.VMEM((4, 128, 512), BF16),
-            pltpu.VMEM((128, 1024), BF16),
-            pltpu.VMEM((4, 128, 512), BF16), pltpu.VMEM((4, 128, 512), BF16),
-            pltpu.VMEM((4, 128, 256), BF16),
-            pltpu.VMEM((128, 512), BF16), pltpu.VMEM((128, 512), BF16),
-            pltpu.VMEM((128, 256), BF16),
-            DMA((4,)), DMA((4,)),
-            DMA((3,)), DMA((3,)),
-            DMA((3, 4)), DMA((3, 4)),
-            DMA((3, 4)), DMA((3, 4)),
-            DMA((3,)), DMA((3,)),
-        ],
-        compiler_params=pltpu.CompilerParams(
-            collective_id=3, has_side_effects=True, vmem_limit_bytes=56 << 20
-        ),
-        name="reduce_weights",
-    )(qp, op, cp, rs)
-
-
-def dot_nn(a, b):
-    return jnp.dot(a, b, preferred_element_type=F32)
-
-
-def dot_nt(a, b):
-    return lax.dot_general(a, b, (((1,), (1,)), ((), ())), preferred_element_type=F32)
-
-
-def dot_tn(a, b):
-    return lax.dot_general(a, b, (((0,), (0,)), ((), ())), preferred_element_type=F32)
+        name="backward",
+    )(*operands)
 
 
 def attention_kernel(q_ref, g_ref, k_ref, v_ref, att_ref, qag_ref, kag_ref, vag_ref):
@@ -754,9 +889,7 @@
         ids, sq, gain.reshape(1, 1024), hidden, out_grad, summary, store,
         w_query, w_out.T, wc, wk, wv,
     )
-    gq, go, gc = gq.reshape(1024, 2048), go.reshape(1024, 2048), gc.reshape(1024, 1024)
     gk, gv = gk.reshape(PE, 2048), gv.reshape(PE, 2048)
-    rstd = lax.rsqrt(jnp.sum(sq_all, axis=0)[:4].reshape(512, 1) / 4096 + EPS)
 
     egain = jnp.pad(enc_gain.reshape(32, 28), ((0, 0), (0, 4))).reshape(PE)
     rawp = dot_nn(raw.reshape(512, DE), wide_columns(32))
@@ -767,42 +900,20 @@
     keys = dot_nn(encoded, gk).astype(BF16)
     values = dot_nn(encoded, gv).astype(BF16)
     att, qag, kag, vag = attention(q, ag, keys, values)
-    kp = dot_tn(encoded, kag).astype(BF16).reshape(4, 4, 2, 32, 2048)
-    vp = dot_tn(encoded, vag).astype(BF16).reshape(4, 4, 2, 32, 2048)
-    eg = (dot_nt(kag, gk) + dot_nt(vag, gv)).astype(BF16).astype(F32)
-    ey = egain * eg
-    emean = jnp.sum(enc_in * ey, axis=-1, keepdims=True) / DE
-    slot = jnp.sum(
-        (enc_rstd * ey - enc_in * enc_rstd**3 * emean).reshape(2, 256, PE), axis=1
-    )
-    cd = slot.astype(BF16).astype(F32)
-    att_all, qag_all, cd_all, kg, vg = ring_gather(att, qag, cd, kp, vp)
-    att_all, qag_all = att_all.reshape(512, 2048), qag_all.reshape(512, 2048)
-    cd_all = cd_all.reshape(8, PE).astype(BF16)
-
-    layer_out = (xf + dot_nt(att_all, go)).astype(BF16)
-    op = dot_nn(out_grad_t, att_all).astype(BF16).reshape(4, 2, 128, 2048)
-    gp = dot_nn(normed_t, qag_all).astype(BF16).reshape(4, 2, 128, 2048)
-    hp = dot_tn(summary, cd_all).astype(BF16).reshape(4, 2, 128, 1024)
-    scaled = dot_nt(qag_all, gq) * gain
-    rs = lines(jnp.sum(xf * scaled, axis=-1))
-    summary_grad = dot_nt(cd_all, gc)
-    qo, oo, co, rs_all = reduce_weights(gp, op, hp, rs)
-
-    row_mean = jnp.sum(rs_all, axis=0)[:4].reshape(512, 1) / 4096
-    hidden_grad = (
-        out_grad.astype(F32)
-        + (rstd * scaled - xf * rstd**3 * row_mean)
-        + jnp.repeat(summary_grad / SPAN, SPAN, axis=0)
+    layer_out, hidden_grad, qo, oo, co, kg, vg = backward(
+        att, qag, kag, vag, encoded, enc_in, egain.reshape(1, PE), hidden, out_grad,
+        gain.reshape(1, 1024), normed_t, out_grad_t, summary, sq_all, gc,
+        gq.reshape(4, 256, 2048), go.reshape(4, 256, 2048),
+        gk.reshape(4, 256, 2048), gv.reshape(4, 256, 2048),
     )
     cond_grad = co.astype(F32).reshape(128, 8, 32)[:, :, :28].reshape(128, 224)
     return (
         layer_out,
         hidden_grad,
-        qo.astype(F32),
+        qo.reshape(128, 512).astype(F32),
         kg[:28],
         vg[:28],
-        oo.T.astype(F32),
+        oo.reshape(128, 512).T.astype(F32),
         cond_grad,
     )
 

time: 318 us -> 262 us (0.82)
  matrix products: 49.4 us -> 13.6 us
  Pallas kernels: 248 us -> 231 us
    dot_general x8 -> x0, matrix products: 28.4 us -> none  [the longest x5 17.5 us: dot_nt(): lax.dot_general(a, b, (((1,), (1,)), ((), ())), preferred_element_type=F32)]
    pallas_call x2 -> x1, Pallas kernels: 124 us -> 107 us  [backward(): pl.pallas_call(backward_kernel, out_shape=(shape((512, 1024), BF16), shap...]
    dot_general x6 -> x4, matrix products: 21 us -> 13.6 us  [dot_nn(): return jnp.dot(a, b, preferred_element_type=F32)]
    add x1 -> x0, other arithmetic: 3.74 us -> none  [shards(): out_grad.astype(F32) + (rstd * scaled - xf * rstd ** 3 * row_mean)]
where the time goes in v3:
time: 262 us
  Pallas kernels  231 us (88%)
  matrix products  13.6 us (5%)
  local copies, waits for them, and re-layouts  8.8 us (3%)
  other arithmetic  7.3 us (3%)
    pallas_call x1, Pallas kernels, backward(): pl.pallas_call(backward_kernel, out_shape=(shape((512, 1024), BF16), shap...  107 us
    pallas_call x1, Pallas kernels, forward(): pl.pallas_call(forward_kernel, out_shape=(shape((4, NL, DE), BF16), shape...  105 us
    pallas_call x1, Pallas kernels, attention(): pl.pallas_call(attention_kernel, grid=(8,), out_shape=(jax.ShapeDtypeStru...  19.4 us
    dot_general x4, matrix products, dot_nn(): return jnp.dot(a, b, preferred_element_type=F32)  13.6 us

profile of v3, /device:TPU:7, one launch (start us, length us, event | category | flops | bytes accessed | tf_op | source)
XLA Modules:
  0.0 261.6 jit_solution(3010492149720443213)
XLA Ops:
  0.6 0.0 copy-start
  0.6 0.0 copy-start.4
  0.7 0.0 copy-start.11
  0.7 0.0 copy-start.14
  0.7 0.0 copy-start.15
  0.7 0.7 pad.19.ids
  1.4 1.5 multiply_reduce_fusion.1
  2.9 0.7 dynamic_slice.3
  3.6 0.0 copy-start.5
  3.6 1.4 bitcast_reduce_fusion
  5.1 0.0 copy-done.11
  5.1 0.0 copy-start.3
  5.1 0.1 copy.26
  5.3 0.0 copy-done
  5.3 0.4 fusion.19.wc
  5.7 0.0 copy-done.14
  5.8 0.0 copy-done.15
  5.8 0.0 copy-done.4
  5.8 104.9 %forward.1 = (bf16[4,128,896]{2,1,0:T(8,128)(2,1)}, f32[4,8,128]{2,1,0:T(8,128)S(1)}, bf16[128,2048]{1,0:T(8,128)(2,1)S(1)}, bf16[128,2048]{1,0:T(8,128)(2,1)S(1...) custom-call(s32[8,128]{1,0:T(8,128)S(1)} %pad.19.ids, ...), custom_call_target="tpu_custom_call" | custom-call | tf_op jit(solution)/shard_map/forward/pallas_call | solution.py:354
  110.7 0.0 copy-done.5
  110.7 0.0 copy-done.3
  110.7 0.0 copy-start.1
  110.7 0.0 copy-start.2
  110.7 0.0 copy-start.6
  110.8 0.0 copy-start.16
  110.9 3.2 %multiply_reduce_fusion = (f32[2,256]{1,0:T(2,128)S(1)}, f32[2,256,1024]{2,1,0:T(8,128)S(1)}) fusion(f32[2,1024]{1,0:T(2,128)S(1)} %convert_convert_fusion, bf16[2,256,896]{2,1,0:T(8,128)(2,1)} %bitcast.67, s32[1024]{0:T(1024)S(1)} %get-tuple-element.70, s32[1024]{0:T(1024)S(1)} %get-tuple-element.75, s32[896]{0:T(1024)S(1)} %get-tuple-element.72, ...), kind=kOutput, calls=%fused_computation.10 | convolution fusion | flops 947518976 | bytes 3059456 | tf_op jit(solution)/shard_map/dot_general | solution.py:409
  114.1 0.0 copy-done.1
  114.1 0.0 copy-done.2
  114.1 0.0 copy-done.6
  114.1 0.0 copy-start.7
  114.1 0.0 copy-done.16
  114.1 0.1 reshape.110
  114.3 0.1 mul.45
  114.3 0.2 multiply_convert_fusion.1
  114.6 0.0 copy-start.8
  114.6 6.2 %convolution_convert_fusion.1.k_ref = bf16[512,2048]{1,0:T(8,128)(2,1)} fusion(bf16[512,1024]{1,0:T(8,128)(2,1)S(1)} %bitcast.59, bf16[1024,2048]{1,0:T(8,128)(2,1)} %bitcast.54), kind=kOutput, calls=%fused_computation.6 | convolution fusion | flops 2148532224 | bytes 7340032 | tf_op jit(solution)/shard_map/dot_general | solution.py:409
  120.8 0.0 copy-done.8
  120.8 3.8 %convolution_convert_fusion.v_ref = bf16[512,2048]{1,0:T(8,128)(2,1)} fusion(bf16[512,1024]{1,0:T(8,128)(2,1)S(1)} %bitcast.60, bf16[1024,2048]{1,0:T(8,128)(2,1)S(1)} %bitcast.57), kind=kOutput, calls=%fused_computation.5 | convolution fusion | flops 2148532224 | bytes 7340032 | tf_op jit(solution)/shard_map/dot_general | solution.py:409
  124.5 19.4 %attention.1 = (bf16[128,2048]{1,0:T(8,128)(2,1)}, bf16[128,2048]{1,0:T(8,128)(2,1)}, bf16[512,2048]{1,0:T(8,128)(2,1)}, bf16[512,2048]{1,0:T(8,128)(2,1)}) custom-call(bf16[128,2048]{1,0:T(8,128)(2,1)} %copy-done.1, bf16[128,2048]{1,0:T(8,128)(2,1)} %copy-done.2, bf16[512,2048]{1,0:T(8,128)(2,1)} %convolution_convert_fusion.1.k_ref, ...), custom_call_target="tpu_custom_call" | custom-call | tf_op jit(solution)/shard_map/attention/pallas_call | solution.py:850
  144.0 0.0 copy-done.7
  144.0 1.2 multiply_convert_fusion.enc
  145.2 0.7 broadcast_in_dim_reshape.3.egain
  145.9 106.6 %backward.1 = (bf16[512,1024]{1,0:T(8,128)(2,1)}, f32[512,1024]{1,0:T(8,128)}, bf16[2,2,32,512]{3,2,1,0:T(8,128)(2,1)}, bf16[2,2,32,512]{3,2,1,0:T(8,128)(2,1)},...) custom-call(bf16[128,2048]{1,0:T(8,128)(2,1)} %get-tuple-element.36.att, ...), custom_call_target="tpu_custom_call" | custom-call | tf_op jit(solution)/shard_map/backward/pallas_call | solution.py:767
  252.5 0.0 copy-start.10
  252.5 1.7 bitcast_convert_fusion.1
  254.2 0.0 copy-start.9
  254.2 1.1 bitcast_convert_fusion
  255.3 0.8 copy.28
  256.1 1.0 reshape.116
  257.2 0.2 copy.32
  257.4 0.7 reshape.121
  258.1 0.0 copy-done.10
  258.1 1.0 copy.38
  259.1 0.0 copy-done.9
  259.1 0.0 copy-start.13
  259.1 0.0 copy-start.12
  259.1 1.3 copy.39
  260.4 0.0 copy-done.13
  260.4 0.6 copy.40
  261.0 0.0 copy-done.12
  261.0 0.6 copy.41
  (21 shorter events, 0.2 us)
Async XLA Ops:
  0.6 4.7 %copy-start = (bf16[128,224]{0,1:T(8,128)(2,1)S(1)}, bf16[128,224]{0,1:T(8,128)(2,1)}, u32[]{:S(2)}) copy-start(bf16[128,224]{0,1:T(8,128)(2,1)} %param.17) | copy-start | bytes 172036
  0.6 5.1 %copy-start.4 = (bf16[128,512]{1,0:T(8,128)(2,1)S(1)}, bf16[128,512]{1,0:T(8,128)(2,1)}, u32[]{:S(2)}) copy-start(bf16[128,512]{1,0:T(8,128)(2,1)} %wq.1) | copy-start | bytes 393220
  0.7 4.4 %copy-start.11 = (bf16[512,128]{1,0:T(8,128)(2,1)S(1)}, bf16[512,128]{1,0:T(8,128)(2,1)}, u32[]{:S(2)}) copy-start(bf16[512,128]{1,0:T(8,128)(2,1)} %param.16) | copy-start | bytes 393220
  0.7 5.1 %copy-start.14 = (bf16[28,512]{1,0:T(8,128)(2,1)S(1)}, bf16[28,512]{1,0:T(8,128)(2,1)}, u32[]{:S(2)}) copy-start(bf16[28,512]{1,0:T(8,128)(2,1)} %param.14) | copy-start | bytes 86020
  0.7 5.1 %copy-start.15 = (bf16[28,512]{1,0:T(8,128)(2,1)S(1)}, bf16[28,512]{1,0:T(8,128)(2,1)}, u32[]{:S(2)}) copy-start(bf16[28,512]{1,0:T(8,128)(2,1)} %param.15) | copy-start | bytes 86020
  3.6 107.1 %copy-start.5 = (f32[1024]{0:T(1024)}, f32[1024]{0:T(1024)S(1)}, u32[]{:S(2)}) copy-start(f32[1024]{0:T(1024)S(1)} %dynamic_slice.3) | copy-start | bytes 12292
  5.1 105.6 %copy-start.3 = (bf16[8,1024]{1,0:T(8,128)(2,1)}, bf16[8,1024]{1,0:T(8,128)(2,1)S(1)}, u32[]{:S(2)}) copy-start(bf16[8,1024]{1,0:T(8,128)(2,1)S(1)} %multiply_convert_fusion.2.sm) | copy-start | bytes 49156
  110.7 3.4 %copy-start.1 = (bf16[128,2048]{1,0:T(8,128)(2,1)}, bf16[128,2048]{1,0:T(8,128)(2,1)S(1)}, u32[]{:S(2)}) copy-start(bf16[128,2048]{1,0:T(8,128)(2,1)S(1)} %get-tuple-element.30.q_ref) | copy-start | bytes 1572868
  110.7 3.4 %copy-start.2 = (bf16[128,2048]{1,0:T(8,128)(2,1)}, bf16[128,2048]{1,0:T(8,128)(2,1)S(1)}, u32[]{:S(2)}) copy-start(bf16[128,2048]{1,0:T(8,128)(2,1)S(1)} %get-tuple-element.31.g_ref) | copy-start | bytes 1572868
  110.7 3.4 %copy-start.6 = (f32[4,8,128]{2,1,0:T(8,128)}, f32[4,8,128]{2,1,0:T(8,128)S(1)}, u32[]{:S(2)}) copy-start(f32[4,8,128]{2,1,0:T(8,128)S(1)} %get-tuple-element.42.sq) | copy-start | bytes 49156
  110.8 3.3 %copy-start.16 = (f32[896]{0:T(1024)S(1)}, f32[896]{0:T(1024)}, u32[]{:S(2)}) copy-start(f32[896]{0:T(1024)} %param.18) | copy-start | bytes 10756
  114.1 29.9 %copy-start.7 = (f32[2,256,1024]{2,1,0:T(8,128)}, f32[2,256,1024]{2,1,0:T(8,128)S(1)}, u32[]{:S(2)}) copy-start(f32[2,256,1024]{2,1,0:T(8,128)S(1)} %get-tuple-element.56) | copy-start | bytes 6291460
  114.6 6.2 %copy-start.8 = (bf16[4,4,2,32,2048]{4,3,2,1,0:T(8,128)(2,1)S(1)}, bf16[4,4,2,32,2048]{4,3,2,1,0:T(8,128)(2,1)}, u32[]{:S(2)}) copy-start(bf16[4,4,2,32,2048]{4,3,2,1,0:T(8,128)(2,1)} %get-tuple-element.35) | copy-start | bytes 12582916
  252.5 5.6 %copy-start.10 = (bf16[512,1024]{1,0:T(8,128)(2,1)S(1)}, bf16[512,1024]{1,0:T(8,128)(2,1)}, u32[]{:S(2)}) copy-start(bf16[512,1024]{1,0:T(8,128)(2,1)} %get-tuple-element.88) | copy-start | bytes 3145732
  254.2 4.8 %copy-start.9 = (f32[512,1024]{1,0:T(8,128)S(1)}, f32[512,1024]{1,0:T(8,128)}, u32[]{:S(2)}) copy-start(f32[512,1024]{1,0:T(8,128)} %get-tuple-element.89) | copy-start | bytes 6291460
  259.1 1.3 copy-start.13
  259.1 2.0 copy-start.12

commit v4 on v3

--- a/solution.py
+++ b/solution.py
@@ -139,12 +139,65 @@
             copy.wait_send()
 
 
+class Sums:
+    def __init__(self, p, bufs, y, right, left, sems):
+        self.p, self.y, self.right, self.left = p, y, right, left
+        self.far_a, self.far_b, self.from_left, self.from_right = bufs
+        self.s, self.r = sems
+        self.far, self.near, self.late = [], [], []
+
+    def send(self, n, src, dst, peer):
+        return remote(src, dst, self.s.at[n], self.r.at[n], peer)
+
+    def first(self):
+        p, y = self.p, self.y
+        a, b = pl.ds(0, 64), pl.ds(64, 64)
+        self.far = [
+            self.send(0, p.at[around(y, 2), a], self.far_a, self.right),
+            self.send(1, p.at[around(y, 2), b], self.far_b, self.left),
+        ]
+        self.near = [
+            self.send(2, p.at[around(y, 1), b], self.from_left.at[b], self.right),
+            self.send(3, p.at[around(y, 3), a], self.from_right.at[a], self.left),
+        ]
+
+    def second(self):
+        p, y = self.p, self.y
+        moves = (
+            (0, self.far_a, around(y, 1), 0, self.from_left, self.right),
+            (1, self.far_b, around(y, 3), 64, self.from_right, self.left),
+        )
+        for n, far, target, low, dst, peer in moves:
+            self.far[n].wait_recv()
+
+            def fold(i, carry, far=far, target=target, low=low):
+                rows = pl.ds(pl.multiple_of(low + i * 16, 16), 16)
+                more = far[pl.ds(pl.multiple_of(i * 16, 16), 16)].astype(F32)
+                p[target, rows] = (p[target, rows].astype(F32) + more).astype(BF16)
+                return carry
+
+            lax.fori_loop(0, 4, fold, 0)
+            half = pl.ds(low, 64)
+            self.late.append(self.send(4 + n, p.at[target, half], dst.at[half], peer))
+
+    def third(self, out):
+        for copy in self.near + self.late:
+            copy.wait_recv()
+        sum_rows(out, [self.p.at[self.y], self.from_left, self.from_right])
+
+    def sent(self):
+        for copy in self.far + self.near + self.late:
+            copy.wait_send()
+
+
 def forward_kernel(
-    ids, sq, gain, xs, og, sm, store, wq, wo, wc, wk, wv,
-    raw, sq_all, q, a, cond, nt, ogt, hq, ho, hc, gk, gv,
-    ids_all, ids_s, out_rows, in_rows, tq, to, tc, yk, yv, gq, go, gc,
-    normed, qp, ap, cp, rq, ra, rc,
-    s_small, r_small, s_row, r_row, s_t, r_t, s_p, r_p, s_w, r_w, s_y, r_y, s_loc, s_out,
+    ids_in, gain, xs, og, egain, store, wq, wo_in, wc_in, wk_in, wv_in,
+    sq_all, sm, q, a, keys, values, enc, ein, nt, ogt, hq, ho, hc, hk, hv,
+    ids_all, ids_s, out_rows, in_rows, tq, to, tc, yk, yv, gq, go, gc, gk, gv,
+    normed, qp, ap, cp, q0, q1, q2, q3, a0, a1, a2, a3, rc,
+    ids, sq, line_up, means, pick_cols, wo, wc, wk, wv,
+    s_small, r_small, s_row, r_row, s_t, r_t, s_p, r_p, s_w, r_w, s_y, r_y, s_q, r_q, s_a, r_a,
+    s_loc, s_out,
 ):
     x, z, c, y = place()
     yp = [at(x, z, c, around(y, k)) for k in (1, 2, 3)]
@@ -157,30 +210,50 @@
 
     moves = ((wq, tq), (wo, to), (wc, tc))
 
-    @pl.when(x != y)
-    def _():
-        for n, (w, t) in enumerate(moves):
+    def cross(n):
+        w, t = moves[n]
+
+        @pl.when(x != y)
+        def _():
             remote(w, t, s_t.at[n], r_t.at[n], partner)
 
-    @pl.when(x == y)
-    def _():
-        for n, (w, t) in enumerate(moves):
+        @pl.when(x == y)
+        def _():
             pltpu.make_async_copy(w, t, r_t.at[n]).start()
 
+    def arrived(n):
+        w, t = moves[n]
+        pltpu.make_async_copy(w, t, r_t.at[n]).wait()
+
+    cross(0)
+    ids[...] = jnp.zeros_like(ids)
+    ids[0:1, 0:4] = ids_in[...]
     small = []
     for k in (1, 2, 3):
         small.append(remote(ids, ids_all.at[y], s_small.at[0, k], r_small.at[0, k], yp[k - 1]))
+    ids_all[y] = ids[...]
+    line_up[...] = jnp.zeros_like(line_up)
+    for j in range(4):
+        part = xs[128 * j : 128 * (j + 1)].astype(F32)
+        line_up[:, j : j + 1] = jnp.sum(part * part, axis=-1, keepdims=True)
+        for i in range(2):
+            row = jnp.sum(part[64 * i : 64 * i + 64], axis=0, keepdims=True) / SPAN
+            means[2 * j + i : 2 * j + i + 1] = row
+    sm[...] = means[...].astype(BF16)
+    sq[...] = line_up[...].T[:8]
+    sq_all[y] = sq[...]
     for k in (1, 2, 3):
         small.append(remote(sq, sq_all.at[y], s_small.at[1, k], r_small.at[1, k], yp[k - 1]))
-    across = []
-    for n, (w, t) in enumerate(((wk, yk), (wv, yv))):
-        for k in (2, 1, 3):
-            across.append(
-                remote(w, t.at[:, cols(y, 512)], s_w.at[n, k], r_w.at[n, k], yp[k - 1])
-            )
-        t[:, cols(y, 512)] = w[...]
-    ids_all[y] = ids[...]
-    sq_all[y] = sq[...]
+    wo[...] = wo_in[...].T
+    spot = lax.broadcasted_iota(jnp.int32, (1, PE), 1)
+    source = jnp.where(spot % 32 < 28, spot // 32 * 28 + spot % 32, -1)
+    for i in range(7):
+        row = lax.broadcasted_iota(jnp.int32, (128, PE), 0) + 128 * i
+        pick_cols[128 * i : 128 * (i + 1)] = jnp.where(row == source, 1.0, 0.0).astype(BF16)
+    wc[...] = dot_nn(wc_in[...], pick_cols[0:224, 0:256]).astype(BF16)
+    for w, v in ((wk, wk_in), (wv, wv_in)):
+        w[...] = jnp.zeros_like(w)
+        w[0:28] = v[...]
     for copy in small[:3]:
         copy.wait_recv()
     to_s = pltpu.make_async_copy(ids_all, ids_s, s_loc.at[0])
@@ -233,15 +306,25 @@
             return gv.at[i, pl.ds(2 * j, 2), c]
         return gk.at[pl.ds(2 * j, 2), i, c]
 
-    def arrived(n, w, t):
-        pltpu.make_async_copy(w, t, r_t.at[n]).wait()
-
-    arrived(0, wq, tq)
+    pk = KeyPlane(
+        kv_put, kv_line, kv_cut, (gk.at[:, :, c], gv.at[:, :, c]), axes, (s_p.at[3], r_p.at[3])
+    )
+    rq = Sums(qp, (q0, q1, q2, q3), y, yp[0], yp[2], (s_q, r_q))
+    ra = Sums(ap, (a0, a1, a2, a3), y, yp[0], yp[2], (s_a, r_a))
+
+    arrived(0)
+    cross(2)
+    cross(1)
     pq.first()
-    arrived(1, wo, to)
-    po.first()
+    across = []
+    for n, (w, t) in enumerate(((wk, yk), (wv, yv))):
+        for k in (2, 1, 3):
+            across.append(
+                remote(w, t.at[:, cols(y, 512)], s_w.at[n, k], r_w.at[n, k], yp[k - 1])
+            )
+        t[:, cols(y, 512)] = w[...]
     pq.second()
-    arrived(2, wc, tc)
+    arrived(2)
     pc.first()
     for copy in small[3:]:
         copy.wait_recv()
@@ -249,82 +332,101 @@
     rstd = lax.rsqrt(total / 4096 + EPS).T
     for j in range(4):
         rows = slice(128 * j, 128 * (j + 1))
-        normed[rows] = (xs[rows].astype(F32) * rstd[:, j : j + 1] * gain[...]).astype(BF16)
+        normed[rows] = (xs[rows].astype(F32) * rstd[:, j : j + 1] * gain[:, cols(y, 1024)]).astype(BF16)
+    arrived(1)
+    po.first()
+    pq.relay()
+    pc.second()
     po.second()
-    pq.relay()
+    pq.swap()
+    pc.relay()
+    outs = []
+
+    def keep(n, g, h):
+        copy = pltpu.make_async_copy(g, h, s_out.at[n])
+        copy.start()
+        outs.append(copy)
+
+    def product(act, g, put):
+        def tile(i, carry):
+            lanes = cols(i, 256)
+            put(lanes, dot_nn(act[...], g[..., lanes].reshape(1024, 256)).astype(BF16))
+            return carry
+
+        lax.fori_loop(0, 8, tile, 0)
+
+    def into(p):
+        def put(lanes, value):
+            p[:, :, lanes] = value.reshape(4, 128, 256)
+
+        return put
+
+    pq.last.wait_recv()
+    product(normed, gq, into(qp))
+    rq.first()
+    keep(0, gq, hq)
+    pc.swap()
+    po.relay()
     for copy in across:
         copy.wait_recv()
-    pk = KeyPlane(kv_put, kv_line, kv_cut, (gk.at[:, :, c], gv.at[:, :, c]), axes, (s_p.at[3], r_p.at[3]))
     pk.first()
-    pc.second()
-    pq.swap()
-    po.relay()
-
-    parts, outs = [], []
-
-    def partial(n, act, g, h, p, r, plane):
-        plane.last.wait_recv()
-        keep = pltpu.make_async_copy(g, h, s_out.at[n])
-        keep.start()
-        outs.append(keep)
-
-        def tile(i, carry):
-            lanes = cols(i, 256)
-            w = g[:, :, :, lanes].reshape(1024, 256)
-            p[:, :, lanes] = dot_nn(act[...], w).astype(BF16).reshape(4, 128, 256)
-            return carry
-
-        lax.fori_loop(0, 8, tile, 0)
-        for k in (2, 1, 3):
-            parts.append(
-                remote(p.at[around(y, k)], r.at[k], s_y.at[n, k], r_y.at[n, k], yp[k - 1])
-            )
-
-    partial(0, normed, gq, hq, qp, rq, pq)
-    pk.second()
-    po.swap()
-    pc.relay()
-    partial(1, og, go, ho, ap, ra, po)
-    pk.relay()
-    pc.swap()
-    for j in range(4):
-        rows = slice(128 * j, 128 * (j + 1))
-        nt[:, rows] = normed[rows].T
-        ogt[:, rows] = og[rows].T
     pc.last.wait_recv()
-    keep = pltpu.make_async_copy(gc, hc, s_out.at[2])
-    keep.start()
-    outs.append(keep)
+    keep(2, gc, hc)
     for i in range(4):
         lanes = slice(256 * i, 256 * (i + 1))
         w = gc[:, :, :, lanes].reshape(1024, 256)
         cp[:, lanes] = dot_nn(sm[...], w)
     for j in range(4):
         rc[j + 4] = cp[2 * j : 2 * j + 2]
+    parts = []
     for k in (2, 1, 3):
         parts.append(
-            remote(rc.at[4 + around(y, k)], rc.at[k], s_y.at[2, k], r_y.at[2, k], yp[k - 1])
+            remote(rc.at[4 + around(y, k)], rc.at[k], s_y.at[k], r_y.at[k], yp[k - 1])
         )
+    rq.second()
+    po.swap()
+    pk.second()
+    po.last.wait_recv()
+    product(og, go, into(ap))
+    ra.first()
+    keep(1, go, ho)
     for copy in row_copies:
         copy.wait_recv()
     owner, row, rank = pick_rows(ids_s, y)
     for k in range(4):
-        raw[k] = in_rows[owner[k], jnp.minimum(rank[k], 1)]
+        rows = slice(128 * k, 128 * (k + 1))
+        ein[rows] = dot_nn(in_rows[owner[k], jnp.minimum(rank[k], 1)], pick_cols[...])
+    pk.relay()
+    for copy in parts:
+        copy.wait_recv()
+    cond = (rc[4 + y] + rc[1] + rc[2] + rc[3]).astype(BF16).astype(F32)
+    for k in range(4):
+        rows = slice(128 * k, 128 * (k + 1))
+        row = ein[rows] + cond[k // 2 : k // 2 + 1]
+        ein[rows] = row
+        scale = lax.rsqrt(jnp.sum(row * row, axis=-1, keepdims=True) / DE + EPS)
+        enc[rows] = (row * scale * egain[...]).astype(BF16)
+    ra.second()
     pk.swap()
-    for copy in parts[:3]:
-        copy.wait_recv()
-    sum_rows(q, [qp.at[y], rq.at[1], rq.at[2], rq.at[3]])
-    for copy in parts[3:]:
-        copy.wait_recv()
-    sum_rows(a, [ap.at[y], ra.at[1], ra.at[2], ra.at[3]])
-    cond[...] = rc[4 + y] + rc[1] + rc[2] + rc[3]
-    for copy in pk.last:
-        copy.wait_recv()
+    for j in range(4):
+        rows = slice(128 * j, 128 * (j + 1))
+        nt[:, rows] = normed[rows].T
+        ogt[:, rows] = og[rows].T
+    rq.third(q)
+    for n, (g, h, out) in enumerate(((gk, hk, keys), (gv, hv, values))):
+        pk.last[n].wait_recv()
+        keep(3 + n, g, h)
+
+        def put(lanes, value, out=out):
+            out[:, lanes] = value
+
+        product(enc, g, put)
+    ra.third(a)
     for copy in outs:
         copy.wait()
     for copy in small + across + row_copies + parts:
         copy.wait_send()
-    for plane in (pq, po, pc, pk):
+    for plane in (pq, po, pc, pk, rq, ra):
         plane.sent()
 
     @pl.when(x != y)
@@ -348,17 +450,26 @@
             copy.wait_send()
 
 
-def forward(ids, sq, gain, xs, og, sm, store, wq, wo, wc, wk, wv):
+def forward(*operands):
     wide, slim, keys = (4, 2, 128, 2048), (4, 2, 128, 1024), (4, 4, 2, 32, 2048)
     shape = jax.ShapeDtypeStruct
+    halves = [
+        pltpu.VMEM((64, 2048), BF16),
+        pltpu.VMEM((64, 2048), BF16),
+        pltpu.VMEM((128, 2048), BF16),
+        pltpu.VMEM((128, 2048), BF16),
+    ]
     return pl.pallas_call(
         forward_kernel,
         out_shape=(
-            shape((4, NL, DE), BF16),
             shape((4, 8, 128), F32),
+            shape((8, 1024), BF16),
             shape((128, 2048), BF16),
             shape((128, 2048), BF16),
-            shape((2, 1024), F32),
+            shape((512, 2048), BF16),
+            shape((512, 2048), BF16),
+            shape((512, PE), BF16),
+            shape((512, PE), F32),
             shape((1024, 512), BF16),
             shape((1024, 512), BF16),
             shape(wide, BF16),
@@ -367,8 +478,8 @@
             shape(keys, BF16),
             shape(keys, BF16),
         ),
-        in_specs=[VM] * 12,
-        out_specs=(VM,) * 7 + (ANY,) * 5,
+        in_specs=[VM] * 11,
+        out_specs=(VM,) * 10 + (ANY,) * 5,
         scratch_shapes=[
             pltpu.VMEM((4, 8, 128), jnp.int32),
             pltpu.SMEM((4, 8, 128), jnp.int32),
@@ -382,27 +493,42 @@
             pltpu.VMEM(wide, BF16),
             pltpu.VMEM(wide, BF16),
             pltpu.VMEM(slim, BF16),
+            pltpu.VMEM(keys, BF16),
+            pltpu.VMEM(keys, BF16),
             pltpu.VMEM((512, 1024), BF16),
             pltpu.VMEM((4, 128, 2048), BF16),
             pltpu.VMEM((4, 128, 2048), BF16),
             pltpu.VMEM((8, 1024), F32),
-            pltpu.VMEM((4, 128, 2048), BF16),
-            pltpu.VMEM((4, 128, 2048), BF16),
+        ]
+        + halves
+        + halves
+        + [
             pltpu.VMEM((8, 2, 1024), F32),
+            pltpu.VMEM((8, 128), jnp.int32),
+            pltpu.VMEM((8, 128), F32),
+            pltpu.VMEM((128, 128), F32),
+            pltpu.VMEM((8, 1024), F32),
+            pltpu.VMEM((DE, PE), BF16),
+            pltpu.VMEM((128, 512), BF16),
+            pltpu.VMEM((128, 256), BF16),
+            pltpu.VMEM((32, 512), BF16),
+            pltpu.VMEM((32, 512), BF16),
             DMA((2, 4)), DMA((2, 4)),
             DMA((4,)), DMA((4,)),
             DMA((3,)), DMA((3,)),
             DMA((4, 2, 11)), DMA((4, 2, 11)),
             DMA((2, 4)), DMA((2, 4)),
-            DMA((3, 4)), DMA((3, 4)),
+            DMA((4,)), DMA((4,)),
+            DMA((6,)), DMA((6,)),
+            DMA((6,)), DMA((6,)),
             DMA((1,)),
-            DMA((3,)),
+            DMA((5,)),
         ],
         compiler_params=pltpu.CompilerParams(
-            collective_id=0, has_side_effects=True, vmem_limit_bytes=52 << 20
+            collective_id=0, has_side_effects=True, vmem_limit_bytes=58 << 20
         ),
         name="forward",
-    )(ids, sq, gain, xs, og, sm, store, wq, wo, wc, wk, wv)
+    )(*operands)
 
 
 def dot_nn(a, b):
@@ -415,15 +541,62 @@
 
 def dot_tn(a, b):
     return lax.dot_general(a, b, (((0,), (0,)), ((), ())), preferred_element_type=F32)
+
+
+class Around:
+    def __init__(self, half, bufs, place, right, left, sems, base):
+        self.half, self.place, self.right, self.left = half, place, right, left
+        self.far, self.from_left, self.from_right = bufs
+        self.s, self.r, self.base = sems[0], sems[1], base
+        self.sends = []
+
+    def send(self, n, src, dst, peer):
+        n = self.base + n
+        self.sends.append(remote(src, dst, self.s.at[n], self.r.at[n], peer))
+
+    def first(self):
+        half, p = self.half, self.place
+        self.send(0, half(around(p, 2), 0), self.far.at[0], self.right)
+        self.send(1, half(around(p, 2), 1), self.far.at[1], self.left)
+        self.send(2, half(around(p, 1), 1), self.from_left.at[1], self.right)
+        self.send(3, half(around(p, 3), 0), self.from_right.at[0], self.left)
+
+    def mid(self):
+        moves = ((0, 1, self.from_left, self.right), (1, 3, self.from_right, self.left))
+        for n, k, dst, peer in moves:
+            self.sends[n].wait_recv()
+            own = self.half(around(self.place, k), n)
+            own[...] = (own[...].astype(F32) + self.far[n].astype(F32)).astype(BF16)
+            self.send(4 + n, own, dst.at[n], peer)
+
+    def here(self):
+        for copy in self.sends[2:]:
+            copy.wait_recv()
+
+    def total(self, i):
+        own = self.half(self.place, i)[...].astype(F32)
+        return (own + self.from_left[i].astype(F32) + self.from_right[i].astype(F32)).astype(BF16)
+
+    def sent(self):
+        for copy in self.sends:
+            copy.wait_send()
 
 
 class Halves:
     def __init__(self, p, bufs, out, w, spots, sems):
         self.p, self.out, self.w = p, out, w
-        self.b, self.ua, self.ub, self.wa, self.wb, self.va, self.vb, self.f = bufs
+        self.b, fa, la, ra, fb, lb, rb, self.wa, self.wb, self.va, self.vb, self.f = bufs
         self.x, self.z, self.c, self.y, self.xp, self.zp, self.sib = spots
         self.s, self.r = sems
-        self.one, self.two, self.swapped = [[], []], [[], []], None
+        self.two, self.swapped = [[], []], None
+        b = self.b
+        self.ringa = Around(
+            lambda t, i: b.at[t, 0, i], (fa, la, ra), self.z, self.zp[0], self.zp[2], sems, 14
+        )
+        self.ringb = Around(
+            lambda t, i: b.at[:, 1, i, :, cols(t, w)], (fb, lb, rb), self.x, self.xp[0],
+            self.xp[2], sems, 20,
+        )
 
     def swap(self):
         src = self.p.at[:, pl.ds(2 * (1 - self.c), 2)]
@@ -439,41 +612,26 @@
             return carry
 
         lax.fori_loop(0, 16, fold, 0)
-        for k in (2, 1, 3):
-            self.one[0].append(
-                remote(b.at[around(self.z, k), 0], self.ua.at[k - 1], self.s.at[k], self.r.at[k], self.zp[k - 1])
-            )
-            lanes = cols(around(self.x, k), self.w)
-            self.one[1].append(
-                remote(b.at[:, 1, :, :, lanes], self.ub.at[k - 1], self.s.at[3 + k], self.r.at[3 + k], self.xp[k - 1])
-            )
+        self.ringa.first()
+        self.ringb.first()
+
+    def mid(self):
+        self.ringa.mid()
+        self.ringb.mid()
 
     def second(self):
-        b, ua, ub, wa, wb = self.b, self.ua, self.ub, self.wa, self.wb
-        for copy in self.one[0]:
-            copy.wait_recv()
+        wa, wb = self.wa, self.wb
+        self.ringa.here()
         for i in range(2):
-            wa[i] = (
-                b[self.z, 0, i].astype(F32) + ua[0, i].astype(F32)
-                + ua[1, i].astype(F32) + ua[2, i].astype(F32)
-            ).astype(BF16)
+            wa[i] = self.ringa.total(i)
         for k in (2, 1, 3):
             lanes = cols(around(self.x, k), self.w)
             self.two[0].append(
                 remote(wa.at[:, :, lanes], self.va.at[k - 1], self.s.at[6 + k], self.r.at[6 + k], self.xp[k - 1])
             )
-        for copy in self.one[1]:
-            copy.wait_recv()
-
-        def fold(i, carry):
-            j, k = i // 2, i % 2
-            wb[j, k] = (
-                b[j, 1, k, :, cols(self.x, self.w)].astype(F32) + ub[0, j, k].astype(F32)
-                + ub[1, j, k].astype(F32) + ub[2, j, k].astype(F32)
-            ).astype(BF16)
-            return carry
-
-        lax.fori_loop(0, 8, fold, 0)
+        self.ringb.here()
+        for i in range(2):
+            wb[:, i] = self.ringb.total(i)
         for k in (2, 1, 3):
             self.two[1].append(
                 remote(wb.at[around(self.z, k)], self.vb.at[k - 1], self.s.at[9 + k], self.r.at[9 + k], self.zp[k - 1])
@@ -503,8 +661,10 @@
 
     def end(self):
         pltpu.make_async_copy(self.f, self.out, self.r.at[13]).wait()
-        for copy in self.one[0] + self.one[1] + self.two[0] + self.two[1]:
+        for copy in self.two[0] + self.two[1]:
             copy.wait_send()
+        self.ringa.sent()
+        self.ringb.sent()
 
         @pl.when(self.x != self.y)
         def _():
@@ -515,12 +675,11 @@
     att, qag, kag, vag, enc, ein, egain, xs, og, gain, nt, ogt, sm, sq, gc, gq, go, gk, gv,
     layer, hidden, qo, oo, co, ko, vo,
     tile, et, att_all, qag_all, cd_all, rs_all, p1, p2, p3, line_up, erstd, emean, rsum, sgrad, slot,
-    b_k, b_v, u_k, u_v, w_k, w_v, x_k, x_v, f_k, f_v,
-    bq0, bq1, bq2, bq3, bq4, bq5, bq6, bq7,
-    bo0, bo1, bo2, bo3, bo4, bo5, bo6, bo7,
-    bc0, bc1, bc2, bc3, bc4, bc5, bc6, bc7,
-    s_y, r_y, s_d, r_d, s_c, r_c, s_1, r_1, s_2, r_2, s_3, r_3, s_h, r_h, s_tile,
+    *scratch,
 ):
+    b_k, b_v, ak, lk, rk, av, lv, rv, w_k, w_v, x_k, x_v, f_k, f_v = scratch[:14]
+    bq, bo, bc = scratch[14:26], scratch[26:38], scratch[38:50]
+    s_y, r_y, s_d, r_d, s_c, r_c, s_1, r_1, s_2, r_2, s_3, r_3, s_h, r_h, s_tile = scratch[50:]
     x, z, c, y = place()
     yp = [at(x, z, c, around(y, k)) for k in (1, 2, 3)]
     xp = [at(around(x, k), z, c, y) for k in (1, 2, 3)]
@@ -528,9 +687,9 @@
     sib = at(x, z, 1 - c, y)
     meet(yp + xp + zp + [sib], at(y, z, c, x), x != y)
     spots = (x, z, c, y, xp, zp, sib)
-    rq = Halves(p1, (bq0, bq1, bq2, bq3, bq4, bq5, bq6, bq7), qo, 512, spots, (s_h.at[0], r_h.at[0]))
-    ro = Halves(p2, (bo0, bo1, bo2, bo3, bo4, bo5, bo6, bo7), oo, 512, spots, (s_h.at[1], r_h.at[1]))
-    rc = Halves(p3, (bc0, bc1, bc2, bc3, bc4, bc5, bc6, bc7), co, 256, spots, (s_h.at[2], r_h.at[2]))
+    rq = Halves(p1, bq, qo, 512, spots, (s_h.at[0], r_h.at[0]))
+    ro = Halves(p2, bo, oo, 512, spots, (s_h.at[1], r_h.at[1]))
+    rc = Halves(p3, bc, co, 256, spots, (s_h.at[2], r_h.at[2]))
 
     ring = []
     for n, (src, dst) in enumerate(((att, att_all), (qag, qag_all))):
@@ -562,8 +721,17 @@
             block = dst.at[around(y, 4 - k), pl.ds(64 * j, 64)]
             passed.append(remote(block, block, s_y.at[n, 2 + j], r_y.at[n, 2 + j], yp[k - 1]))
 
-    sent = []
-    for n, (p, b, u) in enumerate(((p1, b_k, u_k), (p2, b_v, u_v))):
+    def pair(i):
+        return pl.ds(2 * i, 2)
+
+    kring = Around(
+        lambda t, i: b_k.at[pair(i), t], (ak, lk, rk), z, zp[0], zp[2], (s_1, r_1), 0
+    )
+    vring = Around(
+        lambda t, i: b_v.at[t, pair(i)], (av, lv, rv), x, xp[0], xp[2], (s_1, r_1), 6
+    )
+    rings = (kring, vring)
+    for n, (p, b) in enumerate(((p1, b_k), (p2, b_v))):
         swaps[n].wait_recv()
 
         def fold(i, carry, p=p, b=b):
@@ -573,12 +741,7 @@
             return carry
 
         lax.fori_loop(0, 16, fold, 0)
-        for k in (2, 1, 3):
-            if n:
-                src, peer = b.at[around(x, k)], xp[k - 1]
-            else:
-                src, peer = b.at[:, around(z, k)], zp[k - 1]
-            sent.append(remote(src, u.at[k - 1], s_1.at[n, k], r_1.at[n, k], peer))
+        rings[n].first()
     for copy in swaps:
         copy.wait_send()
     relay(0, att_all)
@@ -591,6 +754,8 @@
     emean[...] = jnp.zeros_like(emean)
     fetch(gk, 0, 0).start()
     fetch(gv, 0, 1).start()
+    kring.mid()
+    vring.mid()
 
     def encoder(i, carry):
         lanes = cols(i, 256)
@@ -646,35 +811,29 @@
         lax.fori_loop(0, 4, step, 0)
 
     sent2 = []
-    for n, (b, u, w, v) in enumerate(((b_k, u_k, w_k, x_k), (b_v, u_v, w_v, x_v))):
-        for copy in sent[3 * n : 3 * n + 3]:
-            copy.wait_recv()
-
-        def fold(i, carry, b=b, u=u, w=w, n=n):
-            own = b[x, i] if n else b[i, z]
-            w[i] = (
-                own.astype(F32) + u[0, i].astype(F32) + u[1, i].astype(F32) + u[2, i].astype(F32)
-            ).astype(BF16)
-            return carry
-
-        lax.fori_loop(0, 4, fold, 0)
+    ro.first()
+    for n, (w, v) in enumerate(((w_k, x_k), (w_v, x_v))):
+        rings[n].here()
+        for i in range(2):
+            w[pair(i)] = rings[n].total(i)
         for k in (2, 1, 3):
             if n:
                 src, peer = w.at[around(z, k)], zp[k - 1]
             else:
                 src, peer = w.at[around(x, k)], xp[k - 1]
             sent2.append(remote(src, v.at[k - 1], s_2.at[n, k], r_2.at[n, k], peer))
-    ro.first()
     for copy in passed[2:]:
         copy.wait_recv()
     product(nt, qag_all, p1)
     rq.swap()
+    ro.mid()
 
     def add_out(lanes, value):
         layer[:, lanes] = (xs[:, lanes].astype(F32) + value).astype(BF16)
 
     streamed(go, att_all, add_out)
     rq.first()
+    ro.second()
     sent3 = []
     for n, (w, v, f) in enumerate(((w_k, x_k, f_k), (w_v, x_v, f_v))):
         for copy in sent2[3 * n : 3 * n + 3]:
@@ -693,12 +852,13 @@
         lanes = slice(256 * i, 256 * i + 256)
         p3[..., lanes] = dot_tn(sm[...], cd[:, lanes]).astype(BF16).reshape(4, 4, 2, 32, 256)
     rc.swap()
+    rq.mid()
     for i in range(4):
         sgrad[:, 256 * i : 256 * i + 256] = dot_nt(cd, gc[i].reshape(256, 1024)) / SPAN
     rsum[...] = jnp.zeros_like(rsum)
 
     def add_scaled(lanes, value):
-        scaled = value * gain[:, lanes]
+        scaled = value * gain[:, pl.ds(pl.multiple_of(y * 1024 + lanes.start, 256), 256)]
         hidden[:, lanes] = scaled
         rsum[...] += jnp.sum(xs[:, lanes].astype(F32) * scaled, axis=-1, keepdims=True)
 
@@ -713,7 +873,9 @@
         )
     rs_all[y] = rs_all[4]
     rc.first()
-    ro.second()
+    ro.third()
+    rq.second()
+    rc.mid()
     for n, (out, f) in enumerate(((ko, f_k), (vo, f_v))):
         for copy in sent3[3 * n : 3 * n + 3]:
             copy.wait_recv()
@@ -723,9 +885,8 @@
             + f[2, :, pl.ds(0, 512)].astype(F32)
             + f[3, :, pl.ds(0, 512)].astype(F32)
         )
-    rq.second()
-    ro.third()
     rc.second()
+    rq.third()
     for copy in small[3:]:
         copy.wait_recv()
     total = rs_all[0] + rs_all[1] + rs_all[2] + rs_all[3]
@@ -739,20 +900,21 @@
             + (r * hidden[rows] - xs[rows].astype(F32) * (r * r * r * m))
             + sgrad[s : s + 1]
         )
-    rq.third()
     rc.third()
     for r in (ro, rq, rc):
         r.swapped.wait_send()
         r.end()
-    for copy in small + ring + sent + passed + sent2 + sent3:
+    for r in rings:
+        r.sent()
+    for copy in small + ring + passed + sent2 + sent3:
         copy.wait_send()
 
 
 def halves_scratch(w):
     return [
         pltpu.VMEM((4, 2, 2, 32, 4 * w), BF16),
-        pltpu.VMEM((3, 2, 32, 4 * w), BF16),
-        pltpu.VMEM((3, 4, 2, 32, w), BF16),
+        *[pltpu.VMEM((2, 32, 4 * w), BF16)] * 3,
+        *[pltpu.VMEM((2, 4, 32, w), BF16)] * 3,
         pltpu.VMEM((2, 32, 4 * w), BF16),
         pltpu.VMEM((4, 2, 32, w), BF16),
         pltpu.VMEM((3, 2, 32, w), BF16),
@@ -795,8 +957,7 @@
             pltpu.VMEM((2, 1024), F32),
             pltpu.VMEM((4, 4, 32, 2048), BF16),
             pltpu.VMEM((4, 4, 32, 2048), BF16),
-            pltpu.VMEM((3, 4, 32, 2048), BF16),
-            pltpu.VMEM((3, 4, 32, 2048), BF16),
+            *[pltpu.VMEM((2, 2, 32, 2048), BF16)] * 6,
             pltpu.VMEM((4, 32, 2048), BF16),
             pltpu.VMEM((4, 32, 2048), BF16),
             pltpu.VMEM((3, 32, 2048), BF16),
@@ -811,10 +972,10 @@
             DMA((2, 4)), DMA((2, 4)),
             DMA((2, 4)), DMA((2, 4)),
             DMA((2,)), DMA((2,)),
+            DMA((12,)), DMA((12,)),
             DMA((2, 4)), DMA((2, 4)),
             DMA((2, 4)), DMA((2, 4)),
-            DMA((2, 4)), DMA((2, 4)),
-            DMA((3, 14)), DMA((3, 14)),
+            DMA((3, 26)), DMA((3, 26)),
             DMA((2,)),
         ],
         compiler_params=pltpu.CompilerParams(
@@ -826,22 +987,29 @@
 
 def attention_kernel(q_ref, g_ref, k_ref, v_ref, att_ref, qag_ref, kag_ref, vag_ref):
     scale = HSZ ** (-0.5)
+    spots = []
     for h in range(q_ref.shape[1] // HSZ):
         lanes = slice(h * HSZ, (h + 1) * HSZ)
         for s in range(2):
             rows, keys = slice(s * SPAN, (s + 1) * SPAN), slice(s * 2 * NL, (s + 1) * 2 * NL)
-            q, g = q_ref[rows, lanes], g_ref[rows, lanes]
-            k, v = k_ref[keys, lanes], v_ref[keys, lanes]
-            score = dot_nt(q, k) * scale
-            e = jnp.exp(score - jnp.max(score, axis=-1, keepdims=True))
-            full = e / jnp.sum(e, axis=-1, keepdims=True)
-            weights = full.astype(BF16)
-            att_ref[rows, lanes] = dot_nn(weights, v).astype(BF16)
-            pg = dot_nt(g, v)
-            sg = (full * (pg - jnp.sum(full * pg, axis=-1, keepdims=True)) * scale).astype(BF16)
-            qag_ref[rows, lanes] = dot_nn(sg, k).astype(BF16)
-            kag_ref[keys, lanes] = dot_tn(sg, q).astype(BF16)
-            vag_ref[keys, lanes] = dot_tn(weights, g).astype(BF16)
+            spots.append(((rows, lanes), (keys, lanes)))
+    scores = [dot_nt(q_ref[r], k_ref[k]) * scale for r, k in spots]
+    pgs = [dot_nt(g_ref[r], v_ref[k]) for r, k in spots]
+    tops = [jnp.max(s, axis=-1, keepdims=True) for s in scores]
+    es = [jnp.exp(s - m) for s, m in zip(scores, tops)]
+    sums = [jnp.sum(e, axis=-1, keepdims=True) for e in es]
+    fulls = [e / t for e, t in zip(es, sums)]
+    weights = [f.astype(BF16) for f in fulls]
+    dots = [jnp.sum(f * p, axis=-1, keepdims=True) for f, p in zip(fulls, pgs)]
+    sgs = [(f * (p - d) * scale).astype(BF16) for f, p, d in zip(fulls, pgs, dots)]
+    for (r, k), w in zip(spots, weights):
+        att_ref[r] = dot_nn(w, v_ref[k]).astype(BF16)
+    for (r, k), sg in zip(spots, sgs):
+        qag_ref[r] = dot_nn(sg, k_ref[k]).astype(BF16)
+    for (r, k), sg in zip(spots, sgs):
+        kag_ref[k] = dot_tn(sg, q_ref[r]).astype(BF16)
+    for (r, k), w in zip(spots, weights):
+        vag_ref[k] = dot_tn(w, g_ref[r]).astype(BF16)
 
 
 def attention(q, g, k, v):
@@ -862,47 +1030,23 @@
     )(q, g, k, v)
 
 
-def wide_columns(n):
-    r = lax.broadcasted_iota(jnp.int32, (28 * n, 32 * n), 0)
-    s = lax.broadcasted_iota(jnp.int32, (28 * n, 32 * n), 1)
-    return ((r // 28 == s // 32) & (r % 28 == s % 32)).astype(BF16)
-
-
-def lines(v):
-    return jnp.pad(v.reshape(4, 128), ((0, 4), (0, 0)))
-
-
 def shards(
     hidden, norm_gain, w_query, w_key, w_value, w_out, w_cond, enc_gain, store, neighbour_ids,
     out_grad,
 ):
-    y = lax.axis_index("enc")
-    xf = hidden.astype(F32)
-    gain = lax.dynamic_slice_in_dim(norm_gain, y * 1024, 1024)
-    sq = lines(jnp.sum(xf * xf, axis=-1))
-    summary = jnp.mean(xf.reshape(8, SPAN, 1024), axis=1).astype(BF16)
-    ids = jnp.pad(neighbour_ids.reshape(1, 4), ((0, 7), (0, 124)))
-    wc = dot_nn(w_cond, wide_columns(8)).astype(BF16)
-    wk = jnp.pad(w_key, ((0, 4), (0, 0)))
-    wv = jnp.pad(w_value, ((0, 4), (0, 0)))
-    raw, sq_all, q, ag, cond, normed_t, out_grad_t, gq, go, gc, gk, gv = forward(
-        ids, sq, gain.reshape(1, 1024), hidden, out_grad, summary, store,
-        w_query, w_out.T, wc, wk, wv,
+    egain = jnp.pad(enc_gain.reshape(32, 28), ((0, 0), (0, 4))).reshape(1, PE)
+    gain = norm_gain.reshape(1, 4096)
+    (
+        sq_all, summary, q, ag, keys, values, encoded, enc_in, normed_t, out_grad_t,
+        gq, go, gc, gk, gv,
+    ) = forward(
+        neighbour_ids.reshape(1, 4), gain, hidden, out_grad, egain, store,
+        w_query, w_out, w_cond, w_key, w_value,
     )
-    gk, gv = gk.reshape(PE, 2048), gv.reshape(PE, 2048)
-
-    egain = jnp.pad(enc_gain.reshape(32, 28), ((0, 0), (0, 4))).reshape(PE)
-    rawp = dot_nn(raw.reshape(512, DE), wide_columns(32))
-    cond_rows = cond.astype(BF16).astype(F32)
-    enc_in = (rawp.reshape(2, 256, PE) + cond_rows[:, None, :]).reshape(512, PE)
-    enc_rstd = lax.rsqrt(jnp.sum(enc_in * enc_in, axis=-1, keepdims=True) / DE + EPS)
-    encoded = (enc_in * enc_rstd * egain).astype(BF16)
-    keys = dot_nn(encoded, gk).astype(BF16)
-    values = dot_nn(encoded, gv).astype(BF16)
     att, qag, kag, vag = attention(q, ag, keys, values)
     layer_out, hidden_grad, qo, oo, co, kg, vg = backward(
-        att, qag, kag, vag, encoded, enc_in, egain.reshape(1, PE), hidden, out_grad,
-        gain.reshape(1, 1024), normed_t, out_grad_t, summary, sq_all, gc,
+        att, qag, kag, vag, encoded, enc_in, egain, hidden, out_grad,
+        gain, normed_t, out_grad_t, summary, sq_all, gc,
         gq.reshape(4, 256, 2048), go.reshape(4, 256, 2048),
         gk.reshape(4, 256, 2048), gv.reshape(4, 256, 2048),
     )

time: 262 us -> 228 us (0.87)
  Pallas kernels: 231 us -> 214 us
  matrix products: 13.6 us -> 0 us
  other arithmetic: 7.3 us -> 1.73 us
    dot_general x4 -> x0, matrix products: 13.6 us -> none  [dot_nn(): return jnp.dot(a, b, preferred_element_type=F32)]
    pallas_call x1, Pallas kernels: 19.4 us -> 9.58 us  [attention(): pl.pallas_call(attention_kernel, grid=(8,), out_shape=(jax.ShapeDtypeStru...]
    pallas_call x1, Pallas kernels: 107 us -> 101 us  [backward(): pl.pallas_call(backward_kernel, out_shape=(shape((512, 1024), BF16), shap...]
    convert_element_type x5 -> x0, other arithmetic: 3.18 us -> none  [the longest x1 1.72 us: shards(): qo.reshape(128, 512).astype(F32)]
    reduce_sum x2 -> x0, other arithmetic: 2.94 us -> none  [the longest x1 1.5 us: shards(): sq = lines(jnp.sum(xf * xf, axis=-1))]
    unnamed x41 -> x14, local copies, waits for them, and re-layouts: 3.96 us -> 5.33 us
where the time goes in v4:
time: 228 us; the launch traced here: 226 us
  Pallas kernels  214 us (94%)
  local copies, waits for them, and re-layouts  9.42 us (4%)
    pallas_call x1, Pallas kernels, forward(): pl.pallas_call(forward_kernel, out_shape=(shape((4, 8, 128), F32), shape(...  103 us
    pallas_call x1, Pallas kernels, backward(): pl.pallas_call(backward_kernel, out_shape=(shape((512, 1024), BF16), shap...  101 us
    pallas_call x1, Pallas kernels, attention(): pl.pallas_call(attention_kernel, grid=(8,), out_shape=(jax.ShapeDtypeStru...  9.58 us
    unnamed x14, local copies, waits for them, and re-layouts  5.33 us

profile of v4, /device:TPU:7, one launch (start us, length us, event | category | flops | bytes accessed | tf_op | source)
XLA Modules:
  0.0 225.8 jit_solution(403395070820130146)
XLA Ops:
  0.6 0.8 reshape.56
  1.4 0.7 reshape.57.egain
  2.1 1.6 copy.24.wc_in
  3.7 103.1 %forward.1 = (f32[4,8,128]{2,1,0:T(8,128)}, bf16[8,1024]{1,0:T(8,128)(2,1)}, bf16[128,2048]{1,0:T(8,128)(2,1)}, bf16[128,2048]{1,0:T(8,128)(2,1)}, bf16[512,2048...) custom-call(s32[1,4]{1,0:T(1,128)} %bitcast.30, ...), custom_call_target="tpu_custom_call" | custom-call | tf_op jit(solution)/shard_map/forward/pallas_call | solution.py:462
  106.7 9.6 %attention.1 = (bf16[128,2048]{1,0:T(8,128)(2,1)}, bf16[128,2048]{1,0:T(8,128)(2,1)}, bf16[512,2048]{1,0:T(8,128)(2,1)}, bf16[512,2048]{1,0:T(8,128)(2,1)}) custom-call(bf16[128,2048]{1,0:T(8,128)(2,1)} %get-tuple-element.33.q_ref, bf16[128,2048]{1,0:T(8,128)(2,1)} %get-tuple-element.34.g_ref, bf16[512,2048]{1,0:T(8,128)(2,1)} %get-tuple-element.35.k_ref, ...), custom_call_target="tpu_custom_call" | custom-call | tf_op jit(solution)/shard_map/attention/pallas_call | solution.py:1018
  116.3 101.3 %backward.1 = (bf16[512,1024]{1,0:T(8,128)(2,1)}, f32[512,1024]{1,0:T(8,128)}, bf16[2,2,32,512]{3,2,1,0:T(8,128)(2,1)}, bf16[2,2,32,512]{3,2,1,0:T(8,128)(2,1)},...) custom-call(bf16[128,2048]{1,0:T(8,128)(2,1)} %get-tuple-element.37.att, ...), custom_call_target="tpu_custom_call" | custom-call | tf_op jit(solution)/shard_map/backward/pallas_call | solution.py:929
  217.6 0.0 copy-start.1
  217.7 1.1 reshape.62
  218.8 0.0 copy-start
  218.8 0.2 copy.28
  219.0 0.7 reshape.67
  219.7 1.7 bitcast_convert_fusion
  221.4 0.8 copy.25
  222.3 0.0 copy-done.1
  222.3 1.0 copy.33
  223.2 0.0 copy-done
  223.2 0.0 copy-start.3
  223.2 0.0 copy-start.2
  223.2 1.3 copy.34
  224.6 0.0 copy-done.3
  224.6 0.6 copy.35
  225.2 0.0 copy-done.2
  225.2 0.6 copy.36
  (2 shorter events, 0.0 us)
Async XLA Ops:
  217.6 4.6 %copy-start.1 = (bf16[512,1024]{1,0:T(8,128)(2,1)S(1)}, bf16[512,1024]{1,0:T(8,128)(2,1)}, u32[]{:S(2)}) copy-start(bf16[512,1024]{1,0:T(8,128)(2,1)} %get-tuple-element.68) | copy-start | bytes 3145732
  218.8 4.4 %copy-start = (f32[512,1024]{1,0:T(8,128)S(1)}, f32[512,1024]{1,0:T(8,128)}, u32[]{:S(2)}) copy-start(f32[512,1024]{1,0:T(8,128)} %get-tuple-element.69) | copy-start | bytes 6291460
  223.2 1.3 copy-start.3
  223.2 2.0 copy-start.2

commit v5 on v4

--- a/solution.py
+++ b/solution.py
@@ -191,14 +191,16 @@
 
 
 def forward_kernel(
-    ids_in, gain, xs, og, egain, store, wq, wo_in, wc_in, wk_in, wv_in,
-    sq_all, sm, q, a, keys, values, enc, ein, nt, ogt, hq, ho, hc, hk, hv,
+    ids_in, gain, xs, og_h, egain, store, wq, wo_in, wc_in, wk_in, wv_in,
+    sq_all, sm, q, a, keys, values, enc_h, ein_h, nt_h, ogt_h, hq, ho, hc, hk, hv,
     ids_all, ids_s, out_rows, in_rows, tq, to, tc, yk, yv, gq, go, gc, gk, gv,
     normed, qp, ap, cp, q0, q1, q2, q3, a0, a1, a2, a3, rc,
     ids, sq, line_up, means, pick_cols, wo, wc, wk, wv,
     s_small, r_small, s_row, r_row, s_t, r_t, s_p, r_p, s_w, r_w, s_y, r_y, s_q, r_q, s_a, r_a,
-    s_loc, s_out,
+    s_loc, s_out, og, enc, ein, nt, ogt,
 ):
+    load = pltpu.make_async_copy(og_h, og, s_loc.at[1])
+    load.start()
     x, z, c, y = place()
     yp = [at(x, z, c, around(y, k)) for k in (1, 2, 3)]
     xp = [at(around(x, k), z, c, y) for k in (1, 2, 3)]
@@ -339,7 +341,6 @@
     pc.second()
     po.second()
     pq.swap()
-    pc.relay()
     outs = []
 
     def keep(n, g, h):
@@ -365,11 +366,12 @@
     product(normed, gq, into(qp))
     rq.first()
     keep(0, gq, hq)
-    pc.swap()
+    pc.relay()
     po.relay()
     for copy in across:
         copy.wait_recv()
     pk.first()
+    pc.swap()
     pc.last.wait_recv()
     keep(2, gc, hc)
     for i in range(4):
@@ -387,6 +389,7 @@
     po.swap()
     pk.second()
     po.last.wait_recv()
+    load.wait()
     product(og, go, into(ap))
     ra.first()
     keep(1, go, ho)
@@ -406,12 +409,16 @@
         ein[rows] = row
         scale = lax.rsqrt(jnp.sum(row * row, axis=-1, keepdims=True) / DE + EPS)
         enc[rows] = (row * scale * egain[...]).astype(BF16)
+    keep(5, enc, enc_h)
+    keep(6, ein, ein_h)
     ra.second()
     pk.swap()
     for j in range(4):
         rows = slice(128 * j, 128 * (j + 1))
         nt[:, rows] = normed[rows].T
         ogt[:, rows] = og[rows].T
+    keep(7, nt, nt_h)
+    keep(8, ogt, ogt_h)
     rq.third(q)
     for n, (g, h, out) in enumerate(((gk, hk, keys), (gv, hv, values))):
         pk.last[n].wait_recv()
@@ -478,8 +485,8 @@
             shape(keys, BF16),
             shape(keys, BF16),
         ),
-        in_specs=[VM] * 11,
-        out_specs=(VM,) * 10 + (ANY,) * 5,
+        in_specs=[VM] * 3 + [ANY] + [VM] * 7,
+        out_specs=(VM,) * 6 + (ANY,) * 9,
         scratch_shapes=[
             pltpu.VMEM((4, 8, 128), jnp.int32),
             pltpu.SMEM((4, 8, 128), jnp.int32),
@@ -521,8 +528,13 @@
             DMA((4,)), DMA((4,)),
             DMA((6,)), DMA((6,)),
             DMA((6,)), DMA((6,)),
-            DMA((1,)),
-            DMA((5,)),
+            DMA((2,)),
+            DMA((9,)),
+            pltpu.VMEM((512, 1024), BF16),
+            pltpu.VMEM((512, PE), BF16),
+            pltpu.VMEM((512, PE), F32),
+            pltpu.VMEM((1024, 512), BF16),
+            pltpu.VMEM((1024, 512), BF16),
         ],
         compiler_params=pltpu.CompilerParams(
             collective_id=0, has_side_effects=True, vmem_limit_bytes=58 << 20
@@ -672,14 +684,25 @@
 
 
 def backward_kernel(
-    att, qag, kag, vag, enc, ein, egain, xs, og, gain, nt, ogt, sm, sq, gc, gq, go, gk, gv,
+    att, qag, kag, vag, enc, ein_h, egain, xs_h, og_h, gain, nt_h, ogt_h, sm, sq, gc_h,
+    gq, go, gk, gv,
     layer, hidden, qo, oo, co, ko, vo,
     tile, et, att_all, qag_all, cd_all, rs_all, p1, p2, p3, line_up, erstd, emean, rsum, sgrad, slot,
     *scratch,
 ):
     b_k, b_v, ak, lk, rk, av, lv, rv, w_k, w_v, x_k, x_v, f_k, f_v = scratch[:14]
     bq, bo, bc = scratch[14:26], scratch[26:38], scratch[38:50]
-    s_y, r_y, s_d, r_d, s_c, r_c, s_1, r_1, s_2, r_2, s_3, r_3, s_h, r_h, s_tile = scratch[50:]
+    s_y, r_y, s_d, r_d, s_c, r_c, s_1, r_1, s_2, r_2, s_3, r_3, s_h, r_h, s_tile = scratch[50:65]
+    ein, xs, og, ogt, gc, s_in = scratch[65:]
+    nt = et
+    loads = [
+        pltpu.make_async_copy(h, v, s_in.at[n])
+        for n, (h, v) in enumerate(
+            ((ein_h, ein), (xs_h, xs), (og_h, og), (ogt_h, ogt), (gc_h, gc), (nt_h, nt))
+        )
+    ]
+    for copy in loads[:5]:
+        copy.start()
     x, z, c, y = place()
     yp = [at(x, z, c, around(y, k)) for k in (1, 2, 3)]
     xp = [at(around(x, k), z, c, y) for k in (1, 2, 3)]
@@ -710,6 +733,7 @@
     for n, (act, p, b) in enumerate(((kag, p1, b_k), (vag, p2, b_v))):
         product(et, act, p)
         swaps.append(remote(p.at[:, :, 1 - c], b, s_c.at[n], r_c.at[n], sib))
+    loads[5].start()
     att_all[y] = att[...]
     qag_all[y] = qag[...]
 
@@ -749,13 +773,13 @@
     def fetch(h, i, j):
         return pltpu.make_async_copy(h.at[i], tile.at[j], s_tile.at[j])
 
+    for copy in loads:
+        copy.wait()
     ee = ein[...]
     erstd[...] = lax.rsqrt(jnp.sum(ee * ee, axis=-1, keepdims=True) / DE + EPS)
     emean[...] = jnp.zeros_like(emean)
     fetch(gk, 0, 0).start()
     fetch(gv, 0, 1).start()
-    kring.mid()
-    vring.mid()
 
     def encoder(i, carry):
         lanes = cols(i, 256)
@@ -782,6 +806,12 @@
 
     lax.fori_loop(0, 4, encoder, 0)
     relay(1, qag_all)
+    kring.mid()
+    vring.mid()
+    for copy in passed[:2]:
+        copy.wait_recv()
+    product(ogt, att_all, p2)
+    ro.swap()
     for s in range(2):
         rows = slice(256 * s, 256 * s + 256)
         weight = erstd[rows] ** 3 * (emean[rows] / DE)
@@ -790,10 +820,6 @@
     cd_all[y] = slot[...]
     small = [remote(slot, cd_all.at[y], s_d.at[0, k], r_d.at[0, k], yp[k - 1]) for k in (1, 2, 3)]
 
-    for copy in passed[:2]:
-        copy.wait_recv()
-    product(ogt, att_all, p2)
-    ro.swap()
 
     def streamed(h, act, use):
         fetch(h, 0, 0).start()
@@ -810,8 +836,12 @@
 
         lax.fori_loop(0, 4, step, 0)
 
+    ro.first()
+    for copy in passed[2:]:
+        copy.wait_recv()
+    product(nt, qag_all, p1)
+    rq.swap()
     sent2 = []
-    ro.first()
     for n, (w, v) in enumerate(((w_k, x_k), (w_v, x_v))):
         rings[n].here()
         for i in range(2):
@@ -822,10 +852,6 @@
             else:
                 src, peer = w.at[around(x, k)], xp[k - 1]
             sent2.append(remote(src, v.at[k - 1], s_2.at[n, k], r_2.at[n, k], peer))
-    for copy in passed[2:]:
-        copy.wait_recv()
-    product(nt, qag_all, p1)
-    rq.swap()
     ro.mid()
 
     def add_out(lanes, value):
@@ -833,6 +859,13 @@
 
     streamed(go, att_all, add_out)
     rq.first()
+    for copy in small:
+        copy.wait_recv()
+    cd = cd_all[...].reshape(8, 1024).astype(BF16)
+    for i in range(4):
+        lanes = slice(256 * i, 256 * i + 256)
+        p3[..., lanes] = dot_tn(sm[...], cd[:, lanes]).astype(BF16).reshape(4, 4, 2, 32, 256)
+    rc.swap()
     ro.second()
     sent3 = []
     for n, (w, v, f) in enumerate(((w_k, x_k, f_k), (w_v, x_v, f_v))):
@@ -845,14 +878,8 @@
         for k in (2, 1, 3):
             src, dst = f.at[0, :, cols(around(y, k), 512)], f.at[k, :, pl.ds(0, 512)]
             sent3.append(remote(src, dst, s_3.at[n, k], r_3.at[n, k], yp[k - 1]))
-    for copy in small:
-        copy.wait_recv()
-    cd = cd_all[...].reshape(8, 1024).astype(BF16)
-    for i in range(4):
-        lanes = slice(256 * i, 256 * i + 256)
-        p3[..., lanes] = dot_tn(sm[...], cd[:, lanes]).astype(BF16).reshape(4, 4, 2, 32, 256)
-    rc.swap()
     rq.mid()
+    rc.first()
     for i in range(4):
         sgrad[:, 256 * i : 256 * i + 256] = dot_nt(cd, gc[i].reshape(256, 1024)) / SPAN
     rsum[...] = jnp.zeros_like(rsum)
@@ -872,7 +899,6 @@
             remote(rs_all.at[4], rs_all.at[y], s_d.at[1, k], r_d.at[1, k], yp[k - 1])
         )
     rs_all[y] = rs_all[4]
-    rc.first()
     ro.third()
     rq.second()
     rc.mid()
@@ -885,8 +911,8 @@
             + f[2, :, pl.ds(0, 512)].astype(F32)
             + f[3, :, pl.ds(0, 512)].astype(F32)
         )
+    rq.third()
     rc.second()
-    rq.third()
     for copy in small[3:]:
         copy.wait_recv()
     total = rs_all[0] + rs_all[1] + rs_all[2] + rs_all[3]
@@ -937,7 +963,7 @@
             shape((32, 512), F32),
             shape((32, 512), F32),
         ),
-        in_specs=[VM] * 15 + [ANY] * 4,
+        in_specs=[VM] * 5 + [ANY, VM, ANY, ANY, VM, ANY, ANY, VM, VM] + [ANY] * 5,
         out_specs=(VM,) * 7,
         scratch_shapes=[
             pltpu.VMEM((2, 256, 2048), BF16),
@@ -977,6 +1003,12 @@
             DMA((2, 4)), DMA((2, 4)),
             DMA((3, 26)), DMA((3, 26)),
             DMA((2,)),
+            pltpu.VMEM((512, PE), F32),
+            pltpu.VMEM((512, 1024), BF16),
+            pltpu.VMEM((512, 1024), BF16),
+            pltpu.VMEM((1024, 512), BF16),
+            pltpu.VMEM((4, 2, 128, 1024), BF16),
+            DMA((6,)),
         ],
         compiler_params=pltpu.CompilerParams(
             collective_id=1, has_side_effects=True, vmem_limit_bytes=60 << 20

time: 228 us -> 224 us (0.982)
  Pallas kernels: 214 us -> 209 us
    pallas_call x1, Pallas kernels: 101 us -> 98.4 us  [backward(): pl.pallas_call(backward_kernel, out_shape=(shape((512, 1024), BF16), shap...]
where the time goes in v5:
time: 224 us; the launch traced here: 221 us
  Pallas kernels  209 us (93%)
  local copies, waits for them, and re-layouts  9.42 us (4%)
    pallas_call x1, Pallas kernels, forward(): pl.pallas_call(forward_kernel, out_shape=(shape((4, 8, 128), F32), shape(...  101 us
    pallas_call x1, Pallas kernels, backward(): pl.pallas_call(backward_kernel, out_shape=(shape((512, 1024), BF16), shap...  98.4 us
    pallas_call x1, Pallas kernels, attention(): pl.pallas_call(attention_kernel, grid=(8,), out_shape=(jax.ShapeDtypeStru...  9.58 us
    unnamed x14, local copies, waits for them, and re-layouts  5.33 us

profile of v5, /device:TPU:7, one launch (start us, length us, event | category | flops | bytes accessed | tf_op | source)
XLA Modules:
  0.0 221.2 jit_solution(6327991385982759729)
XLA Ops:
  0.6 0.8 reshape.56
  1.4 0.7 reshape.57.egain
  2.1 1.6 copy.24.wc_in
  3.7 101.3 %forward.1 = (f32[4,8,128]{2,1,0:T(8,128)}, bf16[8,1024]{1,0:T(8,128)(2,1)}, bf16[128,2048]{1,0:T(8,128)(2,1)}, bf16[128,2048]{1,0:T(8,128)(2,1)}, bf16[512,2048...) custom-call(s32[1,4]{1,0:T(1,128)} %bitcast.30, ...), custom_call_target="tpu_custom_call" | custom-call | tf_op jit(solution)/shard_map/forward/pallas_call | solution.py:469
  105.0 9.6 %attention.1 = (bf16[128,2048]{1,0:T(8,128)(2,1)}, bf16[128,2048]{1,0:T(8,128)(2,1)}, bf16[512,2048]{1,0:T(8,128)(2,1)}, bf16[512,2048]{1,0:T(8,128)(2,1)}) custom-call(bf16[128,2048]{1,0:T(8,128)(2,1)} %get-tuple-element.33.q_ref, bf16[128,2048]{1,0:T(8,128)(2,1)} %get-tuple-element.34.g_ref, bf16[512,2048]{1,0:T(8,128)(2,1)} %get-tuple-element.35.k_ref, ...), custom_call_target="tpu_custom_call" | custom-call | tf_op jit(solution)/shard_map/attention/pallas_call | solution.py:1050
  114.5 98.4 %backward.1 = (bf16[512,1024]{1,0:T(8,128)(2,1)}, f32[512,1024]{1,0:T(8,128)}, bf16[2,2,32,512]{3,2,1,0:T(8,128)(2,1)}, bf16[2,2,32,512]{3,2,1,0:T(8,128)(2,1)},...) custom-call(bf16[128,2048]{1,0:T(8,128)(2,1)} %get-tuple-element.37.att, ...), custom_call_target="tpu_custom_call" | custom-call | tf_op jit(solution)/shard_map/backward/pallas_call | solution.py:955
  213.0 0.0 copy-start.1
  213.0 1.1 reshape.62
  214.1 0.0 copy-start
  214.1 0.2 copy.28
  214.4 0.7 reshape.67
  215.0 1.7 bitcast_convert_fusion
  216.8 0.8 copy.25
  217.6 0.0 copy-done.1
  217.6 1.0 copy.33
  218.6 0.0 copy-done
  218.6 0.0 copy-start.3
  218.6 0.0 copy-start.2
  218.6 1.3 copy.34
  219.9 0.0 copy-done.3
  219.9 0.6 copy.35
  220.5 0.0 copy-done.2
  220.5 0.6 copy.36
  (2 shorter events, 0.0 us)
Async XLA Ops:
  213.0 4.6 %copy-start.1 = (bf16[512,1024]{1,0:T(8,128)(2,1)S(1)}, bf16[512,1024]{1,0:T(8,128)(2,1)}, u32[]{:S(2)}) copy-start(bf16[512,1024]{1,0:T(8,128)(2,1)} %get-tuple-element.68) | copy-start | bytes 3145732
  214.1 4.4 %copy-start = (f32[512,1024]{1,0:T(8,128)S(1)}, f32[512,1024]{1,0:T(8,128)}, u32[]{:S(2)}) copy-start(f32[512,1024]{1,0:T(8,128)} %get-tuple-element.69) | copy-start | bytes 6291460
  218.6 1.3 copy-start.3
  218.6 2.0 copy-start.2

commit v6 on v5

--- a/solution.py
+++ b/solution.py
@@ -1045,11 +1045,11 @@
 
 
 def attention(q, g, k, v):
-    few = pl.BlockSpec((128, 256), lambda h: (0, h))
-    many = pl.BlockSpec((512, 256), lambda h: (0, h))
+    few = pl.BlockSpec((128, 512), lambda h: (0, h))
+    many = pl.BlockSpec((512, 512), lambda h: (0, h))
     return pl.pallas_call(
         attention_kernel,
-        grid=(8,),
+        grid=(4,),
         out_shape=(
             jax.ShapeDtypeStruct((128, 2048), BF16),
             jax.ShapeDtypeStruct((128, 2048), BF16),

time: 224 us -> 222 us (level)
    pallas_call x1, Pallas kernels: 9.58 us -> 7.16 us  [attention(): pl.pallas_call(attention_kernel, grid=(4,), out_shape=(jax.ShapeDtypeStru...]
where the time goes in v6:
time: 222 us; the launch traced here: 219 us
  Pallas kernels  207 us (93%)
  local copies, waits for them, and re-layouts  9.42 us (4%)
    pallas_call x1, Pallas kernels, forward(): pl.pallas_call(forward_kernel, out_shape=(shape((4, 8, 128), F32), shape(...  101 us
    pallas_call x1, Pallas kernels, backward(): pl.pallas_call(backward_kernel, out_shape=(shape((512, 1024), BF16), shap...  98.4 us
    pallas_call x1, Pallas kernels, attention(): pl.pallas_call(attention_kernel, grid=(4,), out_shape=(jax.ShapeDtypeStru...  7.16 us
    unnamed x14, local copies, waits for them, and re-layouts  5.33 us

profile of v6, /device:TPU:7, one launch (start us, length us, event | category | flops | bytes accessed | tf_op | source)
XLA Modules:
  0.0 218.7 jit_solution(4737085199646784311)
XLA Ops:
  0.6 0.8 reshape.56
  1.4 0.7 reshape.57.egain
  2.1 1.6 copy.24.wc_in
  3.7 101.3 %forward.1 = (f32[4,8,128]{2,1,0:T(8,128)}, bf16[8,1024]{1,0:T(8,128)(2,1)}, bf16[128,2048]{1,0:T(8,128)(2,1)}, bf16[128,2048]{1,0:T(8,128)(2,1)}, bf16[512,2048...) custom-call(s32[1,4]{1,0:T(1,128)} %bitcast.30, ...), custom_call_target="tpu_custom_call" | custom-call | tf_op jit(solution)/shard_map/forward/pallas_call | solution.py:469
  105.0 7.2 %attention.1 = (bf16[128,2048]{1,0:T(8,128)(2,1)}, bf16[128,2048]{1,0:T(8,128)(2,1)}, bf16[512,2048]{1,0:T(8,128)(2,1)}, bf16[512,2048]{1,0:T(8,128)(2,1)}) custom-call(bf16[128,2048]{1,0:T(8,128)(2,1)} %get-tuple-element.33.q_ref, bf16[128,2048]{1,0:T(8,128)(2,1)} %get-tuple-element.34.g_ref, bf16[512,2048]{1,0:T(8,128)(2,1)} %get-tuple-element.35.k_ref, ...), custom_call_target="tpu_custom_call" | custom-call | tf_op jit(solution)/shard_map/attention/pallas_call | solution.py:1050
  112.1 98.4 %backward.1 = (bf16[512,1024]{1,0:T(8,128)(2,1)}, f32[512,1024]{1,0:T(8,128)}, bf16[2,2,32,512]{3,2,1,0:T(8,128)(2,1)}, bf16[2,2,32,512]{3,2,1,0:T(8,128)(2,1)},...) custom-call(bf16[128,2048]{1,0:T(8,128)(2,1)} %get-tuple-element.37.att, ...), custom_call_target="tpu_custom_call" | custom-call | tf_op jit(solution)/shard_map/backward/pallas_call | solution.py:955
  210.5 0.0 copy-start.1
  210.6 1.1 reshape.62
  211.7 0.0 copy-start
  211.7 0.2 copy.28
  211.9 0.7 reshape.67
  212.6 1.7 bitcast_convert_fusion
  214.3 0.8 copy.25
  215.2 0.0 copy-done.1
  215.2 1.0 copy.33
  216.1 0.0 copy-done
  216.1 0.0 copy-start.3
  216.1 0.0 copy-start.2
  216.1 1.3 copy.34
  217.5 0.0 copy-done.3
  217.5 0.6 copy.35
  218.1 0.0 copy-done.2
  218.1 0.6 copy.36
  (2 shorter events, 0.0 us)
Async XLA Ops:
  210.5 4.6 %copy-start.1 = (bf16[512,1024]{1,0:T(8,128)(2,1)S(1)}, bf16[512,1024]{1,0:T(8,128)(2,1)}, u32[]{:S(2)}) copy-start(bf16[512,1024]{1,0:T(8,128)(2,1)} %get-tuple-element.68) | copy-start | bytes 3145732
  211.7 4.4 %copy-start = (f32[512,1024]{1,0:T(8,128)S(1)}, f32[512,1024]{1,0:T(8,128)}, u32[]{:S(2)}) copy-start(f32[512,1024]{1,0:T(8,128)} %get-tuple-element.69) | copy-start | bytes 6291460
  216.1 1.3 copy-start.3
  216.1 2.0 copy-start.2
